TPU v7x, 128 devices: a whole 4x4x4 slice. The times are simulated.
128 devices in a mesh: dp: 8 (over x, core), space: 16 (over y, z).
Axes of the slice: x: 4, y: 4, z: 4, core: 2. Of those that a mesh axis runs over, the one named last changes fastest.
Arguments:
- layer_input: bfloat16 [8, 64, 32, 1024], P('dp', None, 'space'), may hold values from -6 to 6
- hidden_pre: bfloat16 [8, 128, 32, 1024], P('dp', None, 'space'), may hold values from -6 to 6
- output_pre: bfloat16 [8, 256, 16, 256], P('dp', None, 'space'), may hold values from -6 to 6
- output_grad: bfloat16 [8, 256, 16, 256], P('dp', None, 'space'), may hold values from -48 to 48
- weight_a: bfloat16 [27, 64, 128], replicated, may hold values from -0.15625 to 0.15625
- weight_b: bfloat16 [27, 128, 256], replicated, may hold values from -0.109375 to 0.109375
Outputs:
- input_grad: bfloat16 [8, 64, 32, 1024], P('dp', None, 'space')
- weight_grad_a: float32 [27, 64, 128], replicated
- weight_grad_b: float32 [27, 128, 256], replicated
All inputs are finite; a program needn't handle non-finite values.
Results may differ from a plain program's by a relative error of at most 0.013.
Values may be sent and summed in bfloat16 or wider, within the bound.
A program may use at most 64 MiB of HBM per device.

v0:
```python
import math

import jax
import jax.numpy as jnp
from jax import lax
from jax.sharding import PartitionSpec as P
from jax.experimental import pallas as pl
from jax.experimental.pallas import tpu as pltpu

negative_slope = 0.3


def padded_2(cells, sides, width):
    for axis, dim in sides:
        count = lax.axis_size(axis)
        ends = count - 1
        head = lax.slice_in_dim(cells, 0, width, axis=dim)
        tail = lax.slice_in_dim(cells, cells.shape[dim] - width, cells.shape[dim], axis=dim)
        cells = jnp.concatenate(
            [
                lax.ppermute(tail, axis, [(i, (i + 1) % count) for i in range(ends)]),
                cells,
                lax.ppermute(head, axis, [((i + 1) % count, i) for i in range(ends)]),
            ],
            axis=dim,
        )
    return cells


def slopes(values):
    return jnp.where(values > 0, jnp.ones_like(values), negative_slope * jnp.ones_like(values))


def window(padded, tap_z, tap_y, tap_x, depth, side):
    planes = padded[:, tap_z : tap_z + depth, :]
    margin = side + 1
    wider = jnp.pad(planes, ((0, 0), (0, 0), (margin, margin)))
    offset = (tap_y - 1) * side + (tap_x - 1)
    piece = wider[:, :, margin + offset : margin + offset + side * side]
    column = jnp.arange(side * side, dtype=jnp.int32) % side + (tap_x - 1)
    inside = (column >= 0) & (column < side)
    piece = jnp.where(inside, piece, jnp.zeros_like(piece))
    return piece.reshape(padded.shape[0], depth * side * side)


def outer_product(left, right):
    return lax.dot_general(
        left, right, (((1,), (1,)), ((), ())), preferred_element_type=jnp.float32
    )


def _all_reduce_kernel(x_ref, o_a, o_b, full, recv_a, acc_a, recv_1, acc_1, recv_2, acc_2, recv_3, sends, recvs):
    rows = x_ref.shape[0]
    half = rows // 2
    part = half // 3
    quarter, piece = part // 4, part // 16
    mesh_id = pl.DeviceIdType.MESH
    dp = lax.axis_index("dp")
    sp = lax.axis_index("space")
    core = dp % 2
    spot = {"x": dp // 2, "y": sp // 4, "z": sp % 4}
    partner = (spot["x"] * 2 + (1 - core), sp)

    def peer(axis, k):
        moved = dict(spot)
        moved[axis] = (spot[axis] + k) % 4
        return (moved["x"] * 2 + core, moved["y"] * 4 + moved["z"])

    orders = (("x", "y", "z"), ("y", "z", "x"), ("z", "x", "y"))
    peers = [partner] + [peer(axis, k) for axis in "xyz" for k in (1, 2, 3)]
    barrier = pltpu.get_barrier_semaphore()
    for other in peers:
        pl.semaphore_signal(barrier, inc=1, device_id=other, device_id_type=mesh_id)
    pl.semaphore_wait(barrier, len(peers))

    def rows_at(start, size):
        return pl.ds(pl.multiple_of(start, 8), size)

    used = [0]

    def exchange(triples):
        copies = []
        for src, dst, other in triples:
            copy = pltpu.make_async_remote_copy(
                src_ref=src,
                dst_ref=dst,
                send_sem=sends.at[used[0]],
                recv_sem=recvs.at[used[0]],
                device_id=other,
                device_id_type=mesh_id,
            )
            used[0] += 1
            copy.start()
            copies.append(copy)
        for copy in copies:
            copy.wait()

    exchange([(x_ref.at[rows_at((1 - core) * half, half)], recv_a, partner)])
    acc_a[...] = x_ref[rows_at(core * half, half), :] + recv_a[...]
    triples = []
    for p, order in enumerate(orders):
        for k in (1, 2, 3):
            block = p * part + ((spot[order[0]] + k) % 4) * quarter
            triples.append((acc_a.at[rows_at(block, quarter)], recv_1.at[p, k - 1], peer(order[0], k)))
    exchange(triples)
    for p, order in enumerate(orders):
        mine = p * part + spot[order[0]] * quarter
        acc_1[p] = acc_a[rows_at(mine, quarter), :] + recv_1[p, 0] + recv_1[p, 1] + recv_1[p, 2]
    triples = []
    for p, order in enumerate(orders):
        for k in (1, 2, 3):
            block = ((spot[order[1]] + k) % 4) * piece
            triples.append((acc_1.at[p, rows_at(block, piece)], recv_2.at[p, k - 1], peer(order[1], k)))
    exchange(triples)
    for p, order in enumerate(orders):
        mine = spot[order[1]] * piece
        recv_3[p, 0] = acc_1[p, rows_at(mine, piece), :] + recv_2[p, 0] + recv_2[p, 1] + recv_2[p, 2]
    exchange([(recv_3.at[p, 0], recv_3.at[p, k], peer(order[2], k)) for p, order in enumerate(orders) for k in (1, 2, 3)])
    spans = []
    for p, order in enumerate(orders):
        last = spot[order[2]]
        total = recv_3[p, last % 4]
        for j in (1, 2, 3):
            total = total + recv_3[p, (last - j + 4) % 4]
        outer = core * half + p * part + spot[order[0]] * quarter
        own = outer + spot[order[1]] * piece
        full[rows_at(own, piece), :] = total
        spans.append((outer, own, order))
    exchange([(full.at[rows_at(own, piece)], full.at[rows_at(own, piece)], peer(order[1], k)) for outer, own, order in spans for k in (1, 2, 3)])
    exchange([(full.at[rows_at(outer, quarter)], full.at[rows_at(outer, quarter)], peer(order[0], k)) for outer, own, order in spans for k in (1, 2, 3)])
    block = full.at[rows_at(core * half, half)]
    exchange([(block, block, partner)])
    rows_a, rows_b = o_a.shape[0], o_b.shape[0]
    o_a[...] = full[0:rows_a, :]
    o_b[:, 0:128] = full[rows_a : rows_a + rows_b, :]
    o_b[:, 128:256] = full[rows_a + rows_b : rows_a + 2 * rows_b, :]


def all_reduce(sums_a, sums_b, scale_a, scale_b):
    rows_a = sums_a.shape[0] * sums_a.shape[1]
    rows_b = sums_b.shape[0] * sums_b.shape[1]
    wide = sums_b.reshape(rows_b, 256) * scale_b
    flat = jnp.concatenate([sums_a.reshape(rows_a, 128) * scale_a, wide[:, :128], wide[:, 128:]])
    count = flat.shape[0]
    unit = 6 * 16 * 8
    rows = -(-count // unit) * unit
    flat = jnp.pad(flat, ((0, rows - count), (0, 0)))
    half = rows // 2
    part = half // 3
    quarter, piece = part // 4, part // 16
    f32 = jnp.float32
    out_a, out_b = pl.pallas_call(
        _all_reduce_kernel,
        out_shape=(jax.ShapeDtypeStruct((rows_a, 128), f32), jax.ShapeDtypeStruct((rows_b, 256), f32)),
        in_specs=[pl.BlockSpec(memory_space=pltpu.VMEM)],
        out_specs=(pl.BlockSpec(memory_space=pltpu.VMEM), pl.BlockSpec(memory_space=pltpu.VMEM)),
        scratch_shapes=[
            pltpu.VMEM((rows, 128), f32),
            pltpu.VMEM((half, 128), f32),
            pltpu.VMEM((half, 128), f32),
            pltpu.VMEM((3, 3, quarter, 128), f32),
            pltpu.VMEM((3, quarter, 128), f32),
            pltpu.VMEM((3, 3, piece, 128), f32),
            pltpu.VMEM((3, piece, 128), f32),
            pltpu.VMEM((3, 4, piece, 128), f32),
            pltpu.SemaphoreType.DMA((47,)),
            pltpu.SemaphoreType.DMA((47,)),
        ],
        compiler_params=pltpu.CompilerParams(collective_id=0, has_side_effects=True),
    )(flat)
    return out_a.reshape(sums_a.shape), out_b.reshape(sums_b.shape)


def conv_cells(field, kernel):
    shaped = kernel.reshape(3, 3, 3, kernel.shape[1], kernel.shape[2])
    result = lax.conv_general_dilated(
        field[None],
        shaped,
        (1, 1, 1),
        ((0, 0), (1, 1), (1, 1)),
        dimension_numbers=("NCDHW", "DHWIO", "NCDHW"),
        preferred_element_type=jnp.float32,
    )
    return result[0]


def back_cells(padded, kernel):
    flipped = kernel[::-1].transpose(0, 2, 1)
    return conv_cells(padded, flipped)


def kernel_terms(padded, upstream):
    taps, chan_in, chan_out = 27, padded.shape[0], upstream.shape[0]
    start = jnp.zeros((taps, chan_in, chan_out), jnp.float32)
    field = padded.astype(jnp.float32)
    unused, pull = jax.vjp(lambda w: conv_cells(field, w), start)
    return pull(upstream.astype(jnp.float32))[0]


def per_device(layer_input, hidden_pre, output_pre, output_grad, weight_a, weight_b):
    side = math.isqrt(layer_input.shape[3])
    half = side // 2
    depth_a = layer_input.shape[2]
    depth_b = depth_a // 2
    source = layer_input[0]
    hidden = hidden_pre[0]
    outer = output_pre[0]
    upstream = output_grad[0]
    chan_in = source.shape[0]
    width_a = hidden.shape[0]
    width_b = outer.shape[0]
    grad_outer = (upstream.astype(jnp.float32) * slopes(outer.astype(jnp.float32))).astype(
        jnp.bfloat16
    )
    hidden_f = hidden.astype(jnp.float32)
    active = jnp.where(hidden_f > 0, hidden_f, negative_slope * hidden_f)
    pooled = (
        active.reshape(width_a, depth_b, 2, half, 2, half, 2)
        .mean(axis=(2, 4, 6))
        .astype(jnp.bfloat16)
    )
    pooled = pooled.reshape(width_a, depth_b, half * half)
    outer_pad = padded_2(grad_outer, (("space", 1),), 1).reshape(width_b, depth_b + 2, half, half)
    pooled_pad = padded_2(pooled, (("space", 1),), 1).reshape(width_a, depth_b + 2, half, half)
    back_b = back_cells(outer_pad, weight_b)
    sums_b = kernel_terms(pooled_pad, grad_outer.reshape(width_b, depth_b, half, half))
    upward = jnp.repeat(jnp.repeat(jnp.repeat(back_b, 2, 1), 2, 2), 2, 3) * 0.125
    upward = upward.reshape(width_a, depth_a * side * side)
    grad_hidden = (upward * slopes(hidden_f.reshape(width_a, depth_a * side * side))).astype(
        jnp.bfloat16
    )
    grad_hidden = grad_hidden.reshape(width_a, depth_a, side * side)
    hidden_pad = padded_2(grad_hidden, (("space", 1),), 1).reshape(width_a, depth_a + 2, side, side)
    source_pad = padded_2(source, (("space", 1),), 1).reshape(chan_in, depth_a + 2, side, side)
    back_a = back_cells(hidden_pad, weight_a)
    sums_a = kernel_terms(source_pad, grad_hidden.reshape(width_a, depth_a, side, side))
    input_grad = back_a.astype(jnp.bfloat16).reshape(1, chan_in, depth_a, side * side)
    samples = lax.axis_size("dp")
    planes_a = depth_a * lax.axis_size("space")
    scale_a = 1.0 / math.sqrt(samples * planes_a * side * side)
    scale_b = 1.0 / math.sqrt(samples * (planes_a // 2) * half * half)
    total_a, total_b = all_reduce(sums_a, sums_b, scale_a, scale_b)
    return (input_grad, total_a, total_b)


def solution(mesh):
    in_specs = (
        P("dp", None, "space", None),
        P("dp", None, "space", None),
        P("dp", None, "space", None),
        P("dp", None, "space", None),
        P(),
        P(),
    )
    out_specs = (P("dp", None, "space", None), P(), P())
    return jax.shard_map(
        per_device, mesh=mesh, in_specs=in_specs, out_specs=out_specs, check_vma=False
    )
```

profile of v0, /device:TPU:1, one launch (start us, length us, event | category | flops | bytes accessed | tf_op | source)
XLA Modules:
  0.0 150.6 jit_solution(14710870212709141022)
XLA Ops:
  0.6 1.0 copy.21
  1.6 1.0 copy.20
  2.6 0.1 multiply_convert_fusion.1
  2.7 0.0 copy-start.6
  2.7 1.4 collective-permute-start.1
  4.2 5.6 %collective-permute-start = (bf16[256,1,256]{0,2,1:T(8,128)(2,1)S(1)}, bf16[256,1,256]{0,2,1:T(8,128)(2,1)}, u32[]{:S(2)}, u32[]{:S(2)}) collective-permute-start(bf16[256,1,256]{0,2,1:T(8,128)(2,1)S(1)} %bitcast.67), channel_id=1, source_target_pairs={{0,1},{1,2},{2,3},{3,4},{4,5},{5,6},{6,7},{7,8},{8,9},{9,10},{10,1... | collective-permute-start | bytes 393224 | tf_op jit(solution)/shard_map/ppermute | solution.py:21
  9.8 1.4 copy.25
  11.2 0.2 fusion.16
  11.4 0.0 copy-start.4
  11.4 0.4 reduce_sum.18
  11.8 0.6 multiply_convert_fusion.2
  12.4 1.3 collective-permute-start.7
  13.7 4.6 %collective-permute-start.6 = (bf16[128,1,256]{0,2,1:T(8,128)(2,1)}, bf16[128,1,256]{0,2,1:T(8,128)(2,1)}, u32[]{:S(2)}, u32[]{:S(2)}) collective-permute-start(bf16[128,1,256]{0,2,1:T(8,128)(2,1)} %bitcast.28), channel_id=1, source_target_pairs={{0,1},{1,2},{2,3},{3,4},{4,5},{5,6},{6,7},{7,8},{8,9},{9,10},{10,1... | collective-permute-start | bytes 196616 | tf_op jit(solution)/shard_map/ppermute | solution.py:21
  18.3 0.0 copy-done.6
  18.3 0.3 copy.31
  18.6 0.8 fusion.36
  19.5 2.3 %collective-permute-start.4 = (bf16[64,1,1024]{0,2,1:T(8,128)(2,1)}, bf16[64,1,1024]{0,2,1:T(8,128)(2,1)S(1)}, u32[]{:S(2)}, u32[]{:S(2)}) collective-permute-start(bf16[64,1,1024]{0,2,1:T(8,128)(2,1)} %get-tuple-element.12), channel_id=1, source_target_pairs={{0,1},{1,2},{2,3},{3,4},{4,5},{5,6},{6,7},{7,8},{8,9},{9,10},{10,1... | collective-permute-start | bytes 393224 | tf_op jit(solution)/shard_map/ppermute | solution.py:21
  21.8 0.6 fusion.40
  22.4 0.9 copy.23
  23.4 0.8 rev.7
  24.2 1.1 copy.34
  25.3 1.0 copy.38
  26.3 2.9 %rev.6 = bf16[27,128,256]{2,1,0:T(8,128)(2,1)} reverse(bf16[27,128,256]{2,1,0:T(8,128)(2,1)} %param.11), dimensions={0} | reverse | bytes 3538944 | tf_op jit(solution)/shard_map/rev | solution.py:188
  29.2 0.0 collective-permute-done.7
  29.2 1.3 collective-permute-start.5
  30.5 0.9 copy.39
  31.4 0.0 collective-permute-done.6
  31.4 0.9 copy.37
  32.4 2.4 %convolution_multiply_fusion = f32[3,3,3,128,256]{4,3,2,1,0:T(8,128)S(1)} fusion(bf16[1,128,1,16,16]{1,0,4,3,2:T(2,128)(2,1)S(1)} %copy.39, bf16[1,128,1,16,16]{1,0,4,3,2:T(2,128)(2,1)S(1)} %copy.38, bf16[1,128,1,16,16]{1,0,4,3,2:T(2,128)(2,1)S(1)} %copy.37, bf16[1,256,1,16,16]{1,4,3,2,0:T(8,128)(2,1)S(1)} %bitcast.69), kind=kOutput, calls=%fused_computation.7 | convolution fusion | flops 417497088 | bytes 3866624 | tf_op jit(solution)/shard_map/transpose(jvp())/conv_general_dilated | solution.py:176
  34.8 2.0 %fusion.35 = (f32[3456,128]{1,0:T(8,128)}, f32[3456,128]{1,0:T(8,128)}) fusion(f32[3456,256]{1,0:T(8,128)S(1)} %bitcast.58), kind=kLoop, calls=%fused_computation.47 | loop fusion | bytes 7077888 | tf_op jit(solution)/shard_map/slice | solution.py:143
  36.7 0.0 collective-permute-done.1
  36.7 1.3 copy.24
  38.1 0.0 collective-permute-done
  38.1 1.2 copy.22
  39.2 0.0 collective-permute-done.4
  39.2 0.6 copy.33
  39.8 0.0 collective-permute-done.5
  39.8 0.6 copy.35
  40.4 3.4 %convolution_multiply_fusion.1 = f32[1,128,1,16,16]{1,0,4,3,2:T(1,128)S(1)} fusion(bf16[3,3,3,256,128]{3,4,2,1,0:T(8,128)(2,1)S(1)} %bitcast.62, bf16[1,256,1,16,16]{1,0,4,3,2:T(2,128)(2,1)S(1)} %copy.24, bf16[1,256,1,16,16]{1,0,4,3,2:T(2,128)(2,1)S(1)} %copy-done.7, bf16[1,256,1,16,16]{1,0,4,3,2:T(2,128)(2,1)S(1)} %copy.22), kind=kOutput, calls=%fused_computation.19 | convolution fusion | flops 417234944 | bytes 2293760 | tf_op jit(solution)/shard_map/conv_general_dilated | solution.py:176
  43.9 0.3 broadcast_in_dim.23
  44.2 0.2 fusion.17
  44.4 0.8 fusion.37
  45.2 6.7 %collective-permute-start.2 = (bf16[128,1,1024]{0,2,1:T(8,128)(2,1)}, bf16[128,1,1024]{0,2,1:T(8,128)(2,1)}, u32[]{:S(2)}, u32[]{:S(2)}) collective-permute-start(bf16[128,1,1024]{0,2,1:T(8,128)(2,1)} %get-tuple-element.16), channel_id=1, source_target_pairs={{0,1},{1,2},{2,3},{3,4},{4,5},{5,6},{6,7},{7,8},{8,9},{9,10},{10,1... | collective-permute-start | bytes 786440 | tf_op jit(solution)/shard_map/ppermute | solution.py:21
  51.9 1.5 collective-permute-start.3
  53.3 0.2 multiply_convert_fusion
  53.5 15.4 %fusion.15 = f32[3,3,3,64,128]{4,3,2,1,0:T(8,128)S(1)} fusion(bf16[1,64,1,32,32]{1,0,4,3,2:T(2,128)(2,1)S(1)} %copy.35, bf16[1,64,2,32,32]{1,0,4,3,2:T(2,128)(2,1)S(1)} %copy.34, bf16[1,64,1,32,32]{1,0,4,3,2:T(2,128)(2,1)S(1)} %copy.33, bf16[1,128,2,32,32]{1,4,3,2,0:T(8,128)(2,1)S(1)} %multiply_convert_fusion), kind=kOutput, calls=%fused_computation.17 | convolution fusion | flops 870408192 | bytes 1933312 | tf_op jit(solution)/shard_map/transpose(jvp())/conv_general_dilated | solution.py:176
  69.0 5.6 %select_maximum_fusion.x_ref = f32[9216,128]{1,0:T(8,128)} fusion(f32[3456,128]{1,0:T(8,128)S(1)} %copy-done.1, f32[3456,128]{1,0:T(8,128)S(1)} %copy-done, f32[1728,128]{1,0:T(8,128)S(1)} %bitcast.64), kind=kLoop, calls=%fused_computation | loop fusion | flops 7077888 | bytes 9142272 | tf_op jit(solution)/shard_map/concatenate | solution.py:143
  74.6 61.0 %shard_map.85 = (f32[1728,128]{1,0:T(8,128)}, f32[3456,256]{1,0:T(8,128)}) custom-call(f32[9216,128]{1,0:T(8,128)} %select_maximum_fusion.x_ref), custom_call_target="tpu_custom_call" | custom-call | tf_op jit(solution)/shard_map/pallas_call | solution.py:152
  135.6 0.0 collective-permute-done.2
  135.7 0.0 collective-permute-done.3
  135.7 1.2 maximum_bitcast_fusion
  136.8 0.4 copy.42
  137.2 0.2 pad.5.clone
  137.5 0.0 copy-start.5
  137.5 0.0 copy-start.9
  137.5 0.5 copy.28
  138.0 0.1 slice.28
  138.2 0.3 copy-done.5
  138.5 4.7 %fusion.12 = bf16[2,32,8,5,64]{4,2,3,1,0:T(8,128)(2,1)S(1)} fusion(bf16[3,3,3,128,64]{3,4,2,1,0:T(8,128)(2,1)S(1)} %bitcast.70, bf16[128,4,32,1,7,2]{0,4,5,2,1,3:T(8,128)(2,1)S(1)} %slice.28, bf16[128,4,32,1,8,5]{0,4,5,2,1,3:T(8,128)(2,1)S(1)} %copy.28, pred[8,5]{0,1:T(8,128)(4,1)S(1)} %copy-done.9), kind=kOutput, calls=%fused_computation.16 | convolution fusion | flops 1114701824 | bytes 2539560 | tf_op jit(solution)/shard_map/conv_general_dilated | solution.py:176
  143.2 0.1 copy.29
  143.4 1.0 copy.30
  144.4 2.2 %copy.41 = bf16[1,64,2,1024]{3,2,1,0:T(2,128)(2,1)} copy(bf16[1,64,2,1024]{1,3,2,0:T(8,128)(2,1)} %bitcast.60) | data formatting | bytes 524288
  146.6 2.2 %copy.49 = f32[27,64,128]{2,1,0:T(8,128)} copy(f32[27,64,128]{2,1,0:T(8,128)} %bitcast.65) | data formatting | bytes 1769472
  148.8 1.8 %copy.50 = f32[27,128,256]{2,1,0:T(8,128)} copy(f32[27,128,256]{2,1,0:T(8,128)S(1)} %bitcast.57) | data formatting | bytes 7077888
  (16 shorter events, 0.1 us)
Async XLA Ops:
  2.7 15.6 %copy-start.6 = (bf16[1,64,2,1024]{3,2,1,0:T(2,128)(2,1)S(1)}, bf16[1,64,2,1024]{3,2,1,0:T(2,128)(2,1)}, u32[]{:S(2)}) copy-start(bf16[1,64,2,1024]{3,2,1,0:T(2,128)(2,1)} %param.6) | copy-start | bytes 786436
  2.7 34.0 %collective-permute-start.1 = (bf16[256,1,256]{0,2,1:T(8,128)(2,1)S(1)}, bf16[256,1,256]{0,2,1:T(8,128)(2,1)}, u32[]{:S(2)}, u32[]{:S(2)}) collective-permute-start(bf16[256,1,256]{0,2,1:T(8,128)(2,1)S(1)} %bitcast.66), channel_id=1, source_target_pairs={{1,0},{2,1},{3,2},{4,3},{5,4},{6,5},{7,6},{8,7},{9,8},{10,9},{11,1... | collective-permute-start | bytes 393224 | tf_op jit(solution)/shard_map/ppermute | solution.py:23
  4.2 33.9 %collective-permute-start = (bf16[256,1,256]{0,2,1:T(8,128)(2,1)S(1)}, bf16[256,1,256]{0,2,1:T(8,128)(2,1)}, u32[]{:S(2)}, u32[]{:S(2)}) collective-permute-start(bf16[256,1,256]{0,2,1:T(8,128)(2,1)S(1)} %bitcast.67), channel_id=1, source_target_pairs={{0,1},{1,2},{2,3},{3,4},{4,5},{5,6},{6,7},{7,8},{8,9},{9,10},{10,1... | collective-permute-start | bytes 393224 | tf_op jit(solution)/shard_map/ppermute | solution.py:21
  11.4 12.0 %copy-start.4 = (bf16[27,64,128]{2,1,0:T(8,128)(2,1)S(1)}, bf16[27,64,128]{2,1,0:T(8,128)(2,1)}, u32[]{:S(2)}) copy-start(bf16[27,64,128]{2,1,0:T(8,128)(2,1)} %param.10) | copy-start | bytes 1327108
  12.4 16.8 %collective-permute-start.7 = (bf16[128,1,256]{0,2,1:T(8,128)(2,1)}, bf16[128,1,256]{0,2,1:T(8,128)(2,1)}, u32[]{:S(2)}, u32[]{:S(2)}) collective-permute-start(bf16[128,1,256]{0,2,1:T(8,128)(2,1)} %bitcast.28), channel_id=1, source_target_pairs={{1,0},{2,1},{3,2},{4,3},{5,4},{6,5},{7,6},{8,7},{9,8},{10,9},{11,1... | collective-permute-start | bytes 196616 | tf_op jit(solution)/shard_map/ppermute | solution.py:23
  13.7 17.7 %collective-permute-start.6 = (bf16[128,1,256]{0,2,1:T(8,128)(2,1)}, bf16[128,1,256]{0,2,1:T(8,128)(2,1)}, u32[]{:S(2)}, u32[]{:S(2)}) collective-permute-start(bf16[128,1,256]{0,2,1:T(8,128)(2,1)} %bitcast.28), channel_id=1, source_target_pairs={{0,1},{1,2},{2,3},{3,4},{4,5},{5,6},{6,7},{7,8},{8,9},{9,10},{10,1... | collective-permute-start | bytes 196616 | tf_op jit(solution)/shard_map/ppermute | solution.py:21
  19.5 19.8 %collective-permute-start.4 = (bf16[64,1,1024]{0,2,1:T(8,128)(2,1)}, bf16[64,1,1024]{0,2,1:T(8,128)(2,1)S(1)}, u32[]{:S(2)}, u32[]{:S(2)}) collective-permute-start(bf16[64,1,1024]{0,2,1:T(8,128)(2,1)} %get-tuple-element.12), channel_id=1, source_target_pairs={{0,1},{1,2},{2,3},{3,4},{4,5},{5,6},{6,7},{7,8},{8,9},{9,10},{10,1... | collective-permute-start | bytes 393224 | tf_op jit(solution)/shard_map/ppermute | solution.py:21
  25.3 3.9 %copy-start.8 = (bf16[64,1,1024]{0,2,1:T(8,128)(2,1)S(1)}, bf16[64,1,1024]{0,2,1:T(8,128)(2,1)}, u32[]{:S(2)}) copy-start(bf16[64,1,1024]{0,2,1:T(8,128)(2,1)} %get-tuple-element.13) | copy-start | bytes 393220
  29.2 10.6 %collective-permute-start.5 = (bf16[64,1,1024]{0,2,1:T(8,128)(2,1)S(1)}, bf16[64,1,1024]{0,2,1:T(8,128)(2,1)S(1)}, u32[]{:S(2)}, u32[]{:S(2)}) collective-permute-start(bf16[64,1,1024]{0,2,1:T(8,128)(2,1)S(1)} %copy-done.8), channel_id=1, source_target_pairs={{1,0},{2,1},{3,2},{4,3},{5,4},{6,5},{7,6},{8,7},{9,8},{10,9},{11,1... | collective-permute-start | bytes 393224 | tf_op jit(solution)/shard_map/ppermute | solution.py:23
  36.7 3.7 %copy-start.3 = (bf16[27,128,256]{2,1,0:T(8,128)(2,1)S(1)}, bf16[27,128,256]{2,1,0:T(8,128)(2,1)}, u32[]{:S(2)}) copy-start(bf16[27,128,256]{2,1,0:T(8,128)(2,1)} %rev.6) | copy-start | bytes 5308420
  36.7 3.7 %copy-start.7 = (bf16[1,256,1,16,16]{1,0,4,3,2:T(2,128)(2,1)S(1)}, bf16[1,256,1,16,16]{1,0,4,3,2:T(2,128)(2,1)}, u32[]{:S(2)}) copy-start(bf16[1,256,1,16,16]{1,0,4,3,2:T(2,128)(2,1)} %copy.23) | copy-start | bytes 393220
  45.2 90.5 %collective-permute-start.2 = (bf16[128,1,1024]{0,2,1:T(8,128)(2,1)}, bf16[128,1,1024]{0,2,1:T(8,128)(2,1)}, u32[]{:S(2)}, u32[]{:S(2)}) collective-permute-start(bf16[128,1,1024]{0,2,1:T(8,128)(2,1)} %get-tuple-element.16), channel_id=1, source_target_pairs={{0,1},{1,2},{2,3},{3,4},{4,5},{5,6},{6,7},{7,8},{8,9},{9,10},{10,1... | collective-permute-start | bytes 786440 | tf_op jit(solution)/shard_map/ppermute | solution.py:21
  51.9 83.8 %collective-permute-start.3 = (bf16[128,1,1024]{0,2,1:T(8,128)(2,1)}, bf16[128,1,1024]{0,2,1:T(8,128)(2,1)}, u32[]{:S(2)}, u32[]{:S(2)}) collective-permute-start(bf16[128,1,1024]{0,2,1:T(8,128)(2,1)} %get-tuple-element.17), channel_id=1, source_target_pairs={{1,0},{2,1},{3,2},{4,3},{5,4},{6,5},{7,6},{8,7},{9,8},{10,9},{11,1... | collective-permute-start | bytes 786440 | tf_op jit(solution)/shard_map/ppermute | solution.py:23
  53.5 15.4 %copy-start = (f32[3456,128]{1,0:T(8,128)S(1)}, f32[3456,128]{1,0:T(8,128)}, u32[]{:S(2)}) copy-start(f32[3456,128]{1,0:T(8,128)} %get-tuple-element.10) | copy-start | bytes 5308420
  53.5 15.4 %copy-start.1 = (f32[3456,128]{1,0:T(8,128)S(1)}, f32[3456,128]{1,0:T(8,128)}, u32[]{:S(2)}) copy-start(f32[3456,128]{1,0:T(8,128)} %get-tuple-element.11) | copy-start | bytes 5308420
  137.5 1.0 copy-start.5
  137.5 1.0 copy-start.9
  143.3 5.4 %copy-start.2 = (f32[3456,256]{1,0:T(8,128)S(1)}, f32[3456,256]{1,0:T(8,128)}, u32[]{:S(2)}) copy-start(f32[3456,256]{1,0:T(8,128)} %get-tuple-element.6) | copy-start | bytes 10616836
where the time goes:
time: 151 us
  Pallas kernels  61 us (40%)
  local copies, waits for them, and re-layouts  28.8 us (19%)
  matrix products  25.9 us (17%)
  starting transfers between devices  24.7 us (16%)
  other arithmetic  9.05 us (6%)
    pallas_call x1, Pallas kernels, all_reduce(): pl.pallas_call(_all_reduce_kernel, out_shape=(jax.ShapeDtypeStruct((rows_...  61 us
    conv_general_dilated x4, matrix products, conv_cells(): lax.conv_general_dilated(field[None], shaped, (1, 1, 1), ((0, 0), (1, 1),...  25.9 us
    ppermute x4, starting transfers between devices, padded_2(): lax.ppermute(tail, axis, [(i, (i + 1) % count) for i in range(ends)])  19.3 us
    unnamed x28, local copies, waits for them, and re-layouts  10.6 us
    concatenate x8, local copies, waits for them, and re-layouts, padded_2(): jnp.concatenate([lax.ppermute(tail, axis, [(i, (i + 1) % count) for i in...  6.82 us
    concatenate x1, other arithmetic, all_reduce(): jnp.concatenate([sums_a.reshape(rows_a, 128) * scale_a, wide[:, :128], wi...  5.63 us
    ppermute x4, starting transfers between devices, padded_2(): lax.ppermute(head, axis, [((i + 1) % count, i) for i in range(ends)])  5.45 us
    rev x2, local copies, waits for them, and re-layouts, back_cells(): flipped = kernel[::-1].transpose(0, 2, 1)  3.67 us
  transfers between devices with their start and end apart: 8, of which 0 were waited for; matrix products, arithmetic and copies ran while one was open for 28% of the time, Pallas kernels for 41%

commit v1 on v0

--- a/solution.py
+++ b/solution.py
@@ -95,7 +95,13 @@
         for copy in copies:
             copy.wait()
 
-    exchange([(x_ref.at[rows_at((1 - core) * half, half)], recv_a, partner)])
+    chunk = half // 8
+    exchange(
+        [
+            (x_ref.at[rows_at((1 - core) * half + n * chunk, chunk)], recv_a.at[rows_at(n * chunk, chunk)], partner)
+            for n in range(8)
+        ]
+    )
     acc_a[...] = x_ref[rows_at(core * half, half), :] + recv_a[...]
     triples = []
     for p, order in enumerate(orders):
@@ -128,8 +134,12 @@
         spans.append((outer, own, order))
     exchange([(full.at[rows_at(own, piece)], full.at[rows_at(own, piece)], peer(order[1], k)) for outer, own, order in spans for k in (1, 2, 3)])
     exchange([(full.at[rows_at(outer, quarter)], full.at[rows_at(outer, quarter)], peer(order[0], k)) for outer, own, order in spans for k in (1, 2, 3)])
-    block = full.at[rows_at(core * half, half)]
-    exchange([(block, block, partner)])
+    exchange(
+        [
+            (full.at[rows_at(core * half + n * chunk, chunk)], full.at[rows_at(core * half + n * chunk, chunk)], partner)
+            for n in range(8)
+        ]
+    )
     rows_a, rows_b = o_a.shape[0], o_b.shape[0]
     o_a[...] = full[0:rows_a, :]
     o_b[:, 0:128] = full[rows_a : rows_a + rows_b, :]
@@ -163,8 +173,8 @@
             pltpu.VMEM((3, 3, piece, 128), f32),
             pltpu.VMEM((3, piece, 128), f32),
             pltpu.VMEM((3, 4, piece, 128), f32),
-            pltpu.SemaphoreType.DMA((47,)),
-            pltpu.SemaphoreType.DMA((47,)),
+            pltpu.SemaphoreType.DMA((61,)),
+            pltpu.SemaphoreType.DMA((61,)),
         ],
         compiler_params=pltpu.CompilerParams(collective_id=0, has_side_effects=True),
     )(flat)

time: 151 us -> 151 us (level)
  no operation moved by 1% of the time
where the time goes in v1:
time: 151 us
  Pallas kernels  61.3 us (41%)
  local copies, waits for them, and re-layouts  28.8 us (19%)
  matrix products  26 us (17%)
  starting transfers between devices  24.7 us (16%)
  other arithmetic  9.05 us (6%)
    pallas_call x1, Pallas kernels, all_reduce(): pl.pallas_call(_all_reduce_kernel, out_shape=(jax.ShapeDtypeStruct((rows_...  61.3 us
    conv_general_dilated x4, matrix products, conv_cells(): lax.conv_general_dilated(field[None], shaped, (1, 1, 1), ((0, 0), (1, 1),...  26 us
    ppermute x4, starting transfers between devices, padded_2(): lax.ppermute(tail, axis, [(i, (i + 1) % count) for i in range(ends)])  19.3 us
    unnamed x28, local copies, waits for them, and re-layouts  10.6 us
    concatenate x8, local copies, waits for them, and re-layouts, padded_2(): jnp.concatenate([lax.ppermute(tail, axis, [(i, (i + 1) % count) for i in...  6.82 us
    concatenate x1, other arithmetic, all_reduce(): jnp.concatenate([sums_a.reshape(rows_a, 128) * scale_a, wide[:, :128], wi...  5.63 us
    ppermute x4, starting transfers between devices, padded_2(): lax.ppermute(head, axis, [((i + 1) % count, i) for i in range(ends)])  5.45 us
    rev x2, local copies, waits for them, and re-layouts, back_cells(): flipped = kernel[::-1].transpose(0, 2, 1)  3.67 us
  transfers between devices with their start and end apart: 8, of which 0 were waited for; matrix products, arithmetic and copies ran while one was open for 28% of the time, Pallas kernels for 41%

profile of v1, /device:TPU:1, one launch (start us, length us, event | category | flops | bytes accessed | tf_op | source)
XLA Modules:
  0.0 150.8 jit_solution(15786217139602830479)
XLA Ops:
  0.6 1.0 copy.21
  1.6 1.0 copy.20
  2.6 0.1 multiply_convert_fusion.1
  2.7 0.0 copy-start.6
  2.7 1.4 collective-permute-start.1
  4.2 5.6 %collective-permute-start = (bf16[256,1,256]{0,2,1:T(8,128)(2,1)S(1)}, bf16[256,1,256]{0,2,1:T(8,128)(2,1)}, u32[]{:S(2)}, u32[]{:S(2)}) collective-permute-start(bf16[256,1,256]{0,2,1:T(8,128)(2,1)S(1)} %bitcast.67), channel_id=1, source_target_pairs={{0,1},{1,2},{2,3},{3,4},{4,5},{5,6},{6,7},{7,8},{8,9},{9,10},{10,1... | collective-permute-start | bytes 393224 | tf_op jit(solution)/shard_map/ppermute | solution.py:21
  9.8 1.4 copy.25
  11.2 0.2 fusion.16
  11.4 0.0 copy-start.4
  11.4 0.4 reduce_sum.18
  11.8 0.6 multiply_convert_fusion.2
  12.4 1.3 collective-permute-start.7
  13.7 4.6 %collective-permute-start.6 = (bf16[128,1,256]{0,2,1:T(8,128)(2,1)}, bf16[128,1,256]{0,2,1:T(8,128)(2,1)}, u32[]{:S(2)}, u32[]{:S(2)}) collective-permute-start(bf16[128,1,256]{0,2,1:T(8,128)(2,1)} %bitcast.28), channel_id=1, source_target_pairs={{0,1},{1,2},{2,3},{3,4},{4,5},{5,6},{6,7},{7,8},{8,9},{9,10},{10,1... | collective-permute-start | bytes 196616 | tf_op jit(solution)/shard_map/ppermute | solution.py:21
  18.3 0.0 copy-done.6
  18.3 0.3 copy.31
  18.6 0.8 fusion.36
  19.5 2.3 %collective-permute-start.4 = (bf16[64,1,1024]{0,2,1:T(8,128)(2,1)}, bf16[64,1,1024]{0,2,1:T(8,128)(2,1)S(1)}, u32[]{:S(2)}, u32[]{:S(2)}) collective-permute-start(bf16[64,1,1024]{0,2,1:T(8,128)(2,1)} %get-tuple-element.12), channel_id=1, source_target_pairs={{0,1},{1,2},{2,3},{3,4},{4,5},{5,6},{6,7},{7,8},{8,9},{9,10},{10,1... | collective-permute-start | bytes 393224 | tf_op jit(solution)/shard_map/ppermute | solution.py:21
  21.8 0.6 fusion.40
  22.4 0.9 copy.23
  23.4 0.8 rev.7
  24.2 1.1 copy.34
  25.3 1.0 copy.38
  26.3 2.9 %rev.6 = bf16[27,128,256]{2,1,0:T(8,128)(2,1)} reverse(bf16[27,128,256]{2,1,0:T(8,128)(2,1)} %param.11), dimensions={0} | reverse | bytes 3538944 | tf_op jit(solution)/shard_map/rev | solution.py:198
  29.2 0.0 collective-permute-done.7
  29.2 1.3 collective-permute-start.5
  30.5 0.9 copy.39
  31.4 0.0 collective-permute-done.6
  31.4 0.9 copy.37
  32.4 2.4 %convolution_multiply_fusion = f32[3,3,3,128,256]{4,3,2,1,0:T(8,128)S(1)} fusion(bf16[1,128,1,16,16]{1,0,4,3,2:T(2,128)(2,1)S(1)} %copy.39, bf16[1,128,1,16,16]{1,0,4,3,2:T(2,128)(2,1)S(1)} %copy.38, bf16[1,128,1,16,16]{1,0,4,3,2:T(2,128)(2,1)S(1)} %copy.37, bf16[1,256,1,16,16]{1,4,3,2,0:T(8,128)(2,1)S(1)} %bitcast.69), kind=kOutput, calls=%fused_computation.7 | convolution fusion | flops 417497088 | bytes 3866624 | tf_op jit(solution)/shard_map/transpose(jvp())/conv_general_dilated | solution.py:186
  34.8 2.0 %fusion.35 = (f32[3456,128]{1,0:T(8,128)}, f32[3456,128]{1,0:T(8,128)}) fusion(f32[3456,256]{1,0:T(8,128)S(1)} %bitcast.58), kind=kLoop, calls=%fused_computation.47 | loop fusion | bytes 7077888 | tf_op jit(solution)/shard_map/slice | solution.py:153
  36.7 0.0 collective-permute-done.1
  36.7 1.3 copy.24
  38.1 0.0 collective-permute-done
  38.1 1.2 copy.22
  39.2 0.0 collective-permute-done.4
  39.2 0.6 copy.33
  39.8 0.0 collective-permute-done.5
  39.8 0.6 copy.35
  40.4 3.4 %convolution_multiply_fusion.1 = f32[1,128,1,16,16]{1,0,4,3,2:T(1,128)S(1)} fusion(bf16[3,3,3,256,128]{3,4,2,1,0:T(8,128)(2,1)S(1)} %bitcast.62, bf16[1,256,1,16,16]{1,0,4,3,2:T(2,128)(2,1)S(1)} %copy.24, bf16[1,256,1,16,16]{1,0,4,3,2:T(2,128)(2,1)S(1)} %copy-done.7, bf16[1,256,1,16,16]{1,0,4,3,2:T(2,128)(2,1)S(1)} %copy.22), kind=kOutput, calls=%fused_computation.19 | convolution fusion | flops 417234944 | bytes 2293760 | tf_op jit(solution)/shard_map/conv_general_dilated | solution.py:186
  43.9 0.3 broadcast_in_dim.23
  44.2 0.2 fusion.17
  44.4 0.8 fusion.37
  45.2 6.7 %collective-permute-start.2 = (bf16[128,1,1024]{0,2,1:T(8,128)(2,1)}, bf16[128,1,1024]{0,2,1:T(8,128)(2,1)}, u32[]{:S(2)}, u32[]{:S(2)}) collective-permute-start(bf16[128,1,1024]{0,2,1:T(8,128)(2,1)} %get-tuple-element.16), channel_id=1, source_target_pairs={{0,1},{1,2},{2,3},{3,4},{4,5},{5,6},{6,7},{7,8},{8,9},{9,10},{10,1... | collective-permute-start | bytes 786440 | tf_op jit(solution)/shard_map/ppermute | solution.py:21
  51.9 1.5 collective-permute-start.3
  53.3 0.2 multiply_convert_fusion
  53.5 15.4 %fusion.15 = f32[3,3,3,64,128]{4,3,2,1,0:T(8,128)S(1)} fusion(bf16[1,64,1,32,32]{1,0,4,3,2:T(2,128)(2,1)S(1)} %copy.35, bf16[1,64,2,32,32]{1,0,4,3,2:T(2,128)(2,1)S(1)} %copy.34, bf16[1,64,1,32,32]{1,0,4,3,2:T(2,128)(2,1)S(1)} %copy.33, bf16[1,128,2,32,32]{1,4,3,2,0:T(8,128)(2,1)S(1)} %multiply_convert_fusion), kind=kOutput, calls=%fused_computation.17 | convolution fusion | flops 870408192 | bytes 1933312 | tf_op jit(solution)/shard_map/transpose(jvp())/conv_general_dilated | solution.py:186
  69.0 5.6 %select_maximum_fusion.x_ref = f32[9216,128]{1,0:T(8,128)} fusion(f32[3456,128]{1,0:T(8,128)S(1)} %copy-done.1, f32[3456,128]{1,0:T(8,128)S(1)} %copy-done, f32[1728,128]{1,0:T(8,128)S(1)} %bitcast.64), kind=kLoop, calls=%fused_computation | loop fusion | flops 7077888 | bytes 9142272 | tf_op jit(solution)/shard_map/concatenate | solution.py:153
  74.6 61.3 %shard_map.85 = (f32[1728,128]{1,0:T(8,128)}, f32[3456,256]{1,0:T(8,128)}) custom-call(f32[9216,128]{1,0:T(8,128)} %select_maximum_fusion.x_ref), custom_call_target="tpu_custom_call" | custom-call | tf_op jit(solution)/shard_map/pallas_call | solution.py:162
  135.9 0.0 collective-permute-done.2
  135.9 0.0 collective-permute-done.3
  135.9 1.2 maximum_bitcast_fusion
  137.1 0.4 copy.42
  137.5 0.2 pad.5.clone
  137.7 0.0 copy-start.5
  137.7 0.0 copy-start.9
  137.7 0.5 copy.28
  138.3 0.1 slice.28
  138.4 0.3 copy-done.5
  138.7 4.7 %fusion.12 = bf16[2,32,8,5,64]{4,2,3,1,0:T(8,128)(2,1)S(1)} fusion(bf16[3,3,3,128,64]{3,4,2,1,0:T(8,128)(2,1)S(1)} %bitcast.70, bf16[128,4,32,1,7,2]{0,4,5,2,1,3:T(8,128)(2,1)S(1)} %slice.28, bf16[128,4,32,1,8,5]{0,4,5,2,1,3:T(8,128)(2,1)S(1)} %copy.28, pred[8,5]{0,1:T(8,128)(4,1)S(1)} %copy-done.9), kind=kOutput, calls=%fused_computation.16 | convolution fusion | flops 1114701824 | bytes 2539560 | tf_op jit(solution)/shard_map/conv_general_dilated | solution.py:186
  143.5 0.1 copy.29
  143.7 1.0 copy.30
  144.6 2.2 %copy.41 = bf16[1,64,2,1024]{3,2,1,0:T(2,128)(2,1)} copy(bf16[1,64,2,1024]{1,3,2,0:T(8,128)(2,1)} %bitcast.60) | data formatting | bytes 524288
  146.8 2.2 %copy.49 = f32[27,64,128]{2,1,0:T(8,128)} copy(f32[27,64,128]{2,1,0:T(8,128)} %bitcast.65) | data formatting | bytes 1769472
  149.0 1.8 %copy.50 = f32[27,128,256]{2,1,0:T(8,128)} copy(f32[27,128,256]{2,1,0:T(8,128)S(1)} %bitcast.57) | data formatting | bytes 7077888
  (16 shorter events, 0.1 us)
Async XLA Ops:
  2.7 15.6 %copy-start.6 = (bf16[1,64,2,1024]{3,2,1,0:T(2,128)(2,1)S(1)}, bf16[1,64,2,1024]{3,2,1,0:T(2,128)(2,1)}, u32[]{:S(2)}) copy-start(bf16[1,64,2,1024]{3,2,1,0:T(2,128)(2,1)} %param.6) | copy-start | bytes 786436
  2.7 34.0 %collective-permute-start.1 = (bf16[256,1,256]{0,2,1:T(8,128)(2,1)S(1)}, bf16[256,1,256]{0,2,1:T(8,128)(2,1)}, u32[]{:S(2)}, u32[]{:S(2)}) collective-permute-start(bf16[256,1,256]{0,2,1:T(8,128)(2,1)S(1)} %bitcast.66), channel_id=1, source_target_pairs={{1,0},{2,1},{3,2},{4,3},{5,4},{6,5},{7,6},{8,7},{9,8},{10,9},{11,1... | collective-permute-start | bytes 393224 | tf_op jit(solution)/shard_map/ppermute | solution.py:23
  4.2 33.9 %collective-permute-start = (bf16[256,1,256]{0,2,1:T(8,128)(2,1)S(1)}, bf16[256,1,256]{0,2,1:T(8,128)(2,1)}, u32[]{:S(2)}, u32[]{:S(2)}) collective-permute-start(bf16[256,1,256]{0,2,1:T(8,128)(2,1)S(1)} %bitcast.67), channel_id=1, source_target_pairs={{0,1},{1,2},{2,3},{3,4},{4,5},{5,6},{6,7},{7,8},{8,9},{9,10},{10,1... | collective-permute-start | bytes 393224 | tf_op jit(solution)/shard_map/ppermute | solution.py:21
  11.4 12.0 %copy-start.4 = (bf16[27,64,128]{2,1,0:T(8,128)(2,1)S(1)}, bf16[27,64,128]{2,1,0:T(8,128)(2,1)}, u32[]{:S(2)}) copy-start(bf16[27,64,128]{2,1,0:T(8,128)(2,1)} %param.10) | copy-start | bytes 1327108
  12.4 16.8 %collective-permute-start.7 = (bf16[128,1,256]{0,2,1:T(8,128)(2,1)}, bf16[128,1,256]{0,2,1:T(8,128)(2,1)}, u32[]{:S(2)}, u32[]{:S(2)}) collective-permute-start(bf16[128,1,256]{0,2,1:T(8,128)(2,1)} %bitcast.28), channel_id=1, source_target_pairs={{1,0},{2,1},{3,2},{4,3},{5,4},{6,5},{7,6},{8,7},{9,8},{10,9},{11,1... | collective-permute-start | bytes 196616 | tf_op jit(solution)/shard_map/ppermute | solution.py:23
  13.7 17.7 %collective-permute-start.6 = (bf16[128,1,256]{0,2,1:T(8,128)(2,1)}, bf16[128,1,256]{0,2,1:T(8,128)(2,1)}, u32[]{:S(2)}, u32[]{:S(2)}) collective-permute-start(bf16[128,1,256]{0,2,1:T(8,128)(2,1)} %bitcast.28), channel_id=1, source_target_pairs={{0,1},{1,2},{2,3},{3,4},{4,5},{5,6},{6,7},{7,8},{8,9},{9,10},{10,1... | collective-permute-start | bytes 196616 | tf_op jit(solution)/shard_map/ppermute | solution.py:21
  19.5 19.8 %collective-permute-start.4 = (bf16[64,1,1024]{0,2,1:T(8,128)(2,1)}, bf16[64,1,1024]{0,2,1:T(8,128)(2,1)S(1)}, u32[]{:S(2)}, u32[]{:S(2)}) collective-permute-start(bf16[64,1,1024]{0,2,1:T(8,128)(2,1)} %get-tuple-element.12), channel_id=1, source_target_pairs={{0,1},{1,2},{2,3},{3,4},{4,5},{5,6},{6,7},{7,8},{8,9},{9,10},{10,1... | collective-permute-start | bytes 393224 | tf_op jit(solution)/shard_map/ppermute | solution.py:21
  25.3 3.9 %copy-start.8 = (bf16[64,1,1024]{0,2,1:T(8,128)(2,1)S(1)}, bf16[64,1,1024]{0,2,1:T(8,128)(2,1)}, u32[]{:S(2)}) copy-start(bf16[64,1,1024]{0,2,1:T(8,128)(2,1)} %get-tuple-element.13) | copy-start | bytes 393220
  29.2 10.6 %collective-permute-start.5 = (bf16[64,1,1024]{0,2,1:T(8,128)(2,1)S(1)}, bf16[64,1,1024]{0,2,1:T(8,128)(2,1)S(1)}, u32[]{:S(2)}, u32[]{:S(2)}) collective-permute-start(bf16[64,1,1024]{0,2,1:T(8,128)(2,1)S(1)} %copy-done.8), channel_id=1, source_target_pairs={{1,0},{2,1},{3,2},{4,3},{5,4},{6,5},{7,6},{8,7},{9,8},{10,9},{11,1... | collective-permute-start | bytes 393224 | tf_op jit(solution)/shard_map/ppermute | solution.py:23
  36.7 3.7 %copy-start.3 = (bf16[27,128,256]{2,1,0:T(8,128)(2,1)S(1)}, bf16[27,128,256]{2,1,0:T(8,128)(2,1)}, u32[]{:S(2)}) copy-start(bf16[27,128,256]{2,1,0:T(8,128)(2,1)} %rev.6) | copy-start | bytes 5308420
  36.7 3.7 %copy-start.7 = (bf16[1,256,1,16,16]{1,0,4,3,2:T(2,128)(2,1)S(1)}, bf16[1,256,1,16,16]{1,0,4,3,2:T(2,128)(2,1)}, u32[]{:S(2)}) copy-start(bf16[1,256,1,16,16]{1,0,4,3,2:T(2,128)(2,1)} %copy.23) | copy-start | bytes 393220
  45.2 90.7 %collective-permute-start.2 = (bf16[128,1,1024]{0,2,1:T(8,128)(2,1)}, bf16[128,1,1024]{0,2,1:T(8,128)(2,1)}, u32[]{:S(2)}, u32[]{:S(2)}) collective-permute-start(bf16[128,1,1024]{0,2,1:T(8,128)(2,1)} %get-tuple-element.16), channel_id=1, source_target_pairs={{0,1},{1,2},{2,3},{3,4},{4,5},{5,6},{6,7},{7,8},{8,9},{9,10},{10,1... | collective-permute-start | bytes 786440 | tf_op jit(solution)/shard_map/ppermute | solution.py:21
  51.9 84.0 %collective-permute-start.3 = (bf16[128,1,1024]{0,2,1:T(8,128)(2,1)}, bf16[128,1,1024]{0,2,1:T(8,128)(2,1)}, u32[]{:S(2)}, u32[]{:S(2)}) collective-permute-start(bf16[128,1,1024]{0,2,1:T(8,128)(2,1)} %get-tuple-element.17), channel_id=1, source_target_pairs={{1,0},{2,1},{3,2},{4,3},{5,4},{6,5},{7,6},{8,7},{9,8},{10,9},{11,1... | collective-permute-start | bytes 786440 | tf_op jit(solution)/shard_map/ppermute | solution.py:23
  53.5 15.4 %copy-start = (f32[3456,128]{1,0:T(8,128)S(1)}, f32[3456,128]{1,0:T(8,128)}, u32[]{:S(2)}) copy-start(f32[3456,128]{1,0:T(8,128)} %get-tuple-element.10) | copy-start | bytes 5308420
  53.5 15.4 %copy-start.1 = (f32[3456,128]{1,0:T(8,128)S(1)}, f32[3456,128]{1,0:T(8,128)}, u32[]{:S(2)}) copy-start(f32[3456,128]{1,0:T(8,128)} %get-tuple-element.11) | copy-start | bytes 5308420
  137.7 1.0 copy-start.5
  137.7 1.0 copy-start.9
  143.6 5.4 %copy-start.2 = (f32[3456,256]{1,0:T(8,128)S(1)}, f32[3456,256]{1,0:T(8,128)}, u32[]{:S(2)}) copy-start(f32[3456,256]{1,0:T(8,128)} %get-tuple-element.6) | copy-start | bytes 10616836

commit v2 on v0

--- a/solution.py
+++ b/solution.py
@@ -190,11 +190,25 @@
 
 
 def kernel_terms(padded, upstream):
-    taps, chan_in, chan_out = 27, padded.shape[0], upstream.shape[0]
-    start = jnp.zeros((taps, chan_in, chan_out), jnp.float32)
-    field = padded.astype(jnp.float32)
-    unused, pull = jax.vjp(lambda w: conv_cells(field, w), start)
-    return pull(upstream.astype(jnp.float32))[0]
+    chan_in, chan_out = padded.shape[0], upstream.shape[0]
+    depth, rows, cols = upstream.shape[1:]
+    wider = jnp.pad(padded, ((0, 0), (0, 0), (1, 1), (1, 1)))
+    windows = jnp.stack(
+        [
+            wider[:, a : a + depth, b : b + rows, c : c + cols]
+            for a in range(3)
+            for b in range(3)
+            for c in range(3)
+        ]
+    )
+    cells = depth * rows * cols
+    sums = lax.dot_general(
+        windows.reshape(27 * chan_in, cells),
+        upstream.reshape(chan_out, cells),
+        (((1,), (1,)), ((), ())),
+        preferred_element_type=jnp.float32,
+    )
+    return sums.reshape(27, chan_in, chan_out)
 
 
 def per_device(layer_input, hidden_pre, output_pre, output_grad, weight_a, weight_b):

time: 151 us -> 186 us (1.23); the launches traced: 151 us -> 184 us
  local copies, waits for them, and re-layouts: 28.8 us -> 66.9 us
  matrix products: 25.9 us -> 14.5 us
  waiting for transfers between devices: 0.02 us -> 7.88 us
  starting transfers between devices: 24.7 us -> 21.1 us
  other arithmetic: 9.05 us -> 12.3 us
    reshape x0 -> x1, local copies, waits for them, and re-layouts: none -> 21.7 us  [kernel_terms(): windows.reshape(27 * chan_in, cells)]
    conv_general_dilated x4 -> x2, matrix products: 25.9 us -> 9.72 us  [conv_cells(): lax.conv_general_dilated(field[None], shaped, (1, 1, 1), ((0, 0), (1, 1),...]
    another operation x0 -> x4, local copies, waits for them, and re-layouts: none -> 14.4 us  [kernel_terms(): jnp.stack([wider[:, a:a + depth, b:b + rows, c:c + cols] for a in range(3...]
    unnamed x28 -> x78, local copies, waits for them, and re-layouts: 10.6 us -> 18.3 us
    dot_general x0 -> x2, matrix products: none -> 4.81 us  [kernel_terms(): lax.dot_general(windows.reshape(27 * chan_in, cells), upstream.reshape(ch...]
    concatenate x8 -> x3, local copies, waits for them, and re-layouts: 6.82 us -> 2.53 us  [padded_2(): jnp.concatenate([lax.ppermute(tail, axis, [(i, (i + 1) % count) for i in...]
    ppermute x4, waiting for transfers between devices: 0.01 us -> 4.07 us  [padded_2(): lax.ppermute(tail, axis, [(i, (i + 1) % count) for i in range(ends)])]
    ppermute x4, waiting for transfers between devices: 0.01 us -> 3.82 us  [padded_2(): lax.ppermute(head, axis, [((i + 1) % count, i) for i in range(ends)])]
  transfers between devices with their start and end apart: 8 -> 8, of which waited for: 0 -> 2; matrix products, arithmetic and copies ran while one was open for 28% -> 33% of each run, Pallas kernels for 41% -> 0%
where the time goes in v2:
time: 186 us; the launch traced here: 184 us
  local copies, waits for them, and re-layouts  66.9 us (36%)
  Pallas kernels  59.5 us (32%)
  starting transfers between devices  21.1 us (11%)
  matrix products  14.5 us (8%)
  other arithmetic  12.3 us (7%)
  waiting for transfers between devices  7.88 us (4%)
    pallas_call x1, Pallas kernels, all_reduce(): pl.pallas_call(_all_reduce_kernel, out_shape=(jax.ShapeDtypeStruct((rows_...  59.5 us
    reshape x1, local copies, waits for them, and re-layouts, kernel_terms(): windows.reshape(27 * chan_in, cells)  21.7 us
    unnamed x78, local copies, waits for them, and re-layouts  18.3 us
    ppermute x4, starting transfers between devices, padded_2(): lax.ppermute(tail, axis, [(i, (i + 1) % count) for i in range(ends)])  16 us
    another operation x4, local copies, waits for them, and re-layouts, kernel_terms(): jnp.stack([wider[:, a:a + depth, b:b + rows, c:c + cols] for a in range(3...  14.4 us
    conv_general_dilated x2, matrix products, conv_cells(): lax.conv_general_dilated(field[None], shaped, (1, 1, 1), ((0, 0), (1, 1),...  9.72 us
    concatenate x1, other arithmetic, all_reduce(): jnp.concatenate([sums_a.reshape(rows_a, 128) * scale_a, wide[:, :128], wi...  5.64 us
    ppermute x4, starting transfers between devices, padded_2(): lax.ppermute(head, axis, [((i + 1) % count, i) for i in range(ends)])  5.13 us
  transfers between devices with their start and end apart: 8, of which 2 were waited for; matrix products, arithmetic and copies ran while one was open for 33% of the time, Pallas kernels for 0%

profile of v2, /device:TPU:1, one launch (start us, length us, event | category | flops | bytes accessed | tf_op | source)
XLA Modules:
  0.0 183.5 jit_solution(14700678238749590902)
XLA Ops:
  0.6 1.0 copy.19
  1.6 1.0 copy.20
  2.6 0.7 multiply_convert_fusion.2
  3.3 5.0 %collective-permute-start = (bf16[256,1,256]{0,2,1:T(8,128)(2,1)}, bf16[256,1,256]{0,2,1:T(8,128)(2,1)}, u32[]{:S(2)}, u32[]{:S(2)}) collective-permute-start(bf16[256,1,256]{0,2,1:T(8,128)(2,1)} %bitcast), channel_id=1, source_target_pairs={{0,1},{1,2},{2,3},{3,4},{4,5},{5,6},{6,7},{7,8},{8,9},{9,10},{10,1... | collective-permute-start | bytes 393224 | tf_op jit(solution)/shard_map/ppermute | solution.py:21
  8.4 1.3 collective-permute-start.1
  9.7 1.4 copy.26
  11.3 0.4 reduce_sum.18
  11.7 0.6 multiply_convert_fusion.3
  12.3 4.6 %collective-permute-start.6 = (bf16[128,1,256]{0,2,1:T(8,128)(2,1)}, bf16[128,1,256]{0,2,1:T(8,128)(2,1)}, u32[]{:S(2)}, u32[]{:S(2)}) collective-permute-start(bf16[128,1,256]{0,2,1:T(8,128)(2,1)} %bitcast.56), channel_id=1, source_target_pairs={{0,1},{1,2},{2,3},{3,4},{4,5},{5,6},{6,7},{7,8},{8,9},{9,10},{10,1... | collective-permute-start | bytes 196616 | tf_op jit(solution)/shard_map/ppermute | solution.py:21
  16.9 1.3 collective-permute-start.7
  18.2 1.3 copy.33
  19.4 0.8 fusion.68
  20.3 4.7 %collective-permute-start.4 = (bf16[64,1,1024]{0,2,1:T(8,128)(2,1)}, bf16[64,1,1024]{0,2,1:T(8,128)(2,1)}, u32[]{:S(2)}, u32[]{:S(2)}) collective-permute-start(bf16[64,1,1024]{0,2,1:T(8,128)(2,1)} %get-tuple-element.12), channel_id=1, source_target_pairs={{0,1},{1,2},{2,3},{3,4},{4,5},{5,6},{6,7},{7,8},{8,9},{9,10},{10,1... | collective-permute-start | bytes 393224 | tf_op jit(solution)/shard_map/ppermute | solution.py:21
  25.0 1.9 %copy.22 = bf16[1,256,1,16,16]{1,0,4,3,2:T(2,128)(2,1)} copy(bf16[1,256,1,16,16]{1,4,3,2,0:T(8,128)(2,1)} %bitcast.2) | data formatting | bytes 262144 | tf_op jit(solution)/shard_map/mul | solution.py:226
  26.9 1.3 rev.6
  28.2 1.8 rev.7
  30.0 1.3 collective-permute-start.5
  31.3 1.0 select_maximum_fusion.4
  32.4 0.9 constant_dynamic-update-slice_fusion.23
  33.7 0.9 constant_dynamic-update-slice_fusion.5
  34.7 1.2 copy.38
  35.9 2.7 %convolution_multiply_fusion = f32[3456,256]{1,0:T(8,128)S(1)} fusion(bf16[32,8,27,128]{3,2,1,0:T(8,128)(2,1)S(1)} %bitcast.275, bf16[1,256,1,256]{1,3,2,0:T(8,128)(2,1)} %multiply_convert_fusion.2), kind=kOutput, calls=%fused_computation | convolution fusion | flops 453869568 | bytes 5439488 | tf_op jit(solution)/shard_map/dot_general | solution.py:205
  38.6 1.5 fusion.67
  40.1 1.5 select_maximum_fusion.2
  41.7 0.2 fusion.57
  41.9 0.2 fusion.56
  42.2 1.1 fusion.54
  43.3 0.2 fusion.52
  43.6 0.2 fusion.50
  43.9 0.2 fusion.49
  44.2 0.2 fusion.47
  44.4 0.2 fusion.46
  44.8 0.2 fusion.44
  45.1 0.2 fusion.42
  45.3 0.2 fusion.41
  45.6 0.2 fusion.39
  45.9 0.2 fusion.38
  46.3 0.2 fusion.34
  46.6 0.2 fusion.32
  46.9 0.2 fusion.31
  47.1 12.9 %copy.36 = bf16[27,64,2,32,32]{1,0,4,3,2:T(8,128)(2,1)} copy(bf16[27,64,2,32,32]{1,4,3,2,0:T(8,128)(2,1)S(1)} %fusion.31) | data formatting | bytes 14155776 | tf_op jit(solution)/shard_map/stack | solution.py:196
  60.0 21.7 %reshape.285 = bf16[1728,2048]{0,1:T(8,128)(2,1)} reshape(bf16[27,64,2,32,32]{1,0,4,3,2:T(8,128)(2,1)} %copy.36) | data formatting | bytes 14155776 | tf_op jit(solution)/shard_map/reshape | solution.py:206
  81.7 1.2 copy.21
  82.9 1.2 copy.23
  84.1 5.0 %convolution_multiply_fusion.2 = f32[1,128,1,16,16]{1,0,4,3,2:T(1,128)S(1)} fusion(bf16[3,3,3,256,128]{3,4,2,1,0:T(8,128)(2,1)} %bitcast.289, bf16[1,256,1,16,16]{1,0,4,3,2:T(2,128)(2,1)S(1)} %copy.23, bf16[1,256,1,16,16]{1,0,4,3,2:T(2,128)(2,1)S(1)} %copy-done.6, bf16[1,256,1,16,16]{1,0,4,3,2:T(2,128)(2,1)S(1)} %copy.21), kind=kOutput, calls=%fused_computation.31 | convolution fusion | flops 417234944 | bytes 2293760 | tf_op jit(solution)/shard_map/conv_general_dilated | solution.py:176
  89.4 0.5 multiply_convert_fusion
  90.0 2.1 %convolution_multiply_fusion.1 = f32[1728,128]{1,0:T(8,128)S(1)} fusion(bf16[1728,2048]{0,1:T(8,128)(2,1)S(1)} %bitcast.279, bf16[128,2048]{0,1:T(8,128)(2,1)S(1)} %bitcast.293), kind=kOutput, calls=%fused_computation.13 | convolution fusion | flops 906190848 | bytes 8486912 | tf_op jit(solution)/shard_map/dot_general | solution.py:205
  92.1 5.6 %select_maximum_fusion.x_ref = f32[9216,128]{1,0:T(8,128)} fusion(f32[3456,128]{1,0:T(8,128)S(1)} %copy-done, f32[3456,128]{1,0:T(8,128)S(1)} %get-tuple-element.10, f32[1728,128]{1,0:T(8,128)S(1)} %convolution_multiply_fusion.1), kind=kLoop, calls=%fused_computation.1 | loop fusion | flops 7077888 | bytes 9142272 | tf_op jit(solution)/shard_map/concatenate | solution.py:143
  97.8 59.5 %shard_map.85 = (f32[1728,128]{1,0:T(8,128)}, f32[3456,256]{1,0:T(8,128)}) custom-call(f32[9216,128]{1,0:T(8,128)} %select_maximum_fusion.x_ref), custom_call_target="tpu_custom_call" | custom-call | tf_op jit(solution)/shard_map/pallas_call | solution.py:152
  157.4 0.3 copy.27
  157.7 0.3 broadcast_in_dim.21.clone
  158.0 0.4 copy-done.2
  158.5 1.7 collective-permute-start.2
  160.3 1.3 collective-permute-start.3
  161.7 4.1 %collective-permute-done.2 = bf16[128,1,1024]{0,2,1:T(8,128)(2,1)S(1)} collective-permute-done((bf16[128,1,1024]{0,2,1:T(8,128)(2,1)S(1)}, bf16[128,1,1024]{0,2,1:T(8,128)(2,1)S(1)}, u32[]{:S(2)}, u32[]{:S(2)}) %collective-permute-start.2) | collective-permute-done | bytes 262176 | tf_op jit(solution)/shard_map/ppermute | solution.py:21
  165.8 3.8 %collective-permute-done.3 = bf16[128,1,1024]{0,2,1:T(8,128)(2,1)S(1)} collective-permute-done((bf16[128,1,1024]{0,2,1:T(8,128)(2,1)S(1)}, bf16[128,1,1024]{0,2,1:T(8,128)(2,1)S(1)}, u32[]{:S(2)}, u32[]{:S(2)}) %collective-permute-start.3) | collective-permute-done | bytes 262176 | tf_op jit(solution)/shard_map/ppermute | solution.py:23
  169.7 0.4 copy.41
  170.4 0.5 copy.30
  171.1 0.3 copy-done.5
  171.4 4.7 %fusion.19 = bf16[2,32,8,5,64]{4,2,3,1,0:T(8,128)(2,1)S(1)} fusion(bf16[3,3,3,128,64]{3,4,2,1,0:T(8,128)(2,1)S(1)} %bitcast.294, bf16[128,4,32,1,7,2]{0,4,5,2,1,3:T(8,128)(2,1)S(1)} %slice.240, bf16[128,4,32,1,8,5]{0,4,5,2,1,3:T(8,128)(2,1)S(1)} %copy.30, pred[8,5]{0,1:T(8,128)(4,1)S(1)} %copy-done.7), kind=kOutput, calls=%fused_computation.29 | convolution fusion | flops 1114701824 | bytes 2539560 | tf_op jit(solution)/shard_map/conv_general_dilated | solution.py:176
  176.3 1.0 copy.32
  177.3 2.2 %copy.39 = bf16[1,64,2,1024]{3,2,1,0:T(2,128)(2,1)} copy(bf16[1,64,2,1024]{1,3,2,0:T(8,128)(2,1)} %bitcast.287) | data formatting | bytes 524288
  179.5 2.2 %copy.101 = f32[27,64,128]{2,1,0:T(8,128)} copy(f32[27,64,128]{2,1,0:T(8,128)} %bitcast.292) | data formatting | bytes 1769472
  181.7 1.8 copy.102
  (75 shorter events, 3.1 us)
Async XLA Ops:
  3.3 78.4 %collective-permute-start = (bf16[256,1,256]{0,2,1:T(8,128)(2,1)}, bf16[256,1,256]{0,2,1:T(8,128)(2,1)}, u32[]{:S(2)}, u32[]{:S(2)}) collective-permute-start(bf16[256,1,256]{0,2,1:T(8,128)(2,1)} %bitcast), channel_id=1, source_target_pairs={{0,1},{1,2},{2,3},{3,4},{4,5},{5,6},{6,7},{7,8},{8,9},{9,10},{10,1... | collective-permute-start | bytes 393224 | tf_op jit(solution)/shard_map/ppermute | solution.py:21
  8.4 74.5 %collective-permute-start.1 = (bf16[256,1,256]{0,2,1:T(8,128)(2,1)}, bf16[256,1,256]{0,2,1:T(8,128)(2,1)}, u32[]{:S(2)}, u32[]{:S(2)}) collective-permute-start(bf16[256,1,256]{0,2,1:T(8,128)(2,1)} %bitcast), channel_id=1, source_target_pairs={{1,0},{2,1},{3,2},{4,3},{5,4},{6,5},{7,6},{8,7},{9,8},{10,9},{11,1... | collective-permute-start | bytes 393224 | tf_op jit(solution)/shard_map/ppermute | solution.py:23
  11.0 5.9 %copy-start.1 = (bf16[1,128,2,1024]{1,3,2,0:T(8,128)(2,1)}, bf16[1,128,2,1024]{1,3,2,0:T(8,128)(2,1)S(1)}, u32[]{:S(2)}) copy-start(bf16[1,128,2,1024]{1,3,2,0:T(8,128)(2,1)S(1)} %copy.26) | copy-start | bytes 1572868
  11.7 15.2 %copy-start.4 = (bf16[27,128,256]{2,1,0:T(8,128)(2,1)S(1)}, bf16[27,128,256]{2,1,0:T(8,128)(2,1)}, u32[]{:S(2)}) copy-start(bf16[27,128,256]{2,1,0:T(8,128)(2,1)} %param.11) | copy-start | bytes 5308420
  12.3 17.7 %collective-permute-start.6 = (bf16[128,1,256]{0,2,1:T(8,128)(2,1)}, bf16[128,1,256]{0,2,1:T(8,128)(2,1)}, u32[]{:S(2)}, u32[]{:S(2)}) collective-permute-start(bf16[128,1,256]{0,2,1:T(8,128)(2,1)} %bitcast.56), channel_id=1, source_target_pairs={{0,1},{1,2},{2,3},{3,4},{4,5},{5,6},{6,7},{7,8},{8,9},{9,10},{10,1... | collective-permute-start | bytes 196616 | tf_op jit(solution)/shard_map/ppermute | solution.py:21
  16.9 14.4 %collective-permute-start.7 = (bf16[128,1,256]{0,2,1:T(8,128)(2,1)}, bf16[128,1,256]{0,2,1:T(8,128)(2,1)}, u32[]{:S(2)}, u32[]{:S(2)}) collective-permute-start(bf16[128,1,256]{0,2,1:T(8,128)(2,1)} %bitcast.56), channel_id=1, source_target_pairs={{1,0},{2,1},{3,2},{4,3},{5,4},{6,5},{7,6},{8,7},{9,8},{10,9},{11,1... | collective-permute-start | bytes 196616 | tf_op jit(solution)/shard_map/ppermute | solution.py:23
  20.3 19.8 %collective-permute-start.4 = (bf16[64,1,1024]{0,2,1:T(8,128)(2,1)}, bf16[64,1,1024]{0,2,1:T(8,128)(2,1)}, u32[]{:S(2)}, u32[]{:S(2)}) collective-permute-start(bf16[64,1,1024]{0,2,1:T(8,128)(2,1)} %get-tuple-element.12), channel_id=1, source_target_pairs={{0,1},{1,2},{2,3},{3,4},{4,5},{5,6},{6,7},{7,8},{8,9},{9,10},{10,1... | collective-permute-start | bytes 393224 | tf_op jit(solution)/shard_map/ppermute | solution.py:21
  30.0 10.1 %collective-permute-start.5 = (bf16[64,1,1024]{0,2,1:T(8,128)(2,1)}, bf16[64,1,1024]{0,2,1:T(8,128)(2,1)S(1)}, u32[]{:S(2)}, u32[]{:S(2)}) collective-permute-start(bf16[64,1,1024]{0,2,1:T(8,128)(2,1)} %get-tuple-element.13), channel_id=1, source_target_pairs={{1,0},{2,1},{3,2},{4,3},{5,4},{6,5},{7,6},{8,7},{9,8},{10,9},{11,1... | collective-permute-start | bytes 393224 | tf_op jit(solution)/shard_map/ppermute | solution.py:23
  60.0 24.1 %copy-start.6 = (bf16[1,256,1,16,16]{1,0,4,3,2:T(2,128)(2,1)S(1)}, bf16[1,256,1,16,16]{1,0,4,3,2:T(2,128)(2,1)}, u32[]{:S(2)}) copy-start(bf16[1,256,1,16,16]{1,0,4,3,2:T(2,128)(2,1)} %copy.22) | copy-start | bytes 393220
  84.1 5.9 %slice-start = ((s8[7340032]{0:T(1024)(128)(4,1)}), s8[4194304]{0:T(1024)(128)(4,1)S(1)}, s32[]{:S(2)}) async-start(s8[7340032]{0:T(1024)(128)(4,1)} %bitcast.278), calls=%async_computation | async-start | bytes 8388608
  84.1 5.8 %slice-start.1 = ((s8[7340032]{0:T(1024)(128)(4,1)}), s8[3145728]{0:T(1024)(128)(4,1)S(1)}, s32[]{:S(2)}) async-start(s8[7340032]{0:T(1024)(128)(4,1)} %bitcast.278), calls=%async_computation.1 | async-start | bytes 6291456
  90.0 2.1 %copy-start = (f32[3456,128]{1,0:T(8,128)S(1)}, f32[3456,128]{1,0:T(8,128)}, u32[]{:S(2)}) copy-start(f32[3456,128]{1,0:T(8,128)} %get-tuple-element.11) | copy-start | bytes 5308420
  157.3 1.0 copy-start.2
  158.5 7.2 %collective-permute-start.2 = (bf16[128,1,1024]{0,2,1:T(8,128)(2,1)S(1)}, bf16[128,1,1024]{0,2,1:T(8,128)(2,1)S(1)}, u32[]{:S(2)}, u32[]{:S(2)}) collective-permute-start(bf16[128,1,1024]{0,2,1:T(8,128)(2,1)S(1)} %get-tuple-element.16), channel_id=1, source_target_pairs={{0,1},{1,2},{2,3},{3,4},{4,5},{5,6},{6,7},{7,8},{8,9},{9,10},{10,1... | collective-permute-start | bytes 786440 | tf_op jit(solution)/shard_map/ppermute | solution.py:21
  160.3 9.3 %collective-permute-start.3 = (bf16[128,1,1024]{0,2,1:T(8,128)(2,1)S(1)}, bf16[128,1,1024]{0,2,1:T(8,128)(2,1)S(1)}, u32[]{:S(2)}, u32[]{:S(2)}) collective-permute-start(bf16[128,1,1024]{0,2,1:T(8,128)(2,1)S(1)} %get-tuple-element.17), channel_id=1, source_target_pairs={{1,0},{2,1},{3,2},{4,3},{5,4},{6,5},{7,6},{8,7},{9,8},{10,9},{11,1... | collective-permute-start | bytes 786440 | tf_op jit(solution)/shard_map/ppermute | solution.py:23
  170.4 1.0 copy-start.5
  170.4 1.0 copy-start.7
  176.3 5.4 %copy-start.3 = (f32[3456,256]{1,0:T(8,128)S(1)}, f32[3456,256]{1,0:T(8,128)}, u32[]{:S(2)}) copy-start(f32[3456,256]{1,0:T(8,128)} %get-tuple-element.6) | copy-start | bytes 10616836

commit v3 on v0

--- a/solution.py
+++ b/solution.py
@@ -74,7 +74,7 @@
     pl.semaphore_wait(barrier, len(peers))
 
     def rows_at(start, size):
-        return pl.ds(pl.multiple_of(start, 8), size)
+        return pl.ds(pl.multiple_of(start, 16), size)
 
     used = [0]
 
@@ -124,16 +124,16 @@
             total = total + recv_3[p, (last - j + 4) % 4]
         outer = core * half + p * part + spot[order[0]] * quarter
         own = outer + spot[order[1]] * piece
-        full[rows_at(own, piece), :] = total
+        full[rows_at(own, piece), :] = total.astype(full.dtype)
         spans.append((outer, own, order))
     exchange([(full.at[rows_at(own, piece)], full.at[rows_at(own, piece)], peer(order[1], k)) for outer, own, order in spans for k in (1, 2, 3)])
     exchange([(full.at[rows_at(outer, quarter)], full.at[rows_at(outer, quarter)], peer(order[0], k)) for outer, own, order in spans for k in (1, 2, 3)])
     block = full.at[rows_at(core * half, half)]
     exchange([(block, block, partner)])
     rows_a, rows_b = o_a.shape[0], o_b.shape[0]
-    o_a[...] = full[0:rows_a, :]
-    o_b[:, 0:128] = full[rows_a : rows_a + rows_b, :]
-    o_b[:, 128:256] = full[rows_a + rows_b : rows_a + 2 * rows_b, :]
+    o_a[...] = full[0:rows_a, :].astype(jnp.float32)
+    o_b[:, 0:128] = full[rows_a : rows_a + rows_b, :].astype(jnp.float32)
+    o_b[:, 128:256] = full[rows_a + rows_b : rows_a + 2 * rows_b, :].astype(jnp.float32)
 
 
 def all_reduce(sums_a, sums_b, scale_a, scale_b):
@@ -142,7 +142,7 @@
     wide = sums_b.reshape(rows_b, 256) * scale_b
     flat = jnp.concatenate([sums_a.reshape(rows_a, 128) * scale_a, wide[:, :128], wide[:, 128:]])
     count = flat.shape[0]
-    unit = 6 * 16 * 8
+    unit = 6 * 16 * 16
     rows = -(-count // unit) * unit
     flat = jnp.pad(flat, ((0, rows - count), (0, 0)))
     half = rows // 2
@@ -155,7 +155,7 @@
         in_specs=[pl.BlockSpec(memory_space=pltpu.VMEM)],
         out_specs=(pl.BlockSpec(memory_space=pltpu.VMEM), pl.BlockSpec(memory_space=pltpu.VMEM)),
         scratch_shapes=[
-            pltpu.VMEM((rows, 128), f32),
+            pltpu.VMEM((rows, 128), jnp.bfloat16),
             pltpu.VMEM((half, 128), f32),
             pltpu.VMEM((half, 128), f32),
             pltpu.VMEM((3, 3, quarter, 128), f32),

time: 151 us -> 145 us (0.960)
  Pallas kernels: 61 us -> 55.3 us
    pallas_call x1, Pallas kernels: 61 us -> 55.3 us  [all_reduce(): pl.pallas_call(_all_reduce_kernel, out_shape=(jax.ShapeDtypeStruct((rows_...]
  transfers between devices with their start and end apart: 8 -> 8, of which waited for: 0 -> 0; matrix products, arithmetic and copies ran while one was open for 28% -> 29% of each run, Pallas kernels for 41% -> 38%
where the time goes in v3:
time: 145 us
  Pallas kernels  55.3 us (38%)
  local copies, waits for them, and re-layouts  28.8 us (20%)
  matrix products  25.9 us (18%)
  starting transfers between devices  24.7 us (17%)
  other arithmetic  9.05 us (6%)
    pallas_call x1, Pallas kernels, all_reduce(): pl.pallas_call(_all_reduce_kernel, out_shape=(jax.ShapeDtypeStruct((rows_...  55.3 us
    conv_general_dilated x4, matrix products, conv_cells(): lax.conv_general_dilated(field[None], shaped, (1, 1, 1), ((0, 0), (1, 1),...  25.9 us
    ppermute x4, starting transfers between devices, padded_2(): lax.ppermute(tail, axis, [(i, (i + 1) % count) for i in range(ends)])  19.3 us
    unnamed x28, local copies, waits for them, and re-layouts  10.6 us
    concatenate x8, local copies, waits for them, and re-layouts, padded_2(): jnp.concatenate([lax.ppermute(tail, axis, [(i, (i + 1) % count) for i in...  6.82 us
    concatenate x1, other arithmetic, all_reduce(): jnp.concatenate([sums_a.reshape(rows_a, 128) * scale_a, wide[:, :128], wi...  5.63 us
    ppermute x4, starting transfers between devices, padded_2(): lax.ppermute(head, axis, [((i + 1) % count, i) for i in range(ends)])  5.45 us
    rev x2, local copies, waits for them, and re-layouts, back_cells(): flipped = kernel[::-1].transpose(0, 2, 1)  3.67 us
  transfers between devices with their start and end apart: 8, of which 0 were waited for; matrix products, arithmetic and copies ran while one was open for 29% of the time, Pallas kernels for 38%

profile of v3, /device:TPU:1, one launch (start us, length us, event | category | flops | bytes accessed | tf_op | source)
XLA Modules:
  0.0 144.8 jit_solution(5736898519074801626)
XLA Ops:
  0.6 1.0 copy.21
  1.6 1.0 copy.20
  2.6 0.1 multiply_convert_fusion.1
  2.7 0.0 copy-start.6
  2.7 1.4 collective-permute-start.1
  4.2 5.6 %collective-permute-start = (bf16[256,1,256]{0,2,1:T(8,128)(2,1)S(1)}, bf16[256,1,256]{0,2,1:T(8,128)(2,1)}, u32[]{:S(2)}, u32[]{:S(2)}) collective-permute-start(bf16[256,1,256]{0,2,1:T(8,128)(2,1)S(1)} %bitcast.67), channel_id=1, source_target_pairs={{0,1},{1,2},{2,3},{3,4},{4,5},{5,6},{6,7},{7,8},{8,9},{9,10},{10,1... | collective-permute-start | bytes 393224 | tf_op jit(solution)/shard_map/ppermute | solution.py:21
  9.8 1.4 copy.25
  11.2 0.2 fusion.16
  11.4 0.0 copy-start.4
  11.4 0.4 reduce_sum.18
  11.8 0.6 multiply_convert_fusion.2
  12.4 1.3 collective-permute-start.7
  13.7 4.6 %collective-permute-start.6 = (bf16[128,1,256]{0,2,1:T(8,128)(2,1)}, bf16[128,1,256]{0,2,1:T(8,128)(2,1)}, u32[]{:S(2)}, u32[]{:S(2)}) collective-permute-start(bf16[128,1,256]{0,2,1:T(8,128)(2,1)} %bitcast.28), channel_id=1, source_target_pairs={{0,1},{1,2},{2,3},{3,4},{4,5},{5,6},{6,7},{7,8},{8,9},{9,10},{10,1... | collective-permute-start | bytes 196616 | tf_op jit(solution)/shard_map/ppermute | solution.py:21
  18.3 0.0 copy-done.6
  18.3 0.3 copy.31
  18.6 0.8 fusion.36
  19.5 2.3 %collective-permute-start.4 = (bf16[64,1,1024]{0,2,1:T(8,128)(2,1)}, bf16[64,1,1024]{0,2,1:T(8,128)(2,1)S(1)}, u32[]{:S(2)}, u32[]{:S(2)}) collective-permute-start(bf16[64,1,1024]{0,2,1:T(8,128)(2,1)} %get-tuple-element.12), channel_id=1, source_target_pairs={{0,1},{1,2},{2,3},{3,4},{4,5},{5,6},{6,7},{7,8},{8,9},{9,10},{10,1... | collective-permute-start | bytes 393224 | tf_op jit(solution)/shard_map/ppermute | solution.py:21
  21.8 0.6 fusion.40
  22.4 0.9 copy.23
  23.4 0.8 rev.7
  24.2 1.1 copy.34
  25.3 1.0 copy.38
  26.3 2.9 %rev.6 = bf16[27,128,256]{2,1,0:T(8,128)(2,1)} reverse(bf16[27,128,256]{2,1,0:T(8,128)(2,1)} %param.11), dimensions={0} | reverse | bytes 3538944 | tf_op jit(solution)/shard_map/rev | solution.py:188
  29.2 0.0 collective-permute-done.7
  29.2 1.3 collective-permute-start.5
  30.5 0.9 copy.39
  31.4 0.0 collective-permute-done.6
  31.4 0.9 copy.37
  32.4 2.4 %convolution_multiply_fusion = f32[3,3,3,128,256]{4,3,2,1,0:T(8,128)S(1)} fusion(bf16[1,128,1,16,16]{1,0,4,3,2:T(2,128)(2,1)S(1)} %copy.39, bf16[1,128,1,16,16]{1,0,4,3,2:T(2,128)(2,1)S(1)} %copy.38, bf16[1,128,1,16,16]{1,0,4,3,2:T(2,128)(2,1)S(1)} %copy.37, bf16[1,256,1,16,16]{1,4,3,2,0:T(8,128)(2,1)S(1)} %bitcast.69), kind=kOutput, calls=%fused_computation.7 | convolution fusion | flops 417497088 | bytes 3866624 | tf_op jit(solution)/shard_map/transpose(jvp())/conv_general_dilated | solution.py:176
  34.8 2.0 %fusion.35 = (f32[3456,128]{1,0:T(8,128)}, f32[3456,128]{1,0:T(8,128)}) fusion(f32[3456,256]{1,0:T(8,128)S(1)} %bitcast.58), kind=kLoop, calls=%fused_computation.47 | loop fusion | bytes 7077888 | tf_op jit(solution)/shard_map/slice | solution.py:143
  36.7 0.0 collective-permute-done.1
  36.7 1.3 copy.24
  38.1 0.0 collective-permute-done
  38.1 1.2 copy.22
  39.2 0.0 collective-permute-done.4
  39.2 0.6 copy.33
  39.8 0.0 collective-permute-done.5
  39.8 0.6 copy.35
  40.4 3.4 %convolution_multiply_fusion.1 = f32[1,128,1,16,16]{1,0,4,3,2:T(1,128)S(1)} fusion(bf16[3,3,3,256,128]{3,4,2,1,0:T(8,128)(2,1)S(1)} %bitcast.62, bf16[1,256,1,16,16]{1,0,4,3,2:T(2,128)(2,1)S(1)} %copy.24, bf16[1,256,1,16,16]{1,0,4,3,2:T(2,128)(2,1)S(1)} %copy-done.7, bf16[1,256,1,16,16]{1,0,4,3,2:T(2,128)(2,1)S(1)} %copy.22), kind=kOutput, calls=%fused_computation.19 | convolution fusion | flops 417234944 | bytes 2293760 | tf_op jit(solution)/shard_map/conv_general_dilated | solution.py:176
  43.9 0.3 broadcast_in_dim.23
  44.2 0.2 fusion.17
  44.4 0.8 fusion.37
  45.2 6.7 %collective-permute-start.2 = (bf16[128,1,1024]{0,2,1:T(8,128)(2,1)}, bf16[128,1,1024]{0,2,1:T(8,128)(2,1)}, u32[]{:S(2)}, u32[]{:S(2)}) collective-permute-start(bf16[128,1,1024]{0,2,1:T(8,128)(2,1)} %get-tuple-element.16), channel_id=1, source_target_pairs={{0,1},{1,2},{2,3},{3,4},{4,5},{5,6},{6,7},{7,8},{8,9},{9,10},{10,1... | collective-permute-start | bytes 786440 | tf_op jit(solution)/shard_map/ppermute | solution.py:21
  51.9 1.5 %collective-permute-start.3 = (bf16[128,1,1024]{0,2,1:T(8,128)(2,1)}, bf16[128,1,1024]{0,2,1:T(8,128)(2,1)}, u32[]{:S(2)}, u32[]{:S(2)}) collective-permute-start(bf16[128,1,1024]{0,2,1:T(8,128)(2,1)} %get-tuple-element.17), channel_id=1, source_target_pairs={{1,0},{2,1},{3,2},{4,3},{5,4},{6,5},{7,6},{8,7},{9,8},{10,9},{11,1... | collective-permute-start | bytes 786440 | tf_op jit(solution)/shard_map/ppermute | solution.py:23
  53.3 0.2 multiply_convert_fusion
  53.5 15.4 %fusion.15 = f32[3,3,3,64,128]{4,3,2,1,0:T(8,128)S(1)} fusion(bf16[1,64,1,32,32]{1,0,4,3,2:T(2,128)(2,1)S(1)} %copy.35, bf16[1,64,2,32,32]{1,0,4,3,2:T(2,128)(2,1)S(1)} %copy.34, bf16[1,64,1,32,32]{1,0,4,3,2:T(2,128)(2,1)S(1)} %copy.33, bf16[1,128,2,32,32]{1,4,3,2,0:T(8,128)(2,1)S(1)} %multiply_convert_fusion), kind=kOutput, calls=%fused_computation.17 | convolution fusion | flops 870408192 | bytes 1933312 | tf_op jit(solution)/shard_map/transpose(jvp())/conv_general_dilated | solution.py:176
  69.0 5.6 %select_maximum_fusion.x_ref = f32[9216,128]{1,0:T(8,128)} fusion(f32[3456,128]{1,0:T(8,128)S(1)} %copy-done.1, f32[3456,128]{1,0:T(8,128)S(1)} %copy-done, f32[1728,128]{1,0:T(8,128)S(1)} %bitcast.64), kind=kLoop, calls=%fused_computation | loop fusion | flops 7077888 | bytes 9142272 | tf_op jit(solution)/shard_map/concatenate | solution.py:143
  74.6 55.3 %shard_map.85 = (f32[1728,128]{1,0:T(8,128)}, f32[3456,256]{1,0:T(8,128)}) custom-call(f32[9216,128]{1,0:T(8,128)} %select_maximum_fusion.x_ref), custom_call_target="tpu_custom_call" | custom-call | tf_op jit(solution)/shard_map/pallas_call | solution.py:152
  129.9 0.0 collective-permute-done.2
  129.9 0.0 collective-permute-done.3
  129.9 1.2 maximum_bitcast_fusion
  131.0 0.4 copy.42
  131.5 0.2 pad.5.clone
  131.7 0.0 copy-start.5
  131.7 0.0 copy-start.9
  131.7 0.5 copy.28
  132.2 0.1 slice.28
  132.4 0.3 copy-done.5
  132.7 4.7 %fusion.12 = bf16[2,32,8,5,64]{4,2,3,1,0:T(8,128)(2,1)S(1)} fusion(bf16[3,3,3,128,64]{3,4,2,1,0:T(8,128)(2,1)S(1)} %bitcast.70, bf16[128,4,32,1,7,2]{0,4,5,2,1,3:T(8,128)(2,1)S(1)} %slice.28, bf16[128,4,32,1,8,5]{0,4,5,2,1,3:T(8,128)(2,1)S(1)} %copy.28, pred[8,5]{0,1:T(8,128)(4,1)S(1)} %copy-done.9), kind=kOutput, calls=%fused_computation.16 | convolution fusion | flops 1114701824 | bytes 2539560 | tf_op jit(solution)/shard_map/conv_general_dilated | solution.py:176
  137.5 0.1 copy.29
  137.6 1.0 copy.30
  138.6 2.2 %copy.41 = bf16[1,64,2,1024]{3,2,1,0:T(2,128)(2,1)} copy(bf16[1,64,2,1024]{1,3,2,0:T(8,128)(2,1)} %bitcast.60) | data formatting | bytes 524288
  140.8 2.2 %copy.49 = f32[27,64,128]{2,1,0:T(8,128)} copy(f32[27,64,128]{2,1,0:T(8,128)} %bitcast.65) | data formatting | bytes 1769472
  143.0 1.8 %copy.50 = f32[27,128,256]{2,1,0:T(8,128)} copy(f32[27,128,256]{2,1,0:T(8,128)S(1)} %bitcast.57) | data formatting | bytes 7077888
  (16 shorter events, 0.1 us)
Async XLA Ops:
  2.7 15.6 %copy-start.6 = (bf16[1,64,2,1024]{3,2,1,0:T(2,128)(2,1)S(1)}, bf16[1,64,2,1024]{3,2,1,0:T(2,128)(2,1)}, u32[]{:S(2)}) copy-start(bf16[1,64,2,1024]{3,2,1,0:T(2,128)(2,1)} %param.6) | copy-start | bytes 786436
  2.7 34.0 %collective-permute-start.1 = (bf16[256,1,256]{0,2,1:T(8,128)(2,1)S(1)}, bf16[256,1,256]{0,2,1:T(8,128)(2,1)}, u32[]{:S(2)}, u32[]{:S(2)}) collective-permute-start(bf16[256,1,256]{0,2,1:T(8,128)(2,1)S(1)} %bitcast.66), channel_id=1, source_target_pairs={{1,0},{2,1},{3,2},{4,3},{5,4},{6,5},{7,6},{8,7},{9,8},{10,9},{11,1... | collective-permute-start | bytes 393224 | tf_op jit(solution)/shard_map/ppermute | solution.py:23
  4.2 33.9 %collective-permute-start = (bf16[256,1,256]{0,2,1:T(8,128)(2,1)S(1)}, bf16[256,1,256]{0,2,1:T(8,128)(2,1)}, u32[]{:S(2)}, u32[]{:S(2)}) collective-permute-start(bf16[256,1,256]{0,2,1:T(8,128)(2,1)S(1)} %bitcast.67), channel_id=1, source_target_pairs={{0,1},{1,2},{2,3},{3,4},{4,5},{5,6},{6,7},{7,8},{8,9},{9,10},{10,1... | collective-permute-start | bytes 393224 | tf_op jit(solution)/shard_map/ppermute | solution.py:21
  11.4 12.0 %copy-start.4 = (bf16[27,64,128]{2,1,0:T(8,128)(2,1)S(1)}, bf16[27,64,128]{2,1,0:T(8,128)(2,1)}, u32[]{:S(2)}) copy-start(bf16[27,64,128]{2,1,0:T(8,128)(2,1)} %param.10) | copy-start | bytes 1327108
  12.4 16.8 %collective-permute-start.7 = (bf16[128,1,256]{0,2,1:T(8,128)(2,1)}, bf16[128,1,256]{0,2,1:T(8,128)(2,1)}, u32[]{:S(2)}, u32[]{:S(2)}) collective-permute-start(bf16[128,1,256]{0,2,1:T(8,128)(2,1)} %bitcast.28), channel_id=1, source_target_pairs={{1,0},{2,1},{3,2},{4,3},{5,4},{6,5},{7,6},{8,7},{9,8},{10,9},{11,1... | collective-permute-start | bytes 196616 | tf_op jit(solution)/shard_map/ppermute | solution.py:23
  13.7 17.7 %collective-permute-start.6 = (bf16[128,1,256]{0,2,1:T(8,128)(2,1)}, bf16[128,1,256]{0,2,1:T(8,128)(2,1)}, u32[]{:S(2)}, u32[]{:S(2)}) collective-permute-start(bf16[128,1,256]{0,2,1:T(8,128)(2,1)} %bitcast.28), channel_id=1, source_target_pairs={{0,1},{1,2},{2,3},{3,4},{4,5},{5,6},{6,7},{7,8},{8,9},{9,10},{10,1... | collective-permute-start | bytes 196616 | tf_op jit(solution)/shard_map/ppermute | solution.py:21
  19.5 19.8 %collective-permute-start.4 = (bf16[64,1,1024]{0,2,1:T(8,128)(2,1)}, bf16[64,1,1024]{0,2,1:T(8,128)(2,1)S(1)}, u32[]{:S(2)}, u32[]{:S(2)}) collective-permute-start(bf16[64,1,1024]{0,2,1:T(8,128)(2,1)} %get-tuple-element.12), channel_id=1, source_target_pairs={{0,1},{1,2},{2,3},{3,4},{4,5},{5,6},{6,7},{7,8},{8,9},{9,10},{10,1... | collective-permute-start | bytes 393224 | tf_op jit(solution)/shard_map/ppermute | solution.py:21
  25.3 3.9 %copy-start.8 = (bf16[64,1,1024]{0,2,1:T(8,128)(2,1)S(1)}, bf16[64,1,1024]{0,2,1:T(8,128)(2,1)}, u32[]{:S(2)}) copy-start(bf16[64,1,1024]{0,2,1:T(8,128)(2,1)} %get-tuple-element.13) | copy-start | bytes 393220
  29.2 10.6 %collective-permute-start.5 = (bf16[64,1,1024]{0,2,1:T(8,128)(2,1)S(1)}, bf16[64,1,1024]{0,2,1:T(8,128)(2,1)S(1)}, u32[]{:S(2)}, u32[]{:S(2)}) collective-permute-start(bf16[64,1,1024]{0,2,1:T(8,128)(2,1)S(1)} %copy-done.8), channel_id=1, source_target_pairs={{1,0},{2,1},{3,2},{4,3},{5,4},{6,5},{7,6},{8,7},{9,8},{10,9},{11,1... | collective-permute-start | bytes 393224 | tf_op jit(solution)/shard_map/ppermute | solution.py:23
  36.7 3.7 %copy-start.3 = (bf16[27,128,256]{2,1,0:T(8,128)(2,1)S(1)}, bf16[27,128,256]{2,1,0:T(8,128)(2,1)}, u32[]{:S(2)}) copy-start(bf16[27,128,256]{2,1,0:T(8,128)(2,1)} %rev.6) | copy-start | bytes 5308420
  36.7 3.7 %copy-start.7 = (bf16[1,256,1,16,16]{1,0,4,3,2:T(2,128)(2,1)S(1)}, bf16[1,256,1,16,16]{1,0,4,3,2:T(2,128)(2,1)}, u32[]{:S(2)}) copy-start(bf16[1,256,1,16,16]{1,0,4,3,2:T(2,128)(2,1)} %copy.23) | copy-start | bytes 393220
  45.2 84.7 %collective-permute-start.2 = (bf16[128,1,1024]{0,2,1:T(8,128)(2,1)}, bf16[128,1,1024]{0,2,1:T(8,128)(2,1)}, u32[]{:S(2)}, u32[]{:S(2)}) collective-permute-start(bf16[128,1,1024]{0,2,1:T(8,128)(2,1)} %get-tuple-element.16), channel_id=1, source_target_pairs={{0,1},{1,2},{2,3},{3,4},{4,5},{5,6},{6,7},{7,8},{8,9},{9,10},{10,1... | collective-permute-start | bytes 786440 | tf_op jit(solution)/shard_map/ppermute | solution.py:21
  51.9 78.0 %collective-permute-start.3 = (bf16[128,1,1024]{0,2,1:T(8,128)(2,1)}, bf16[128,1,1024]{0,2,1:T(8,128)(2,1)}, u32[]{:S(2)}, u32[]{:S(2)}) collective-permute-start(bf16[128,1,1024]{0,2,1:T(8,128)(2,1)} %get-tuple-element.17), channel_id=1, source_target_pairs={{1,0},{2,1},{3,2},{4,3},{5,4},{6,5},{7,6},{8,7},{9,8},{10,9},{11,1... | collective-permute-start | bytes 786440 | tf_op jit(solution)/shard_map/ppermute | solution.py:23
  53.5 15.4 %copy-start = (f32[3456,128]{1,0:T(8,128)S(1)}, f32[3456,128]{1,0:T(8,128)}, u32[]{:S(2)}) copy-start(f32[3456,128]{1,0:T(8,128)} %get-tuple-element.10) | copy-start | bytes 5308420
  53.5 15.4 %copy-start.1 = (f32[3456,128]{1,0:T(8,128)S(1)}, f32[3456,128]{1,0:T(8,128)}, u32[]{:S(2)}) copy-start(f32[3456,128]{1,0:T(8,128)} %get-tuple-element.11) | copy-start | bytes 5308420
  131.7 1.0 copy-start.5
  131.7 1.0 copy-start.9
  137.6 5.4 %copy-start.2 = (f32[3456,256]{1,0:T(8,128)S(1)}, f32[3456,256]{1,0:T(8,128)}, u32[]{:S(2)}) copy-start(f32[3456,256]{1,0:T(8,128)} %get-tuple-element.6) | copy-start | bytes 10616836

commit v4 on v3

--- a/solution.py
+++ b/solution.py
@@ -197,6 +197,40 @@
     return pull(upstream.astype(jnp.float32))[0]
 
 
+def _kernel_terms_body(src_ref, up_ref, out_ref):
+    cells = up_ref.shape[1]
+    width = src_ref.shape[1]
+    margin = 128
+    plane = 1024
+    side = 32
+    spot = lax.broadcasted_iota(jnp.int32, (1, cells), 1)
+    column = spot % side
+    row = (spot // side) % side
+    upstream = up_ref[...]
+    for b in range(3):
+        for c in range(3):
+            shift = (b - 1) * side + (c - 1)
+            moved = pltpu.roll(src_ref[...], (width - shift) % width, 1)
+            inside = (column + c - 1 >= 0) & (column + c - 1 < side) & (row + b - 1 >= 0) & (row + b - 1 < side)
+            for a in range(3):
+                window = moved[:, margin + a * plane : margin + a * plane + cells]
+                window = jnp.where(inside, window, 0.0).astype(jnp.bfloat16)
+                out_ref[9 * a + 3 * b + c] = lax.dot_general(
+                    window, upstream, (((1,), (1,)), ((), ())), preferred_element_type=jnp.float32
+                )
+
+
+def kernel_terms_flat(padded, upstream):
+    chan_in, chan_out = padded.shape[0], upstream.shape[0]
+    field = jnp.pad(padded.reshape(chan_in, -1).astype(jnp.float32), ((0, 0), (128, 128)))
+    return pl.pallas_call(
+        _kernel_terms_body,
+        out_shape=jax.ShapeDtypeStruct((27, chan_in, chan_out), jnp.float32),
+        in_specs=[pl.BlockSpec(memory_space=pltpu.VMEM)] * 2,
+        out_specs=pl.BlockSpec(memory_space=pltpu.VMEM),
+    )(field, upstream.reshape(chan_out, -1))
+
+
 def per_device(layer_input, hidden_pre, output_pre, output_grad, weight_a, weight_b):
     side = math.isqrt(layer_input.shape[3])
     half = side // 2
@@ -233,7 +267,7 @@
     hidden_pad = padded_2(grad_hidden, (("space", 1),), 1).reshape(width_a, depth_a + 2, side, side)
     source_pad = padded_2(source, (("space", 1),), 1).reshape(chan_in, depth_a + 2, side, side)
     back_a = back_cells(hidden_pad, weight_a)
-    sums_a = kernel_terms(source_pad, grad_hidden.reshape(width_a, depth_a, side, side))
+    sums_a = kernel_terms_flat(source_pad, grad_hidden)
     input_grad = back_a.astype(jnp.bfloat16).reshape(1, chan_in, depth_a, side * side)
     samples = lax.axis_size("dp")
     planes_a = depth_a * lax.axis_size("space")

time: 145 us -> 147 us (1.014)
  matrix products: 25.9 us -> 11.5 us
  Pallas kernels: 55.3 us -> 62.6 us
  other arithmetic: 9.05 us -> 15.3 us
  local copies, waits for them, and re-layouts: 28.8 us -> 31.5 us
    conv_general_dilated x4 -> x3, matrix products: 25.9 us -> 11.5 us  [conv_cells(): lax.conv_general_dilated(field[None], shaped, (1, 1, 1), ((0, 0), (1, 1),...]
    pallas_call x0 -> x1, Pallas kernels: none -> 7.29 us  [kernel_terms_flat(): pl.pallas_call(_kernel_terms_body, out_shape=jax.ShapeDtypeStruct((27, ch...]
    mul x0 -> x3, local copies, waits for them, and re-layouts: none -> 3.67 us  [per_device(): jnp.repeat(jnp.repeat(jnp.repeat(back_b, 2, 1), 2, 2), 2, 3) * 0.125]
    convert_element_type x2 -> x3, other arithmetic: 0.34 us -> 2.79 us  [per_device(): (upward * slopes(hidden_f.reshape(width_a, depth_a * side * side))).astyp...]
    concatenate x8 -> x5, local copies, waits for them, and re-layouts: 6.82 us -> 4.41 us  [padded_2(): jnp.concatenate([lax.ppermute(tail, axis, [(i, (i + 1) % count) for i in...]
    concatenate x1 -> x2, other arithmetic: 1.15 us -> 3.12 us  [padded_2(): jnp.concatenate([lax.ppermute(tail, axis, [(i, (i + 1) % count) for i in...]
    broadcast_in_dim x1 -> x3, local copies, waits for them, and re-layouts: 0.28 us -> 1.81 us  [per_device(): jnp.repeat(jnp.repeat(jnp.repeat(back_b, 2, 1), 2, 2), 2, 3) * 0.125]
    unnamed x28 -> x29, local copies, waits for them, and re-layouts: 10.6 us -> 10.9 us
  transfers between devices with their start and end apart: 8 -> 8, of which waited for: 0 -> 0; matrix products, arithmetic and copies ran while one was open for 29% -> 22% of each run, Pallas kernels for 38% -> 43%
where the time goes in v4:
time: 147 us
  Pallas kernels  62.6 us (43%)
  local copies, waits for them, and re-layouts  31.5 us (21%)
  starting transfers between devices  24.7 us (17%)
  other arithmetic  15.3 us (10%)
  matrix products  11.5 us (8%)
    pallas_call x1, Pallas kernels, all_reduce(): pl.pallas_call(_all_reduce_kernel, out_shape=(jax.ShapeDtypeStruct((rows_...  55.3 us
    ppermute x4, starting transfers between devices, padded_2(): lax.ppermute(tail, axis, [(i, (i + 1) % count) for i in range(ends)])  19.3 us
    conv_general_dilated x3, matrix products, conv_cells(): lax.conv_general_dilated(field[None], shaped, (1, 1, 1), ((0, 0), (1, 1),...  11.5 us
    unnamed x29, local copies, waits for them, and re-layouts  10.9 us
    pallas_call x1, Pallas kernels, kernel_terms_flat(): pl.pallas_call(_kernel_terms_body, out_shape=jax.ShapeDtypeStruct((27, ch...  7.29 us
    concatenate x1, other arithmetic, all_reduce(): jnp.concatenate([sums_a.reshape(rows_a, 128) * scale_a, wide[:, :128], wi...  5.6 us
    ppermute x4, starting transfers between devices, padded_2(): lax.ppermute(head, axis, [((i + 1) % count, i) for i in range(ends)])  5.45 us
    concatenate x5, local copies, waits for them, and re-layouts, padded_2(): jnp.concatenate([lax.ppermute(tail, axis, [(i, (i + 1) % count) for i in...  4.41 us
  transfers between devices with their start and end apart: 8, of which 0 were waited for; matrix products, arithmetic and copies ran while one was open for 22% of the time, Pallas kernels for 43%

profile of v4, /device:TPU:1, one launch (start us, length us, event | category | flops | bytes accessed | tf_op | source)
XLA Modules:
  0.0 146.6 jit_solution(12773342289054912651)
XLA Ops:
  0.6 1.0 copy.16
  1.6 1.0 copy.15
  2.6 0.1 multiply_convert_fusion.2
  2.7 0.0 copy-start.1
  2.7 1.4 collective-permute-start.1
  4.2 5.7 %collective-permute-start = (bf16[256,1,256]{0,2,1:T(8,128)(2,1)S(1)}, bf16[256,1,256]{0,2,1:T(8,128)(2,1)}, u32[]{:S(2)}, u32[]{:S(2)}) collective-permute-start(bf16[256,1,256]{0,2,1:T(8,128)(2,1)S(1)} %bitcast.73), channel_id=1, source_target_pairs={{0,1},{1,2},{2,3},{3,4},{4,5},{5,6},{6,7},{7,8},{8,9},{9,10},{10,1... | collective-permute-start | bytes 393224 | tf_op jit(solution)/shard_map/ppermute | solution.py:21
  9.8 1.4 copy.22
  11.2 0.2 fusion.14
  11.4 0.4 reduce_sum.18
  11.8 0.6 multiply_convert_fusion.3
  12.4 1.3 collective-permute-start.7
  13.7 4.6 %collective-permute-start.6 = (bf16[128,1,256]{0,2,1:T(8,128)(2,1)}, bf16[128,1,256]{0,2,1:T(8,128)(2,1)}, u32[]{:S(2)}, u32[]{:S(2)}) collective-permute-start(bf16[128,1,256]{0,2,1:T(8,128)(2,1)} %bitcast.27), channel_id=1, source_target_pairs={{0,1},{1,2},{2,3},{3,4},{4,5},{5,6},{6,7},{7,8},{8,9},{9,10},{10,1... | collective-permute-start | bytes 196616 | tf_op jit(solution)/shard_map/ppermute | solution.py:21
  18.3 1.2 fusion.33
  19.5 3.0 %collective-permute-start.4 = (bf16[64,1,1024]{2,1,0:T(2,128)(2,1)}, bf16[64,1,1024]{2,1,0:T(2,128)(2,1)}, u32[]{:S(2)}, u32[]{:S(2)}) collective-permute-start(bf16[64,1,1024]{2,1,0:T(2,128)(2,1)} %get-tuple-element.16), channel_id=1, source_target_pairs={{0,1},{1,2},{2,3},{3,4},{4,5},{5,6},{6,7},{7,8},{8,9},{9,10},{10,1... | collective-permute-start | bytes 393224 | tf_op jit(solution)/shard_map/ppermute | solution.py:21
  22.5 0.0 copy-start.4
  22.5 0.9 copy.18
  23.5 1.8 %rev.7 = bf16[27,64,128]{2,1,0:T(8,128)(2,1)} reverse(bf16[27,64,128]{2,1,0:T(8,128)(2,1)} %param.10), dimensions={0} | reverse | bytes 884736 | tf_op jit(solution)/shard_map/rev | solution.py:188
  25.3 0.7 copy.33
  26.0 1.3 copy.37
  27.3 1.3 rev.6
  28.6 1.3 collective-permute-start.5
  29.9 0.9 copy.34
  30.9 0.9 copy.32
  31.8 3.3 %convolution_multiply_fusion = f32[3,3,3,128,256]{4,3,2,1,0:T(8,128)S(1)} fusion(bf16[1,128,1,16,16]{1,0,4,3,2:T(2,128)(2,1)S(1)} %copy.34, bf16[1,128,1,16,16]{1,0,4,3,2:T(2,128)(2,1)} %copy.33, bf16[1,128,1,16,16]{1,0,4,3,2:T(2,128)(2,1)S(1)} %copy.32, bf16[1,256,1,16,16]{1,4,3,2,0:T(8,128)(2,1)S(1)} %bitcast.75), kind=kOutput, calls=%fused_computation.5 | convolution fusion | flops 417497088 | bytes 3866624 | tf_op jit(solution)/shard_map/transpose(jvp())/conv_general_dilated | solution.py:176
  35.1 1.5 %fusion.31 = (f32[3456,128]{1,0:T(8,128)S(1)}, f32[3456,128]{1,0:T(8,128)}) fusion(f32[3456,256]{1,0:T(8,128)S(1)} %bitcast.58), kind=kLoop, calls=%fused_computation.46 | loop fusion | bytes 7077888 | tf_op jit(solution)/shard_map/slice | solution.py:143
  36.6 1.2 copy.19
  37.8 1.2 copy.17
  39.0 0.0 copy-start.5
  39.0 0.0 copy-start.8
  39.0 2.0 %pad_maximum_fusion.2 = bf16[64,4,1024]{2,1,0:T(4,128)(2,1)S(1)} fusion(bf16[64,1,1024]{2,1,0:T(2,128)(2,1)S(1)} %collective-permute-done.5, bf16[64,2,1024]{2,1,0:T(2,128)(2,1)S(1)} %bitcast.60, bf16[64,1,1024]{2,1,0:T(2,128)(2,1)} %collective-permute-done.4), kind=kLoop, calls=%fused_computation.30 | loop fusion | flops 1572864 | bytes 1048576 | tf_op jit(solution)/shard_map/concatenate | solution.py:19
  41.0 0.2 copy.40
  41.2 1.1 pad_convert_fusion.src_ref
  42.2 3.4 %convolution_multiply_fusion.1 = f32[1,128,1,16,16]{1,0,4,3,2:T(1,128)S(1)} fusion(bf16[3,3,3,256,128]{3,4,2,1,0:T(8,128)(2,1)S(1)} %bitcast.70, bf16[1,256,1,16,16]{1,0,4,3,2:T(2,128)(2,1)S(1)} %copy.19, bf16[1,256,1,16,16]{1,0,4,3,2:T(2,128)(2,1)S(1)} %copy-done.8, bf16[1,256,1,16,16]{1,0,4,3,2:T(2,128)(2,1)S(1)} %copy.17), kind=kOutput, calls=%fused_computation.16 | convolution fusion | flops 417234944 | bytes 2293760 | tf_op jit(solution)/shard_map/conv_general_dilated | solution.py:176
  45.7 0.1 broadcast_in_dim.22
  45.9 0.2 copy.38
  46.0 0.1 broadcast_in_dim.23
  46.1 1.1 copy.23
  47.2 0.3 broadcast_in_dim.23.clone
  47.5 0.2 fusion.15
  47.7 0.8 fusion.32
  48.5 6.0 %collective-permute-start.2 = (bf16[128,1,1024]{0,2,1:T(8,128)(2,1)}, bf16[128,1,1024]{0,2,1:T(8,128)(2,1)}, u32[]{:S(2)}, u32[]{:S(2)}) collective-permute-start(bf16[128,1,1024]{0,2,1:T(8,128)(2,1)} %get-tuple-element.14), channel_id=1, source_target_pairs={{0,1},{1,2},{2,3},{3,4},{4,5},{5,6},{6,7},{7,8},{8,9},{9,10},{10,1... | collective-permute-start | bytes 786440 | tf_op jit(solution)/shard_map/ppermute | solution.py:21
  54.5 1.5 collective-permute-start.3
  56.0 1.5 %broadcast_in_dim.27 = f32[128,2,32,16,2]{0,4,3,2,1:T(2,128)} broadcast(f32[128,32,16]{0,2,1:T(8,128)S(1)} %copy.38), dimensions={0,2,3} | broadcast | bytes 1310720 | tf_op jit(solution)/shard_map/broadcast_in_dim | solution.py:261
  57.5 2.5 %copy.31 = f32[128,2048]{1,0:T(8,128)} copy(f32[128,2048]{0,1:T(8,128)} %bitcast.55) | data formatting | bytes 2097152 | tf_op jit(solution)/shard_map/mul | solution.py:261
  60.0 2.5 %multiply_convert_fusion.up_ref = bf16[128,2048]{1,0:T(8,128)(2,1)} fusion(f32[128,2048]{1,0:T(8,128)} %copy.31, f32[128,2048]{1,0:T(8,128)} %copy.37), kind=kLoop, calls=%fused_computation.21 | loop fusion | flops 524288 | bytes 2621440 | tf_op jit(solution)/shard_map/convert_element_type | solution.py:263
  62.4 7.3 %shard_map.85 = f32[27,64,128]{2,1,0:T(8,128)} custom-call(f32[64,4352]{1,0:T(8,128)} %pad_convert_fusion.src_ref, bf16[128,2048]{1,0:T(8,128)(2,1)} %multiply_convert_fusion.up_ref), custom_call_target="tpu_custom_call" | custom-call | tf_op jit(solution)/shard_map/pallas_call | solution.py:226
  69.7 1.4 broadcast_multiply_fusion
  71.1 0.3 copy-done
  71.5 5.6 %select_maximum_fusion.x_ref = f32[9216,128]{1,0:T(8,128)} fusion(f32[3456,128]{1,0:T(8,128)S(1)} %copy-done, f32[3456,128]{1,0:T(8,128)S(1)} %get-tuple-element.10, f32[1728,128]{1,0:T(8,128)S(1)} %bitcast.56), kind=kLoop, calls=%fused_computation | loop fusion | flops 7077888 | bytes 9142272 | tf_op jit(solution)/shard_map/concatenate | solution.py:143
  77.1 55.3 %shard_map.86 = (f32[1728,128]{1,0:T(8,128)}, f32[3456,256]{1,0:T(8,128)}) custom-call(f32[9216,128]{1,0:T(8,128)} %select_maximum_fusion.x_ref), custom_call_target="tpu_custom_call" | custom-call | tf_op jit(solution)/shard_map/pallas_call | solution.py:152
  132.4 0.2 multiply_convert_fusion.1
  132.6 1.2 maximum_bitcast_fusion
  133.8 0.4 copy.39
  134.2 0.2 pad.13.clone
  134.4 0.0 copy-start.9
  134.5 0.5 copy.26
  135.0 0.1 slice.28
  135.1 0.3 copy-done.7
  135.5 4.7 %fusion.11 = bf16[2,32,8,5,64]{4,2,3,1,0:T(8,128)(2,1)S(1)} fusion(bf16[3,3,3,128,64]{3,4,2,1,0:T(8,128)(2,1)S(1)} %bitcast.76, bf16[128,4,32,1,7,2]{0,4,5,2,1,3:T(8,128)(2,1)S(1)} %slice.28, bf16[128,4,32,1,8,5]{0,4,5,2,1,3:T(8,128)(2,1)S(1)} %copy.26, pred[8,5]{0,1:T(8,128)(4,1)S(1)} %copy-done.9), kind=kOutput, calls=%fused_computation.14 | convolution fusion | flops 1114701824 | bytes 2539560 | tf_op jit(solution)/shard_map/conv_general_dilated | solution.py:176
  140.2 0.1 copy.27
  140.4 0.2 copy.28
  140.6 1.0 copy.36
  141.5 0.9 copy.45
  142.5 4.2 %copy.46 = f32[27,128,256]{2,1,0:T(8,128)} copy(f32[27,128,256]{2,1,0:T(8,128)} %bitcast.57) | data formatting | bytes 7077888
  (24 shorter events, 0.1 us)
Async XLA Ops:
  2.7 15.6 %copy-start.1 = (bf16[1,64,2,1024]{3,2,1,0:T(2,128)(2,1)S(1)}, bf16[1,64,2,1024]{3,2,1,0:T(2,128)(2,1)}, u32[]{:S(2)}) copy-start(bf16[1,64,2,1024]{3,2,1,0:T(2,128)(2,1)} %param.6) | copy-start | bytes 786436
  2.7 33.9 %collective-permute-start.1 = (bf16[256,1,256]{0,2,1:T(8,128)(2,1)S(1)}, bf16[256,1,256]{0,2,1:T(8,128)(2,1)}, u32[]{:S(2)}, u32[]{:S(2)}) collective-permute-start(bf16[256,1,256]{0,2,1:T(8,128)(2,1)S(1)} %bitcast.72), channel_id=1, source_target_pairs={{1,0},{2,1},{3,2},{4,3},{5,4},{6,5},{7,6},{8,7},{9,8},{10,9},{11,1... | collective-permute-start | bytes 393224 | tf_op jit(solution)/shard_map/ppermute | solution.py:23
  4.2 33.6 %collective-permute-start = (bf16[256,1,256]{0,2,1:T(8,128)(2,1)S(1)}, bf16[256,1,256]{0,2,1:T(8,128)(2,1)}, u32[]{:S(2)}, u32[]{:S(2)}) collective-permute-start(bf16[256,1,256]{0,2,1:T(8,128)(2,1)S(1)} %bitcast.73), channel_id=1, source_target_pairs={{0,1},{1,2},{2,3},{3,4},{4,5},{5,6},{6,7},{7,8},{8,9},{9,10},{10,1... | collective-permute-start | bytes 393224 | tf_op jit(solution)/shard_map/ppermute | solution.py:21
  12.4 16.2 %collective-permute-start.7 = (bf16[128,1,256]{0,2,1:T(8,128)(2,1)}, bf16[128,1,256]{0,2,1:T(8,128)(2,1)}, u32[]{:S(2)}, u32[]{:S(2)}) collective-permute-start(bf16[128,1,256]{0,2,1:T(8,128)(2,1)} %bitcast.27), channel_id=1, source_target_pairs={{1,0},{2,1},{3,2},{4,3},{5,4},{6,5},{7,6},{8,7},{9,8},{10,9},{11,1... | collective-permute-start | bytes 196616 | tf_op jit(solution)/shard_map/ppermute | solution.py:23
  13.7 17.2 %collective-permute-start.6 = (bf16[128,1,256]{0,2,1:T(8,128)(2,1)}, bf16[128,1,256]{0,2,1:T(8,128)(2,1)}, u32[]{:S(2)}, u32[]{:S(2)}) collective-permute-start(bf16[128,1,256]{0,2,1:T(8,128)(2,1)} %bitcast.27), channel_id=1, source_target_pairs={{0,1},{1,2},{2,3},{3,4},{4,5},{5,6},{6,7},{7,8},{8,9},{9,10},{10,1... | collective-permute-start | bytes 196616 | tf_op jit(solution)/shard_map/ppermute | solution.py:21
  19.5 19.5 %collective-permute-start.4 = (bf16[64,1,1024]{2,1,0:T(2,128)(2,1)}, bf16[64,1,1024]{2,1,0:T(2,128)(2,1)}, u32[]{:S(2)}, u32[]{:S(2)}) collective-permute-start(bf16[64,1,1024]{2,1,0:T(2,128)(2,1)} %get-tuple-element.16), channel_id=1, source_target_pairs={{0,1},{1,2},{2,3},{3,4},{4,5},{5,6},{6,7},{7,8},{8,9},{9,10},{10,1... | collective-permute-start | bytes 393224 | tf_op jit(solution)/shard_map/ppermute | solution.py:21
  22.5 4.8 %copy-start.4 = (bf16[27,128,256]{2,1,0:T(8,128)(2,1)S(1)}, bf16[27,128,256]{2,1,0:T(8,128)(2,1)}, u32[]{:S(2)}) copy-start(bf16[27,128,256]{2,1,0:T(8,128)(2,1)} %param.11) | copy-start | bytes 5308420
  28.6 10.3 %collective-permute-start.5 = (bf16[64,1,1024]{2,1,0:T(2,128)(2,1)}, bf16[64,1,1024]{2,1,0:T(2,128)(2,1)S(1)}, u32[]{:S(2)}, u32[]{:S(2)}) collective-permute-start(bf16[64,1,1024]{2,1,0:T(2,128)(2,1)} %get-tuple-element.17), channel_id=1, source_target_pairs={{1,0},{2,1},{3,2},{4,3},{5,4},{6,5},{7,6},{8,7},{9,8},{10,9},{11,1... | collective-permute-start | bytes 393224 | tf_op jit(solution)/shard_map/ppermute | solution.py:23
  35.1 3.9 %copy-start.2 = (bf16[1,64,2,1024]{3,2,1,0:T(2,128)(2,1)S(1)}, bf16[1,64,2,1024]{3,2,1,0:T(2,128)(2,1)}, u32[]{:S(2)}) copy-start(bf16[1,64,2,1024]{3,2,1,0:T(2,128)(2,1)} %param.6) | copy-start | bytes 786436
  39.0 3.3 %copy-start.5 = (bf16[27,128,256]{2,1,0:T(8,128)(2,1)S(1)}, bf16[27,128,256]{2,1,0:T(8,128)(2,1)}, u32[]{:S(2)}) copy-start(bf16[27,128,256]{2,1,0:T(8,128)(2,1)} %rev.6) | copy-start | bytes 5308420
  39.0 3.3 %copy-start.8 = (bf16[1,256,1,16,16]{1,0,4,3,2:T(2,128)(2,1)S(1)}, bf16[1,256,1,16,16]{1,0,4,3,2:T(2,128)(2,1)}, u32[]{:S(2)}) copy-start(bf16[1,256,1,16,16]{1,0,4,3,2:T(2,128)(2,1)} %copy.18) | copy-start | bytes 393220
  48.5 84.1 %collective-permute-start.2 = (bf16[128,1,1024]{0,2,1:T(8,128)(2,1)}, bf16[128,1,1024]{0,2,1:T(8,128)(2,1)}, u32[]{:S(2)}, u32[]{:S(2)}) collective-permute-start(bf16[128,1,1024]{0,2,1:T(8,128)(2,1)} %get-tuple-element.14), channel_id=1, source_target_pairs={{0,1},{1,2},{2,3},{3,4},{4,5},{5,6},{6,7},{7,8},{8,9},{9,10},{10,1... | collective-permute-start | bytes 786440 | tf_op jit(solution)/shard_map/ppermute | solution.py:21
  54.5 78.1 %collective-permute-start.3 = (bf16[128,1,1024]{0,2,1:T(8,128)(2,1)}, bf16[128,1,1024]{0,2,1:T(8,128)(2,1)}, u32[]{:S(2)}, u32[]{:S(2)}) collective-permute-start(bf16[128,1,1024]{0,2,1:T(8,128)(2,1)} %get-tuple-element.15), channel_id=1, source_target_pairs={{1,0},{2,1},{3,2},{4,3},{5,4},{6,5},{7,6},{8,7},{9,8},{10,9},{11,1... | collective-permute-start | bytes 786440 | tf_op jit(solution)/shard_map/ppermute | solution.py:23
  69.7 1.7 %copy-start = (f32[3456,128]{1,0:T(8,128)S(1)}, f32[3456,128]{1,0:T(8,128)}, u32[]{:S(2)}) copy-start(f32[3456,128]{1,0:T(8,128)} %get-tuple-element.11) | copy-start | bytes 5308420
  77.1 55.3 %copy-start.3 = (f32[128,32,32]{0,2,1:T(8,128)S(1)}, f32[128,32,32]{0,2,1:T(8,128)}, u32[]{:S(2)}) copy-start(f32[128,32,32]{0,2,1:T(8,128)} %copy.23) | copy-start | bytes 1572868
  134.4 1.0 copy-start.7
  134.4 1.0 copy-start.9
  140.2 1.3 copy-start.6

commit v5 on v4

--- a/solution.py
+++ b/solution.py
@@ -197,38 +197,50 @@
     return pull(upstream.astype(jnp.float32))[0]
 
 
-def _kernel_terms_body(src_ref, up_ref, out_ref):
+def _layer_a_body(src_ref, up_ref, pad_ref, w_ref, terms_ref, back_ref):
     cells = up_ref.shape[1]
     width = src_ref.shape[1]
-    margin = 128
-    plane = 1024
+    plane = width // 4
     side = 32
     spot = lax.broadcasted_iota(jnp.int32, (1, cells), 1)
     column = spot % side
     row = (spot // side) % side
     upstream = up_ref[...]
+    field = src_ref[...].astype(jnp.float32)
+    back = jnp.zeros((back_ref.shape[0], cells), jnp.float32)
     for b in range(3):
         for c in range(3):
             shift = (b - 1) * side + (c - 1)
-            moved = pltpu.roll(src_ref[...], (width - shift) % width, 1)
+            moved = pltpu.roll(field, (width - shift) % width, 1)
             inside = (column + c - 1 >= 0) & (column + c - 1 < side) & (row + b - 1 >= 0) & (row + b - 1 < side)
+            total = jnp.zeros_like(back)
             for a in range(3):
-                window = moved[:, margin + a * plane : margin + a * plane + cells]
+                tap = 9 * a + 3 * b + c
+                window = moved[:, a * plane : a * plane + cells]
                 window = jnp.where(inside, window, 0.0).astype(jnp.bfloat16)
-                out_ref[9 * a + 3 * b + c] = lax.dot_general(
+                terms_ref[tap] = lax.dot_general(
                     window, upstream, (((1,), (1,)), ((), ())), preferred_element_type=jnp.float32
                 )
-
-
-def kernel_terms_flat(padded, upstream):
-    chan_in, chan_out = padded.shape[0], upstream.shape[0]
-    field = jnp.pad(padded.reshape(chan_in, -1).astype(jnp.float32), ((0, 0), (128, 128)))
+                total = total + jnp.dot(
+                    w_ref[tap], pad_ref[:, (2 - a) * plane : (2 - a) * plane + cells], preferred_element_type=jnp.float32
+                )
+            back_in = (column - c + 1 >= 0) & (column - c + 1 < side) & (row - b + 1 >= 0) & (row - b + 1 < side)
+            back = back + jnp.where(back_in, pltpu.roll(total, shift % cells, 1), 0.0)
+    back_ref[...] = back.astype(back_ref.dtype)
+
+
+def layer_a_grads(source_pad, hidden_pad, grad_hidden, weight_a):
+    chan_in, chan_out = source_pad.shape[0], grad_hidden.shape[0]
+    cells = grad_hidden.shape[1] * grad_hidden.shape[2]
     return pl.pallas_call(
-        _kernel_terms_body,
-        out_shape=jax.ShapeDtypeStruct((27, chan_in, chan_out), jnp.float32),
-        in_specs=[pl.BlockSpec(memory_space=pltpu.VMEM)] * 2,
-        out_specs=pl.BlockSpec(memory_space=pltpu.VMEM),
-    )(field, upstream.reshape(chan_out, -1))
+        _layer_a_body,
+        out_shape=(
+            jax.ShapeDtypeStruct((27, chan_in, chan_out), jnp.float32),
+            jax.ShapeDtypeStruct((chan_in, cells), jnp.bfloat16),
+        ),
+        in_specs=[pl.BlockSpec(memory_space=pltpu.VMEM)] * 4,
+        out_specs=(pl.BlockSpec(memory_space=pltpu.VMEM), pl.BlockSpec(memory_space=pltpu.VMEM)),
+    )(source_pad.reshape(chan_in, -1), grad_hidden.reshape(chan_out, -1), hidden_pad.reshape(chan_out, -1), weight_a)
 
 
 def per_device(layer_input, hidden_pre, output_pre, output_grad, weight_a, weight_b):
@@ -264,10 +276,9 @@
         jnp.bfloat16
     )
     grad_hidden = grad_hidden.reshape(width_a, depth_a, side * side)
-    hidden_pad = padded_2(grad_hidden, (("space", 1),), 1).reshape(width_a, depth_a + 2, side, side)
-    source_pad = padded_2(source, (("space", 1),), 1).reshape(chan_in, depth_a + 2, side, side)
-    back_a = back_cells(hidden_pad, weight_a)
-    sums_a = kernel_terms_flat(source_pad, grad_hidden)
+    hidden_pad = padded_2(grad_hidden, (("space", 1),), 1)
+    source_pad = padded_2(source, (("space", 1),), 1)
+    sums_a, back_a = layer_a_grads(source_pad, hidden_pad, grad_hidden, weight_a)
     input_grad = back_a.astype(jnp.bfloat16).reshape(1, chan_in, depth_a, side * side)
     samples = lax.axis_size("dp")
     planes_a = depth_a * lax.axis_size("space")

time: 147 us -> 148 us (level)
  waiting for transfers between devices: 0.02 us -> 12.4 us
  local copies, waits for them, and re-layouts: 31.5 us -> 25.2 us
  matrix products: 11.5 us -> 5.77 us
    ppermute x4, waiting for transfers between devices: 0.01 us -> 7.94 us  [padded_2(): lax.ppermute(head, axis, [((i + 1) % count, i) for i in range(ends)])]
    conv_general_dilated x3 -> x2, matrix products: 11.5 us -> 5.77 us  [conv_cells(): lax.conv_general_dilated(field[None], shaped, (1, 1, 1), ((0, 0), (1, 1),...]
    ppermute x4, waiting for transfers between devices: 0.01 us -> 4.47 us  [padded_2(): lax.ppermute(tail, axis, [(i, (i + 1) % count) for i in range(ends)])]
    concatenate x5 -> x4, local copies, waits for them, and re-layouts: 4.41 us -> 0.71 us  [padded_2(): jnp.concatenate([lax.ppermute(tail, axis, [(i, (i + 1) % count) for i in...]
    reduce_sum x2, other arithmetic: 0.6 us -> 3.3 us  [per_device(): pooled = active.reshape(width_a, depth_b, 2, half, 2, half, 2).mean(axis=...]
    mul x3 -> x2, local copies, waits for them, and re-layouts: 3.67 us -> 1.51 us  [per_device(): jnp.repeat(jnp.repeat(jnp.repeat(back_b, 2, 1), 2, 2), 2, 3) * 0.125]
    pallas_call x1, Pallas kernels: 7.29 us -> 9.25 us  [layer_a_grads(): pl.pallas_call(_layer_a_body, out_shape=(jax.ShapeDtypeStruct((27, chan_i...]
    reshape x0 -> x1, local copies, waits for them, and re-layouts: none -> 1.85 us  [per_device(): back_a.astype(jnp.bfloat16).reshape(1, chan_in, depth_a, side * side)]
  transfers between devices with their start and end apart: 8 -> 8, of which waited for: 0 -> 3; matrix products, arithmetic and copies ran while one was open for 22% -> 11% of each run, Pallas kernels for 43% -> 0%
where the time goes in v5:
time: 148 us; the launch traced here: 147 us
  Pallas kernels  62.9 us (42%)
  local copies, waits for them, and re-layouts  25.2 us (17%)
  starting transfers between devices  23.3 us (16%)
  other arithmetic  16.4 us (11%)
  waiting for transfers between devices  12.4 us (8%)
  matrix products  5.77 us (4%)
    pallas_call x1, Pallas kernels, all_reduce(): pl.pallas_call(_all_reduce_kernel, out_shape=(jax.ShapeDtypeStruct((rows_...  53.6 us
    ppermute x4, starting transfers between devices, padded_2(): lax.ppermute(tail, axis, [(i, (i + 1) % count) for i in range(ends)])  17.8 us
    unnamed x19, local copies, waits for them, and re-layouts  12.7 us
    pallas_call x1, Pallas kernels, layer_a_grads(): pl.pallas_call(_layer_a_body, out_shape=(jax.ShapeDtypeStruct((27, chan_i...  9.25 us
    ppermute x4, waiting for transfers between devices, padded_2(): lax.ppermute(head, axis, [((i + 1) % count, i) for i in range(ends)])  7.94 us
    concatenate x1, other arithmetic, all_reduce(): jnp.concatenate([sums_a.reshape(rows_a, 128) * scale_a, wide[:, :128], wi...  5.89 us
    conv_general_dilated x2, matrix products, conv_cells(): lax.conv_general_dilated(field[None], shaped, (1, 1, 1), ((0, 0), (1, 1),...  5.77 us
    ppermute x4, starting transfers between devices, padded_2(): lax.ppermute(head, axis, [((i + 1) % count, i) for i in range(ends)])  5.56 us
  transfers between devices with their start and end apart: 8, of which 3 were waited for; matrix products, arithmetic and copies ran while one was open for 11% of the time, Pallas kernels for 0%

profile of v5, /device:TPU:1, one launch (start us, length us, event | category | flops | bytes accessed | tf_op | source)
XLA Modules:
  0.0 146.9 jit_solution(1359068426807982191)
XLA Ops:
  0.6 0.0 copy-start.2
  0.6 1.0 copy.25
  1.7 1.0 copy.24
  2.7 0.1 multiply_convert_fusion.1
  2.8 1.3 collective-permute-start.3
  4.1 5.0 %collective-permute-start.2 = (bf16[256,1,256]{0,2,1:T(8,128)(2,1)S(1)}, bf16[256,1,256]{0,2,1:T(8,128)(2,1)S(1)}, u32[]{:S(2)}, u32[]{:S(2)}) collective-permute-start(bf16[256,1,256]{0,2,1:T(8,128)(2,1)S(1)} %bitcast.53), channel_id=1, source_target_pairs={{0,1},{1,2},{2,3},{3,4},{4,5},{5,6},{6,7},{7,8},{8,9},{9,10},{10,1... | collective-permute-start | bytes 393224 | tf_op jit(solution)/shard_map/ppermute | solution.py:21
  9.1 2.9 %fusion = (f32[128,1024]{1,0:T(8,128)S(1)}, f32[1,128,2,1024]{3,2,1,0:T(2,128)S(1)}) fusion(bf16[1,128,2,1024]{3,2,1,0:T(2,128)(2,1)} %param.7), kind=kLoop, calls=%fused_computation.7 | loop fusion | flops 1441792 | bytes 2097152 | tf_op jit(solution)/shard_map/reduce_sum | solution.py:265
  12.0 0.2 copy.31
  12.2 0.4 reduce_sum.18
  12.6 1.3 collective-permute-start.7
  13.9 4.2 %collective-permute-start.6 = (bf16[128,1,256]{0,2,1:T(8,128)(2,1)S(1)}, bf16[128,1,256]{0,2,1:T(8,128)(2,1)S(1)}, u32[]{:S(2)}, u32[]{:S(2)}) collective-permute-start(bf16[128,1,256]{0,2,1:T(8,128)(2,1)S(1)} %bitcast.60), channel_id=1, source_target_pairs={{0,1},{1,2},{2,3},{3,4},{4,5},{5,6},{6,7},{7,8},{8,9},{9,10},{10,1... | collective-permute-start | bytes 196616 | tf_op jit(solution)/shard_map/ppermute | solution.py:21
  18.1 0.0 copy-done.2
  18.1 0.4 fusion.15
  18.5 3.4 %collective-permute-start = (bf16[64,1,1024]{2,1,0:T(2,128)(2,1)S(1)}, bf16[64,1,1024]{2,1,0:T(2,128)(2,1)S(1)}, u32[]{:S(2)}, u32[]{:S(2)}) collective-permute-start(bf16[64,1,1024]{2,1,0:T(2,128)(2,1)S(1)} %get-tuple-element.17), channel_id=1, source_target_pairs={{0,1},{1,2},{2,3},{3,4},{4,5},{5,6},{6,7},{7,8},{8,9},{9,10},{10,1... | collective-permute-start | bytes 393224 | tf_op jit(solution)/shard_map/ppermute | solution.py:21
  21.9 0.9 copy.27
  22.8 1.3 copy.37
  24.1 0.1 copy.33
  24.2 2.9 %rev.3 = bf16[27,128,256]{2,1,0:T(8,128)(2,1)} reverse(bf16[27,128,256]{2,1,0:T(8,128)(2,1)} %param.11), dimensions={0} | reverse | bytes 3538944 | tf_op jit(solution)/shard_map/rev | solution.py:188
  27.1 0.0 collective-permute-done.7
  27.1 1.5 collective-permute-start.1
  28.6 0.1 copy.34
  28.7 0.0 collective-permute-done.6
  28.7 0.1 copy.32
  28.8 2.3 %convolution_multiply_fusion = f32[3,3,3,128,256]{4,3,2,1,0:T(8,128)S(1)} fusion(bf16[1,128,1,16,16]{1,0,4,3,2:T(2,128)(2,1)S(1)} %copy.34, bf16[1,128,1,16,16]{1,0,4,3,2:T(2,128)(2,1)S(1)} %copy.33, bf16[1,128,1,16,16]{1,0,4,3,2:T(2,128)(2,1)S(1)} %copy.32, bf16[1,256,1,16,16]{1,4,3,2,0:T(8,128)(2,1)S(1)} %bitcast.55), kind=kOutput, calls=%fused_computation.5 | convolution fusion | flops 417497088 | bytes 3866624 | tf_op jit(solution)/shard_map/transpose(jvp())/conv_general_dilated | solution.py:176
  31.2 0.0 copy-start.4
  31.2 0.0 copy-start.5
  31.2 1.5 %fusion.13 = (f32[3456,128]{1,0:T(8,128)S(1)}, f32[3456,128]{1,0:T(8,128)}) fusion(f32[3456,256]{1,0:T(8,128)S(1)} %bitcast.40), kind=kLoop, calls=%fused_computation.29 | loop fusion | bytes 7077888 | tf_op jit(solution)/shard_map/slice | solution.py:143
  32.6 0.0 collective-permute-done.3
  32.7 0.3 copy.28
  32.9 0.0 collective-permute-done.2
  32.9 0.3 copy.26
  33.2 0.0 collective-permute-done
  33.2 4.1 %collective-permute-done.1 = bf16[64,1,1024]{2,1,0:T(2,128)(2,1)S(1)} collective-permute-done((bf16[64,1,1024]{2,1,0:T(2,128)(2,1)S(1)}, bf16[64,1,1024]{2,1,0:T(2,128)(2,1)S(1)}, u32[]{:S(2)}, u32[]{:S(2)}) %collective-permute-start.1) | collective-permute-done | bytes 131104 | tf_op jit(solution)/shard_map/ppermute | solution.py:23
  37.3 0.9 pad_maximum_fusion.3
  38.1 1.0 copy.36
  39.1 0.0 copy-done.4
  39.1 0.0 copy-done.5
  39.1 0.0 copy-start.3
  39.1 3.4 %convolution_multiply_fusion.1 = f32[1,128,1,16,16]{1,0,4,3,2:T(1,128)S(1)} fusion(bf16[3,3,3,256,128]{3,4,2,1,0:T(8,128)(2,1)S(1)} %bitcast.50, bf16[1,256,1,16,16]{1,0,4,3,2:T(2,128)(2,1)S(1)} %copy.28, bf16[1,256,1,16,16]{1,0,4,3,2:T(2,128)(2,1)S(1)} %copy-done.5, bf16[1,256,1,16,16]{1,0,4,3,2:T(2,128)(2,1)S(1)} %copy.26), kind=kOutput, calls=%fused_computation.6 | convolution fusion | flops 417234944 | bytes 2293760 | tf_op jit(solution)/shard_map/conv_general_dilated | solution.py:176
  42.6 0.0 copy-start.1
  42.6 0.7 copy-done.1
  43.3 0.3 broadcast_in_dim.23
  43.6 0.2 copy.30
  43.8 0.0 copy-done.3
  43.8 0.7 fusion.1
  44.5 1.5 broadcast_in_dim.21
  46.0 1.3 copy.29
  47.3 0.7 fusion.14
  48.0 5.2 %collective-permute-start.4 = (bf16[128,1,1024]{2,1,0:T(2,128)(2,1)S(1)}, bf16[128,1,1024]{2,1,0:T(2,128)(2,1)S(1)}, u32[]{:S(2)}, u32[]{:S(2)}) collective-permute-start(bf16[128,1,1024]{2,1,0:T(2,128)(2,1)S(1)} %get-tuple-element.15), channel_id=1, source_target_pairs={{0,1},{1,2},{2,3},{3,4},{4,5},{5,6},{6,7},{7,8},{8,9},{9,10},{10,1... | collective-permute-start | bytes 786440 | tf_op jit(solution)/shard_map/ppermute | solution.py:21
  53.3 1.5 %collective-permute-start.5 = (bf16[128,1,1024]{2,1,0:T(2,128)(2,1)S(1)}, bf16[128,1,1024]{2,1,0:T(2,128)(2,1)S(1)}, u32[]{:S(2)}, u32[]{:S(2)}) collective-permute-start(bf16[128,1,1024]{2,1,0:T(2,128)(2,1)S(1)} %get-tuple-element.16), channel_id=1, source_target_pairs={{1,0},{2,1},{3,2},{4,3},{5,4},{6,5},{7,6},{8,7},{9,8},{10,9},{11,1... | collective-permute-start | bytes 786440 | tf_op jit(solution)/shard_map/ppermute | solution.py:23
  54.8 2.5 %multiply_convert_fusion.up_ref = bf16[128,2048]{1,0:T(8,128)(2,1)} fusion(f32[128,2048]{1,0:T(8,128)} %copy.29, f32[128,2048]{1,0:T(8,128)} %bitcast.35), kind=kLoop, calls=%fused_computation.11 | loop fusion | flops 524288 | bytes 2621440 | tf_op jit(solution)/shard_map/convert_element_type | solution.py:275
  57.3 4.5 %collective-permute-done.4 = bf16[128,1,1024]{2,1,0:T(2,128)(2,1)S(1)} collective-permute-done((bf16[128,1,1024]{2,1,0:T(2,128)(2,1)S(1)}, bf16[128,1,1024]{2,1,0:T(2,128)(2,1)S(1)}, u32[]{:S(2)}, u32[]{:S(2)}) %collective-permute-start.4) | collective-permute-done | bytes 262176 | tf_op jit(solution)/shard_map/ppermute | solution.py:21
  61.7 3.9 %collective-permute-done.5 = bf16[128,1,1024]{2,1,0:T(2,128)(2,1)S(1)} collective-permute-done((bf16[128,1,1024]{2,1,0:T(2,128)(2,1)S(1)}, bf16[128,1,1024]{2,1,0:T(2,128)(2,1)S(1)}, u32[]{:S(2)}, u32[]{:S(2)}) %collective-permute-start.5) | collective-permute-done | bytes 262176 | tf_op jit(solution)/shard_map/ppermute | solution.py:23
  65.6 1.8 %pad_maximum_fusion = bf16[128,4,1024]{2,1,0:T(4,128)(2,1)S(1)} fusion(bf16[128,1,1024]{2,1,0:T(2,128)(2,1)S(1)} %collective-permute-done.5, bf16[128,2,1024]{2,1,0:T(2,128)(2,1)S(1)} %fusion.1, bf16[128,1,1024]{2,1,0:T(2,128)(2,1)S(1)} %collective-permute-done.4), kind=kLoop, calls=%fused_computation.8 | loop fusion | flops 3145728 | bytes 2097152 | tf_op jit(solution)/shard_map/concatenate | solution.py:19
  67.3 0.0 copy-start
  67.4 1.3 copy.38
  68.7 9.3 %shard_map.85 = (f32[27,64,128]{2,1,0:T(8,128)}, bf16[64,2048]{1,0:T(8,128)(2,1)}) custom-call(bf16[64,4096]{1,0:T(8,128)(2,1)} %bitcast.46, bf16[128,2048]{1,0:T(8,128)(2,1)} %multiply_convert_fusion.up_ref, bf16[128,4096]{1,0:T(8,128)(2,1)} %bitcast.37, bf16[27,64,128]{2,1,0:T(8,128)(2,1)} %w_ref.1), custom_call_target="tpu_custom_call" | custom-call | tf_op jit(solution)/shard_map/pallas_call | solution.py:235
  77.9 1.8 %reshape.212 = bf16[1,64,2,1024]{3,2,1,0:T(2,128)(2,1)} reshape(bf16[64,2048]{1,0:T(8,128)(2,1)} %get-tuple-element.7) | data formatting | bytes 524288 | tf_op jit(solution)/shard_map/reshape | solution.py:282
  79.8 1.3 broadcast_multiply_fusion
  81.1 0.0 copy-done
  81.1 5.9 %select_maximum_fusion.x_ref = f32[9216,128]{1,0:T(8,128)} fusion(f32[3456,128]{1,0:T(8,128)S(1)} %copy-done, f32[3456,128]{1,0:T(8,128)S(1)} %get-tuple-element.11, f32[1728,128]{1,0:T(8,128)S(1)} %bitcast.39), kind=kLoop, calls=%fused_computation | loop fusion | flops 7077888 | bytes 9142272 | tf_op jit(solution)/shard_map/concatenate | solution.py:143
  87.0 53.6 %shard_map.86 = (f32[1728,128]{1,0:T(8,128)}, f32[3456,256]{1,0:T(8,128)}) custom-call(f32[9216,128]{1,0:T(8,128)} %select_maximum_fusion.x_ref), custom_call_target="tpu_custom_call" | custom-call | tf_op jit(solution)/shard_map/pallas_call | solution.py:152
  140.6 2.2 %copy.43 = f32[27,64,128]{2,1,0:T(8,128)} copy(f32[27,64,128]{2,1,0:T(8,128)} %bitcast.51) | data formatting | bytes 1769472
  142.7 4.2 %copy.44 = f32[27,128,256]{2,1,0:T(8,128)} copy(f32[27,128,256]{2,1,0:T(8,128)} %bitcast.41) | data formatting | bytes 7077888
  (3 shorter events, 0.0 us)
Async XLA Ops:
  0.6 17.5 %copy-start.2 = (bf16[1,64,2,1024]{3,2,1,0:T(2,128)(2,1)S(1)}, bf16[1,64,2,1024]{3,2,1,0:T(2,128)(2,1)}, u32[]{:S(2)}) copy-start(bf16[1,64,2,1024]{3,2,1,0:T(2,128)(2,1)} %param.6) | copy-start | bytes 786436
  2.8 29.9 %collective-permute-start.3 = (bf16[256,1,256]{0,2,1:T(8,128)(2,1)S(1)}, bf16[256,1,256]{0,2,1:T(8,128)(2,1)S(1)}, u32[]{:S(2)}, u32[]{:S(2)}) collective-permute-start(bf16[256,1,256]{0,2,1:T(8,128)(2,1)S(1)} %bitcast.52), channel_id=1, source_target_pairs={{1,0},{2,1},{3,2},{4,3},{5,4},{6,5},{7,6},{8,7},{9,8},{10,9},{11,1... | collective-permute-start | bytes 393224 | tf_op jit(solution)/shard_map/ppermute | solution.py:23
  4.1 28.9 %collective-permute-start.2 = (bf16[256,1,256]{0,2,1:T(8,128)(2,1)S(1)}, bf16[256,1,256]{0,2,1:T(8,128)(2,1)S(1)}, u32[]{:S(2)}, u32[]{:S(2)}) collective-permute-start(bf16[256,1,256]{0,2,1:T(8,128)(2,1)S(1)} %bitcast.53), channel_id=1, source_target_pairs={{0,1},{1,2},{2,3},{3,4},{4,5},{5,6},{6,7},{7,8},{8,9},{9,10},{10,1... | collective-permute-start | bytes 393224 | tf_op jit(solution)/shard_map/ppermute | solution.py:21
  12.6 14.5 %collective-permute-start.7 = (bf16[128,1,256]{0,2,1:T(8,128)(2,1)S(1)}, bf16[128,1,256]{0,2,1:T(8,128)(2,1)S(1)}, u32[]{:S(2)}, u32[]{:S(2)}) collective-permute-start(bf16[128,1,256]{0,2,1:T(8,128)(2,1)S(1)} %bitcast.59), channel_id=1, source_target_pairs={{1,0},{2,1},{3,2},{4,3},{5,4},{6,5},{7,6},{8,7},{9,8},{10,9},{11,1... | collective-permute-start | bytes 196616 | tf_op jit(solution)/shard_map/ppermute | solution.py:23
  13.9 14.8 %collective-permute-start.6 = (bf16[128,1,256]{0,2,1:T(8,128)(2,1)S(1)}, bf16[128,1,256]{0,2,1:T(8,128)(2,1)S(1)}, u32[]{:S(2)}, u32[]{:S(2)}) collective-permute-start(bf16[128,1,256]{0,2,1:T(8,128)(2,1)S(1)} %bitcast.60), channel_id=1, source_target_pairs={{0,1},{1,2},{2,3},{3,4},{4,5},{5,6},{6,7},{7,8},{8,9},{9,10},{10,1... | collective-permute-start | bytes 196616 | tf_op jit(solution)/shard_map/ppermute | solution.py:21
  18.5 14.7 %collective-permute-start = (bf16[64,1,1024]{2,1,0:T(2,128)(2,1)S(1)}, bf16[64,1,1024]{2,1,0:T(2,128)(2,1)S(1)}, u32[]{:S(2)}, u32[]{:S(2)}) collective-permute-start(bf16[64,1,1024]{2,1,0:T(2,128)(2,1)S(1)} %get-tuple-element.17), channel_id=1, source_target_pairs={{0,1},{1,2},{2,3},{3,4},{4,5},{5,6},{6,7},{7,8},{8,9},{9,10},{10,1... | collective-permute-start | bytes 393224 | tf_op jit(solution)/shard_map/ppermute | solution.py:21
  27.1 10.2 %collective-permute-start.1 = (bf16[64,1,1024]{2,1,0:T(2,128)(2,1)S(1)}, bf16[64,1,1024]{2,1,0:T(2,128)(2,1)S(1)}, u32[]{:S(2)}, u32[]{:S(2)}) collective-permute-start(bf16[64,1,1024]{2,1,0:T(2,128)(2,1)S(1)} %get-tuple-element.18), channel_id=1, source_target_pairs={{1,0},{2,1},{3,2},{4,3},{5,4},{6,5},{7,6},{8,7},{9,8},{10,9},{11,1... | collective-permute-start | bytes 393224 | tf_op jit(solution)/shard_map/ppermute | solution.py:23
  31.2 8.0 %copy-start.4 = (bf16[27,128,256]{2,1,0:T(8,128)(2,1)S(1)}, bf16[27,128,256]{2,1,0:T(8,128)(2,1)}, u32[]{:S(2)}) copy-start(bf16[27,128,256]{2,1,0:T(8,128)(2,1)} %rev.3) | copy-start | bytes 5308420
  31.2 8.0 %copy-start.5 = (bf16[1,256,1,16,16]{1,0,4,3,2:T(2,128)(2,1)S(1)}, bf16[1,256,1,16,16]{1,0,4,3,2:T(2,128)(2,1)}, u32[]{:S(2)}) copy-start(bf16[1,256,1,16,16]{1,0,4,3,2:T(2,128)(2,1)} %copy.27) | copy-start | bytes 393220
  39.1 4.7 %copy-start.3 = (bf16[1,128,2,1024]{3,2,1,0:T(2,128)(2,1)S(1)}, bf16[1,128,2,1024]{3,2,1,0:T(2,128)(2,1)}, u32[]{:S(2)}) copy-start(bf16[1,128,2,1024]{3,2,1,0:T(2,128)(2,1)} %param.7) | copy-start | bytes 1572868
  42.6 0.7 copy-start.1
  48.0 13.7 %collective-permute-start.4 = (bf16[128,1,1024]{2,1,0:T(2,128)(2,1)S(1)}, bf16[128,1,1024]{2,1,0:T(2,128)(2,1)S(1)}, u32[]{:S(2)}, u32[]{:S(2)}) collective-permute-start(bf16[128,1,1024]{2,1,0:T(2,128)(2,1)S(1)} %get-tuple-element.15), channel_id=1, source_target_pairs={{0,1},{1,2},{2,3},{3,4},{4,5},{5,6},{6,7},{7,8},{8,9},{9,10},{10,1... | collective-permute-start | bytes 786440 | tf_op jit(solution)/shard_map/ppermute | solution.py:21
  53.3 12.3 %collective-permute-start.5 = (bf16[128,1,1024]{2,1,0:T(2,128)(2,1)S(1)}, bf16[128,1,1024]{2,1,0:T(2,128)(2,1)S(1)}, u32[]{:S(2)}, u32[]{:S(2)}) collective-permute-start(bf16[128,1,1024]{2,1,0:T(2,128)(2,1)S(1)} %get-tuple-element.16), channel_id=1, source_target_pairs={{1,0},{2,1},{3,2},{4,3},{5,4},{6,5},{7,6},{8,7},{9,8},{10,9},{11,1... | collective-permute-start | bytes 786440 | tf_op jit(solution)/shard_map/ppermute | solution.py:23
  67.3 13.7 %copy-start = (f32[3456,128]{1,0:T(8,128)S(1)}, f32[3456,128]{1,0:T(8,128)}, u32[]{:S(2)}) copy-start(f32[3456,128]{1,0:T(8,128)} %get-tuple-element.12) | copy-start | bytes 5308420

commit v6 on v5

--- a/solution.py
+++ b/solution.py
@@ -243,6 +243,67 @@
     )(source_pad.reshape(chan_in, -1), grad_hidden.reshape(chan_out, -1), hidden_pad.reshape(chan_out, -1), weight_a)
 
 
+def _halo_body(heads_ref, tails_ref, below_ref, above_ref, got_below, got_above, sends, recvs):
+    mesh_id = pl.DeviceIdType.MESH
+    count = lax.axis_size("space")
+    dp = lax.axis_index("dp")
+    sp = lax.axis_index("space")
+    up = (dp, (sp + 1) % count)
+    down = (dp, (sp + count - 1) % count)
+    barrier = pltpu.get_barrier_semaphore()
+    for other in (up, down):
+        pl.semaphore_signal(barrier, inc=1, device_id=other, device_id_type=mesh_id)
+    pl.semaphore_wait(barrier, 2)
+    copies = [
+        pltpu.make_async_remote_copy(
+            src_ref=tails_ref, dst_ref=got_below, send_sem=sends.at[0], recv_sem=recvs.at[0], device_id=up, device_id_type=mesh_id
+        ),
+        pltpu.make_async_remote_copy(
+            src_ref=heads_ref, dst_ref=got_above, send_sem=sends.at[1], recv_sem=recvs.at[1], device_id=down, device_id_type=mesh_id
+        ),
+    ]
+    for copy in copies:
+        copy.start()
+    for copy in copies:
+        copy.wait()
+    below_ref[...] = jnp.where(sp > 0, got_below[...], jnp.zeros_like(got_below[...]))
+    above_ref[...] = jnp.where(sp < count - 1, got_above[...], jnp.zeros_like(got_above[...]))
+
+
+def halos(arrays, tag):
+    heads = jnp.concatenate([a[:, :1].reshape(-1) for a in arrays])
+    tails = jnp.concatenate([a[:, -1:].reshape(-1) for a in arrays])
+    count = heads.shape[0]
+    unit = 16 * 128
+    size = -(-count // unit) * unit
+    heads = jnp.pad(heads, (0, size - count)).reshape(size // 128, 128)
+    tails = jnp.pad(tails, (0, size - count)).reshape(size // 128, 128)
+    block = jax.ShapeDtypeStruct(heads.shape, heads.dtype)
+    below, above = pl.pallas_call(
+        _halo_body,
+        out_shape=(block, block),
+        in_specs=[pl.BlockSpec(memory_space=pltpu.VMEM)] * 2,
+        out_specs=(pl.BlockSpec(memory_space=pltpu.VMEM), pl.BlockSpec(memory_space=pltpu.VMEM)),
+        scratch_shapes=[
+            pltpu.VMEM(heads.shape, heads.dtype),
+            pltpu.VMEM(heads.shape, heads.dtype),
+            pltpu.SemaphoreType.DMA((2,)),
+            pltpu.SemaphoreType.DMA((2,)),
+        ],
+        compiler_params=pltpu.CompilerParams(collective_id=tag, has_side_effects=True),
+    )(heads, tails)
+    below, above = below.reshape(-1), above.reshape(-1)
+    out, start = [], 0
+    for a in arrays:
+        plane = a.shape[0] * a.shape[2]
+        shape = (a.shape[0], 1, a.shape[2])
+        low = below[start : start + plane].reshape(shape)
+        high = above[start : start + plane].reshape(shape)
+        out.append(jnp.concatenate([low, a, high], axis=1))
+        start += plane
+    return out
+
+
 def per_device(layer_input, hidden_pre, output_pre, output_grad, weight_a, weight_b):
     side = math.isqrt(layer_input.shape[3])
     half = side // 2
@@ -266,8 +327,9 @@
         .astype(jnp.bfloat16)
     )
     pooled = pooled.reshape(width_a, depth_b, half * half)
-    outer_pad = padded_2(grad_outer, (("space", 1),), 1).reshape(width_b, depth_b + 2, half, half)
-    pooled_pad = padded_2(pooled, (("space", 1),), 1).reshape(width_a, depth_b + 2, half, half)
+    outer_pad, pooled_pad, source_pad = halos([grad_outer, pooled, source], 1)
+    outer_pad = outer_pad.reshape(width_b, depth_b + 2, half, half)
+    pooled_pad = pooled_pad.reshape(width_a, depth_b + 2, half, half)
     back_b = back_cells(outer_pad, weight_b)
     sums_b = kernel_terms(pooled_pad, grad_outer.reshape(width_b, depth_b, half, half))
     upward = jnp.repeat(jnp.repeat(jnp.repeat(back_b, 2, 1), 2, 2), 2, 3) * 0.125
@@ -276,8 +338,7 @@
         jnp.bfloat16
     )
     grad_hidden = grad_hidden.reshape(width_a, depth_a, side * side)
-    hidden_pad = padded_2(grad_hidden, (("space", 1),), 1)
-    source_pad = padded_2(source, (("space", 1),), 1)
+    (hidden_pad,) = halos([grad_hidden], 2)
     sums_a, back_a = layer_a_grads(source_pad, hidden_pad, grad_hidden, weight_a)
     input_grad = back_a.astype(jnp.bfloat16).reshape(1, chan_in, depth_a, side * side)
     samples = lax.axis_size("dp")

time: 148 us -> 150 us (1.014)
  Pallas kernels: 62.9 us -> 86.2 us
  starting transfers between devices: 23.3 us -> 0 us
  local copies, waits for them, and re-layouts: 25.2 us -> 39.1 us
  waiting for transfers between devices: 12.4 us -> 0 us
    pallas_call x0 -> x2, Pallas kernels: none -> 27.9 us  [halos(): pl.pallas_call(_halo_body, out_shape=(block, block), in_specs=[pl.BlockSp...]
    ppermute x8 -> x0, starting transfers between devices: 23.3 us -> none  [the longest x4 17.8 us: padded_2(): lax.ppermute(tail, axis, [(i, (i + 1) % count) for i in range(ends)])]
    ppermute x8 -> x0, waiting for transfers between devices: 12.4 us -> none  [the longest x4 7.94 us: padded_2(): lax.ppermute(head, axis, [((i + 1) % count, i) for i in range(ends)])]
    slice x2 -> x5, local copies, waits for them, and re-layouts: 1.09 us -> 7.16 us  [the longest x2 4.34 us: halos(): tails = jnp.concatenate([a[:, -1:].reshape(-1) for a in arrays])]
    concatenate x4 -> x8, local copies, waits for them, and re-layouts: 0.71 us -> 6.54 us  [halos(): out.append(jnp.concatenate([low, a, high], axis=1))]
    pallas_call x1, Pallas kernels: 53.6 us -> 49 us  [all_reduce(): pl.pallas_call(_all_reduce_kernel, out_shape=(jax.ShapeDtypeStruct((rows_...]
    another operation x0 -> x3, local copies, waits for them, and re-layouts: none -> 4.3 us  [the longest x1 2.21 us: halos(): high = above[start:start + plane].reshape(shape)]
    select_n x0 -> x1, other arithmetic: none -> 2.93 us  [slopes(): jnp.where(values > 0, jnp.ones_like(values), negative_slope * jnp.ones_li...]
  transfers between devices with their start and end apart: 8 -> 0, of which waited for: 3 -> 0; matrix products, arithmetic and copies ran while one was open for 11% -> 0% of each run, Pallas kernels for 0% -> 0%
where the time goes in v6:
time: 150 us; the launch traced here: 149 us
  Pallas kernels  86.2 us (57%)
  local copies, waits for them, and re-layouts  39.1 us (26%)
  other arithmetic  15.7 us (10%)
  matrix products  7.18 us (5%)
    pallas_call x1, Pallas kernels, all_reduce(): pl.pallas_call(_all_reduce_kernel, out_shape=(jax.ShapeDtypeStruct((rows_...  49 us
    pallas_call x2, Pallas kernels, halos(): pl.pallas_call(_halo_body, out_shape=(block, block), in_specs=[pl.BlockSp...  27.9 us
    unnamed x20, local copies, waits for them, and re-layouts  11.2 us
    pallas_call x1, Pallas kernels, layer_a_grads(): pl.pallas_call(_layer_a_body, out_shape=(jax.ShapeDtypeStruct((27, chan_i...  9.25 us
    conv_general_dilated x2, matrix products, conv_cells(): lax.conv_general_dilated(field[None], shaped, (1, 1, 1), ((0, 0), (1, 1),...  7.18 us
    concatenate x8, local copies, waits for them, and re-layouts, halos(): out.append(jnp.concatenate([low, a, high], axis=1))  6.54 us
    concatenate x1, other arithmetic, all_reduce(): jnp.concatenate([sums_a.reshape(rows_a, 128) * scale_a, wide[:, :128], wi...  5.87 us
    slice x2, local copies, waits for them, and re-layouts, halos(): tails = jnp.concatenate([a[:, -1:].reshape(-1) for a in arrays])  4.34 us

profile of v6, /device:TPU:1, one launch (start us, length us, event | category | flops | bytes accessed | tf_op | source)
XLA Modules:
  0.0 149.3 jit_solution(16115898428005063374)
XLA Ops:
  0.6 1.0 copy.53
  1.6 1.0 copy.52
  2.6 0.1 multiply_convert_fusion.1
  2.7 0.1 copy.54
  2.8 0.1 copy.70
  2.9 0.3 copy.60
  3.2 2.2 %slice_reduce_fusion.2 = (bf16[64,1024]{1,0:T(8,128)(2,1)S(1)}, bf16[64,1024]{1,0:T(8,128)(2,1)S(1)}) fusion(bf16[64,2,1024]{2,1,0:T(2,128)(2,1)} %bitcast.49), kind=kLoop, calls=%fused_computation.28 | loop fusion | bytes 524288 | tf_op jit(solution)/shard_map/slice | solution.py:275
  5.4 2.9 %compare_select_fusion = (f32[1,128,2,1024]{3,2,1,0:T(2,128)S(1)}, f32[128,1024]{1,0:T(8,128)S(1)}) fusion(bf16[1,128,2,1024]{3,2,1,0:T(2,128)(2,1)} %param.7), kind=kLoop, calls=%fused_computation.3 | loop fusion | flops 1441792 | bytes 2097152 | tf_op jit(solution)/shard_map/jit(_where)/select_n | solution.py:31
  8.4 0.3 copy.74
  8.7 0.0 copy-start
  8.7 0.2 copy.55
  8.9 0.4 reduce_sum.18
  9.3 0.7 copy.67
  10.1 0.4 copy.56
  10.5 0.3 convert_element_type.86
  10.9 0.9 maximum_bitcast_fusion.1
  11.7 16.4 %shard_map.85 = (bf16[1280,128]{1,0:T(8,128)(2,1)}, bf16[1280,128]{1,0:T(8,128)(2,1)}) custom-call(bf16[1280,128]{1,0:T(8,128)(2,1)} %get-tuple-element.32.heads_ref, bf16[1280,128]{1,0:T(8,128)(2,1)} %get-tuple-element.31.tails_ref), custom_call_target="tpu_custom_call" | custom-call | tf_op jit(solution)/shard_map/pallas_call | solution.py:282
  28.1 0.8 slice.50
  29.0 0.8 slice.51
  29.8 1.1 fusion.14
  31.1 0.0 copy-done
  31.1 0.9 pad_maximum_fusion.3
  32.0 1.0 copy.73
  32.9 0.4 concatenate.39
  33.3 1.1 copy.68
  34.4 0.4 concatenate.38
  34.8 1.1 copy.66
  35.9 0.7 concatenate.34
  36.6 1.2 copy.59
  37.8 0.7 concatenate.35
  38.5 1.0 copy.61
  39.5 2.9 %rev.3 = bf16[27,128,256]{2,1,0:T(8,128)(2,1)} reverse(bf16[27,128,256]{2,1,0:T(8,128)(2,1)} %param.11), dimensions={0} | reverse | bytes 3538944 | tf_op jit(solution)/shard_map/rev | solution.py:188
  42.4 0.0 copy-start.1
  42.4 4.8 %convolution_multiply_fusion.1 = f32[1,128,1,16,16]{1,0,4,3,2:T(1,128)S(1)} fusion(bf16[3,3,3,256,128]{3,4,2,1,0:T(8,128)(2,1)} %bitcast.55, bf16[1,256,1,16,16]{1,0,4,3,2:T(2,128)(2,1)S(1)} %copy.61, bf16[1,256,1,16,16]{1,0,4,3,2:T(2,128)(2,1)S(1)} %copy.60, bf16[1,256,1,16,16]{1,0,4,3,2:T(2,128)(2,1)S(1)} %copy.59), kind=kOutput, calls=%fused_computation.6 | convolution fusion | flops 417234944 | bytes 2293760 | tf_op jit(solution)/shard_map/conv_general_dilated | solution.py:176
  47.3 0.3 broadcast_in_dim.23
  47.6 0.2 copy.63
  47.8 0.0 copy-done.1
  47.8 0.7 fusion.1
  48.5 2.2 %slice_reduce_fusion = (bf16[128,1024]{1,0:T(8,128)(2,1)S(1)}, bf16[128,1024]{1,0:T(8,128)(2,1)S(1)}) fusion(bf16[128,2,1024]{2,1,0:T(2,128)(2,1)S(1)} %fusion.1), kind=kLoop, calls=%fused_computation.16 | loop fusion | bytes 1048576 | tf_op jit(solution)/shard_map/slice | solution.py:275
  50.7 0.8 reshape.231.tails_ref
  51.5 0.8 reshape.230.heads_ref
  52.3 11.6 %shard_map.86 = (bf16[1024,128]{1,0:T(8,128)(2,1)}, bf16[1024,128]{1,0:T(8,128)(2,1)}) custom-call(bf16[1024,128]{1,0:T(8,128)(2,1)} %reshape.230.heads_ref, bf16[1024,128]{1,0:T(8,128)(2,1)} %reshape.231.tails_ref), custom_call_target="tpu_custom_call" | custom-call | tf_op jit(solution)/shard_map/pallas_call | solution.py:282
  63.9 2.0 %reshape_reshape.10 = bf16[128,1,1024]{2,1,0:T(2,128)(2,1)S(1)} reshape(bf16[1024,128]{1,0:T(8,128)(2,1)} %get-tuple-element.13) | data formatting | bytes 524288 | tf_op jit(solution)/shard_map/reshape;reshape | solution.py:300
  65.9 2.2 %reshape_reshape.11 = bf16[128,1,1024]{2,1,0:T(2,128)(2,1)S(1)} reshape(bf16[1024,128]{1,0:T(8,128)(2,1)} %get-tuple-element.14) | data formatting | bytes 524288 | tf_op jit(solution)/shard_map/reshape;reshape | solution.py:301
  68.1 1.8 %pad_maximum_fusion = bf16[128,4,1024]{2,1,0:T(4,128)(2,1)S(1)} fusion(bf16[128,1,1024]{2,1,0:T(2,128)(2,1)S(1)} %reshape_reshape.11, bf16[128,2,1024]{2,1,0:T(2,128)(2,1)S(1)} %fusion.1, bf16[128,1,1024]{2,1,0:T(2,128)(2,1)S(1)} %reshape_reshape.10), kind=kLoop, calls=%fused_computation.8 | loop fusion | flops 3145728 | bytes 2097152 | tf_op jit(solution)/shard_map/concatenate | solution.py:302
  69.9 1.3 copy.75
  71.2 0.5 broadcast_in_dim.21
  71.7 0.3 copy.62
  72.1 0.0 copy-start.2
  72.1 0.0 copy-start.3
  72.1 0.0 copy-start.4
  72.1 0.9 multiply_convert_fusion.up_ref
  73.0 9.2 %shard_map.87 = (f32[27,64,128]{2,1,0:T(8,128)}, bf16[64,2048]{1,0:T(8,128)(2,1)}) custom-call(bf16[64,4096]{1,0:T(8,128)(2,1)} %bitcast.51, bf16[128,2048]{1,0:T(8,128)(2,1)} %multiply_convert_fusion.up_ref, bf16[128,4096]{1,0:T(8,128)(2,1)} %bitcast.41, bf16[27,64,128]{2,1,0:T(8,128)(2,1)} %w_ref.1), custom_call_target="tpu_custom_call" | custom-call | tf_op jit(solution)/shard_map/pallas_call | solution.py:235
  82.3 1.8 %reshape.233 = bf16[1,64,2,1024]{3,2,1,0:T(2,128)(2,1)} reshape(bf16[64,2048]{1,0:T(8,128)(2,1)} %get-tuple-element.15) | data formatting | bytes 524288 | tf_op jit(solution)/shard_map/reshape | solution.py:343
  84.1 1.3 broadcast_multiply_fusion
  85.4 0.0 copy-done.2
  85.4 0.0 copy-done.3
  85.4 0.0 copy-done.4
  85.4 2.3 %convolution_multiply_fusion = f32[3,3,3,128,256]{4,3,2,1,0:T(8,128)S(1)} fusion(bf16[1,128,1,16,16]{1,0,4,3,2:T(2,128)(2,1)S(1)} %copy-done.2, bf16[1,128,1,16,16]{1,0,4,3,2:T(2,128)(2,1)S(1)} %copy-done.4, bf16[1,128,1,16,16]{1,0,4,3,2:T(2,128)(2,1)S(1)} %copy-done.3, bf16[1,256,1,16,16]{1,4,3,2,0:T(8,128)(2,1)S(1)} %bitcast.57), kind=kOutput, calls=%fused_computation.5 | convolution fusion | flops 417497088 | bytes 3866624 | tf_op jit(solution)/shard_map/transpose(jvp())/conv_general_dilated | solution.py:176
  87.7 0.2 fusion.13
  88.0 5.9 %select_maximum_fusion.x_ref = f32[9216,128]{1,0:T(8,128)} fusion(f32[3456,128]{1,0:T(8,128)S(1)} %get-tuple-element.24, f32[3456,128]{1,0:T(8,128)S(1)} %get-tuple-element.23, f32[1728,128]{1,0:T(8,128)S(1)} %bitcast.44), kind=kLoop, calls=%fused_computation | loop fusion | flops 7077888 | bytes 9142272 | tf_op jit(solution)/shard_map/concatenate | solution.py:143
  93.8 49.0 %shard_map.88 = (f32[1728,128]{1,0:T(8,128)}, f32[3456,256]{1,0:T(8,128)}) custom-call(f32[9216,128]{1,0:T(8,128)} %select_maximum_fusion.x_ref), custom_call_target="tpu_custom_call" | custom-call | tf_op jit(solution)/shard_map/pallas_call | solution.py:152
  142.9 2.2 %copy.80 = f32[27,64,128]{2,1,0:T(8,128)} copy(f32[27,64,128]{2,1,0:T(8,128)} %bitcast.58) | data formatting | bytes 1769472
  145.1 4.2 %copy.81 = f32[27,128,256]{2,1,0:T(8,128)} copy(f32[27,128,256]{2,1,0:T(8,128)} %bitcast.46) | data formatting | bytes 7077888
  (7 shorter events, 0.2 us)
Async XLA Ops:
  8.7 22.4 %copy-start = (bf16[1,64,2,1024]{3,2,1,0:T(2,128)(2,1)S(1)}, bf16[1,64,2,1024]{3,2,1,0:T(2,128)(2,1)}, u32[]{:S(2)}) copy-start(bf16[1,64,2,1024]{3,2,1,0:T(2,128)(2,1)} %param.6) | copy-start | bytes 786436
  42.4 5.4 %copy-start.1 = (bf16[1,128,2,1024]{3,2,1,0:T(2,128)(2,1)S(1)}, bf16[1,128,2,1024]{3,2,1,0:T(2,128)(2,1)}, u32[]{:S(2)}) copy-start(bf16[1,128,2,1024]{3,2,1,0:T(2,128)(2,1)} %param.7) | copy-start | bytes 1572868
  72.1 13.3 %copy-start.2 = (bf16[1,128,1,16,16]{1,0,4,3,2:T(2,128)(2,1)S(1)}, bf16[1,128,1,16,16]{1,0,4,3,2:T(2,128)(2,1)}, u32[]{:S(2)}) copy-start(bf16[1,128,1,16,16]{1,0,4,3,2:T(2,128)(2,1)} %copy.68) | copy-start | bytes 196612
  72.1 13.3 %copy-start.3 = (bf16[1,128,1,16,16]{1,0,4,3,2:T(2,128)(2,1)S(1)}, bf16[1,128,1,16,16]{1,0,4,3,2:T(2,128)(2,1)}, u32[]{:S(2)}) copy-start(bf16[1,128,1,16,16]{1,0,4,3,2:T(2,128)(2,1)} %copy.66) | copy-start | bytes 196612
  72.1 13.3 %copy-start.4 = (bf16[1,128,1,16,16]{1,0,4,3,2:T(2,128)(2,1)S(1)}, bf16[1,128,1,16,16]{1,0,4,3,2:T(2,128)(2,1)}, u32[]{:S(2)}) copy-start(bf16[1,128,1,16,16]{1,0,4,3,2:T(2,128)(2,1)} %copy.67) | copy-start | bytes 196612

commit v7 on v4

--- a/solution.py
+++ b/solution.py
@@ -197,38 +197,37 @@
     return pull(upstream.astype(jnp.float32))[0]
 
 
-def _kernel_terms_body(src_ref, up_ref, out_ref):
+def _terms_a_body(src_ref, up_ref, terms_ref):
     cells = up_ref.shape[1]
     width = src_ref.shape[1]
-    margin = 128
-    plane = 1024
+    plane = width // 4
     side = 32
     spot = lax.broadcasted_iota(jnp.int32, (1, cells), 1)
     column = spot % side
     row = (spot // side) % side
     upstream = up_ref[...]
+    field = src_ref[...].astype(jnp.float32)
     for b in range(3):
         for c in range(3):
             shift = (b - 1) * side + (c - 1)
-            moved = pltpu.roll(src_ref[...], (width - shift) % width, 1)
+            moved = pltpu.roll(field, (width - shift) % width, 1)
             inside = (column + c - 1 >= 0) & (column + c - 1 < side) & (row + b - 1 >= 0) & (row + b - 1 < side)
             for a in range(3):
-                window = moved[:, margin + a * plane : margin + a * plane + cells]
+                window = moved[:, a * plane : a * plane + cells]
                 window = jnp.where(inside, window, 0.0).astype(jnp.bfloat16)
-                out_ref[9 * a + 3 * b + c] = lax.dot_general(
+                terms_ref[9 * a + 3 * b + c] = lax.dot_general(
                     window, upstream, (((1,), (1,)), ((), ())), preferred_element_type=jnp.float32
                 )
 
 
-def kernel_terms_flat(padded, upstream):
-    chan_in, chan_out = padded.shape[0], upstream.shape[0]
-    field = jnp.pad(padded.reshape(chan_in, -1).astype(jnp.float32), ((0, 0), (128, 128)))
+def kernel_terms_flat(source_pad, grad_hidden):
+    chan_in, chan_out = source_pad.shape[0], grad_hidden.shape[0]
     return pl.pallas_call(
-        _kernel_terms_body,
+        _terms_a_body,
         out_shape=jax.ShapeDtypeStruct((27, chan_in, chan_out), jnp.float32),
         in_specs=[pl.BlockSpec(memory_space=pltpu.VMEM)] * 2,
         out_specs=pl.BlockSpec(memory_space=pltpu.VMEM),
-    )(field, upstream.reshape(chan_out, -1))
+    )(source_pad.reshape(chan_in, -1), grad_hidden.reshape(chan_out, -1))
 
 
 def per_device(layer_input, hidden_pre, output_pre, output_grad, weight_a, weight_b):
@@ -265,7 +264,7 @@
     )
     grad_hidden = grad_hidden.reshape(width_a, depth_a, side * side)
     hidden_pad = padded_2(grad_hidden, (("space", 1),), 1).reshape(width_a, depth_a + 2, side, side)
-    source_pad = padded_2(source, (("space", 1),), 1).reshape(chan_in, depth_a + 2, side, side)
+    source_pad = padded_2(source, (("space", 1),), 1)
     back_a = back_cells(hidden_pad, weight_a)
     sums_a = kernel_terms_flat(source_pad, grad_hidden)
     input_grad = back_a.astype(jnp.bfloat16).reshape(1, chan_in, depth_a, side * side)

time: 147 us -> 147 us (level)
  no operation moved by 1% of the time
where the time goes in v7:
time: 147 us; the launch traced here: 146 us
  Pallas kernels  62.5 us (43%)
  local copies, waits for them, and re-layouts  32.5 us (22%)
  starting transfers between devices  24.7 us (17%)
  other arithmetic  14.1 us (10%)
  matrix products  11.4 us (8%)
    pallas_call x1, Pallas kernels, all_reduce(): pl.pallas_call(_all_reduce_kernel, out_shape=(jax.ShapeDtypeStruct((rows_...  55.3 us
    ppermute x4, starting transfers between devices, padded_2(): lax.ppermute(tail, axis, [(i, (i + 1) % count) for i in range(ends)])  19.3 us
    unnamed x29, local copies, waits for them, and re-layouts  11.7 us
    conv_general_dilated x3, matrix products, conv_cells(): lax.conv_general_dilated(field[None], shaped, (1, 1, 1), ((0, 0), (1, 1),...  11.4 us
    pallas_call x1, Pallas kernels, kernel_terms_flat(): pl.pallas_call(_terms_a_body, out_shape=jax.ShapeDtypeStruct((27, chan_in...  7.13 us
    concatenate x1, other arithmetic, all_reduce(): jnp.concatenate([sums_a.reshape(rows_a, 128) * scale_a, wide[:, :128], wi...  5.6 us
    ppermute x4, starting transfers between devices, padded_2(): lax.ppermute(head, axis, [((i + 1) % count, i) for i in range(ends)])  5.45 us
    concatenate x5, local copies, waits for them, and re-layouts, padded_2(): jnp.concatenate([lax.ppermute(tail, axis, [(i, (i + 1) % count) for i in...  4.56 us
  transfers between devices with their start and end apart: 8, of which 0 were waited for; matrix products, arithmetic and copies ran while one was open for 22% of the time, Pallas kernels for 43%

profile of v7, /device:TPU:1, one launch (start us, length us, event | category | flops | bytes accessed | tf_op | source)
XLA Modules:
  0.0 146.2 jit_solution(15641777617909506349)
XLA Ops:
  0.6 1.0 copy.16
  1.6 1.0 copy.15
  2.6 0.1 multiply_convert_fusion.2
  2.7 0.0 copy-start.1
  2.7 1.4 collective-permute-start.1
  4.2 5.7 %collective-permute-start = (bf16[256,1,256]{0,2,1:T(8,128)(2,1)S(1)}, bf16[256,1,256]{0,2,1:T(8,128)(2,1)}, u32[]{:S(2)}, u32[]{:S(2)}) collective-permute-start(bf16[256,1,256]{0,2,1:T(8,128)(2,1)S(1)} %bitcast.73), channel_id=1, source_target_pairs={{0,1},{1,2},{2,3},{3,4},{4,5},{5,6},{6,7},{7,8},{8,9},{9,10},{10,1... | collective-permute-start | bytes 393224 | tf_op jit(solution)/shard_map/ppermute | solution.py:21
  9.8 1.4 copy.22
  11.2 0.2 fusion.14
  11.4 0.4 reduce_sum.18
  11.8 0.6 multiply_convert_fusion.3
  12.4 1.3 collective-permute-start.7
  13.7 4.6 %collective-permute-start.6 = (bf16[128,1,256]{0,2,1:T(8,128)(2,1)}, bf16[128,1,256]{0,2,1:T(8,128)(2,1)}, u32[]{:S(2)}, u32[]{:S(2)}) collective-permute-start(bf16[128,1,256]{0,2,1:T(8,128)(2,1)} %bitcast.27), channel_id=1, source_target_pairs={{0,1},{1,2},{2,3},{3,4},{4,5},{5,6},{6,7},{7,8},{8,9},{9,10},{10,1... | collective-permute-start | bytes 196616 | tf_op jit(solution)/shard_map/ppermute | solution.py:21
  18.3 1.2 fusion.33
  19.5 3.0 %collective-permute-start.4 = (bf16[64,1,1024]{2,1,0:T(2,128)(2,1)}, bf16[64,1,1024]{2,1,0:T(2,128)(2,1)}, u32[]{:S(2)}, u32[]{:S(2)}) collective-permute-start(bf16[64,1,1024]{2,1,0:T(2,128)(2,1)} %get-tuple-element.16), channel_id=1, source_target_pairs={{0,1},{1,2},{2,3},{3,4},{4,5},{5,6},{6,7},{7,8},{8,9},{9,10},{10,1... | collective-permute-start | bytes 393224 | tf_op jit(solution)/shard_map/ppermute | solution.py:21
  22.5 0.0 copy-start.4
  22.5 0.9 copy.18
  23.5 1.8 %rev.7 = bf16[27,64,128]{2,1,0:T(8,128)(2,1)} reverse(bf16[27,64,128]{2,1,0:T(8,128)(2,1)} %param.10), dimensions={0} | reverse | bytes 884736 | tf_op jit(solution)/shard_map/rev | solution.py:188
  25.3 0.8 copy.33
  26.0 1.3 copy.37
  27.4 1.3 rev.6
  28.7 0.0 collective-permute-done.7
  28.7 1.3 collective-permute-start.5
  30.0 0.9 copy.34
  30.9 0.0 collective-permute-done.6
  30.9 0.9 copy.32
  31.9 3.3 %convolution_multiply_fusion = f32[3,3,3,128,256]{4,3,2,1,0:T(8,128)S(1)} fusion(bf16[1,128,1,16,16]{1,0,4,3,2:T(2,128)(2,1)S(1)} %copy.34, bf16[1,128,1,16,16]{1,0,4,3,2:T(2,128)(2,1)} %copy.33, bf16[1,128,1,16,16]{1,0,4,3,2:T(2,128)(2,1)S(1)} %copy.32, bf16[1,256,1,16,16]{1,4,3,2,0:T(8,128)(2,1)S(1)} %bitcast.75), kind=kOutput, calls=%fused_computation.5 | convolution fusion | flops 417497088 | bytes 3866624 | tf_op jit(solution)/shard_map/transpose(jvp())/conv_general_dilated | solution.py:176
  35.2 0.0 copy-start.2
  35.2 1.5 %fusion.31 = (f32[3456,128]{1,0:T(8,128)S(1)}, f32[3456,128]{1,0:T(8,128)}) fusion(f32[3456,256]{1,0:T(8,128)S(1)} %bitcast.58), kind=kLoop, calls=%fused_computation.45 | loop fusion | bytes 7077888 | tf_op jit(solution)/shard_map/slice | solution.py:143
  36.7 1.3 copy.19
  38.0 1.2 copy.17
  39.2 1.8 %pad_maximum_fusion.2 = bf16[64,4,1024]{2,1,0:T(4,128)(2,1)S(1)} fusion(bf16[64,1,1024]{2,1,0:T(2,128)(2,1)S(1)} %collective-permute-done.5, bf16[64,2,1024]{2,1,0:T(2,128)(2,1)S(1)} %bitcast.60, bf16[64,1,1024]{2,1,0:T(2,128)(2,1)} %collective-permute-done.4), kind=kLoop, calls=%fused_computation.29 | loop fusion | flops 1572864 | bytes 1048576 | tf_op jit(solution)/shard_map/concatenate | solution.py:19
  41.0 1.0 copy.40
  42.0 3.4 %convolution_multiply_fusion.1 = f32[1,128,1,16,16]{1,0,4,3,2:T(1,128)S(1)} fusion(bf16[3,3,3,256,128]{3,4,2,1,0:T(8,128)(2,1)S(1)} %bitcast.70, bf16[1,256,1,16,16]{1,0,4,3,2:T(2,128)(2,1)S(1)} %copy.19, bf16[1,256,1,16,16]{1,0,4,3,2:T(2,128)(2,1)S(1)} %copy-done.8, bf16[1,256,1,16,16]{1,0,4,3,2:T(2,128)(2,1)S(1)} %copy.17), kind=kOutput, calls=%fused_computation.16 | convolution fusion | flops 417234944 | bytes 2293760 | tf_op jit(solution)/shard_map/conv_general_dilated | solution.py:176
  45.5 0.1 broadcast_in_dim.22
  45.6 0.2 copy.38
  45.8 0.1 broadcast_in_dim.23
  45.8 1.1 copy.23
  46.9 0.3 broadcast_in_dim.23.clone
  47.2 0.2 fusion.15
  47.4 0.8 fusion.32
  48.2 6.0 %collective-permute-start.2 = (bf16[128,1,1024]{0,2,1:T(8,128)(2,1)}, bf16[128,1,1024]{0,2,1:T(8,128)(2,1)}, u32[]{:S(2)}, u32[]{:S(2)}) collective-permute-start(bf16[128,1,1024]{0,2,1:T(8,128)(2,1)} %get-tuple-element.14), channel_id=1, source_target_pairs={{0,1},{1,2},{2,3},{3,4},{4,5},{5,6},{6,7},{7,8},{8,9},{9,10},{10,1... | collective-permute-start | bytes 786440 | tf_op jit(solution)/shard_map/ppermute | solution.py:21
  54.2 1.5 collective-permute-start.3
  55.7 1.5 %broadcast_in_dim.27 = f32[128,2,32,16,2]{0,4,3,2,1:T(2,128)} broadcast(f32[128,32,16]{0,2,1:T(8,128)S(1)} %copy.38), dimensions={0,2,3} | broadcast | bytes 1310720 | tf_op jit(solution)/shard_map/broadcast_in_dim | solution.py:260
  57.2 2.5 %copy.31 = f32[128,2048]{1,0:T(8,128)} copy(f32[128,2048]{0,1:T(8,128)} %bitcast.55) | data formatting | bytes 2097152 | tf_op jit(solution)/shard_map/mul | solution.py:260
  59.7 2.5 %multiply_convert_fusion.up_ref = bf16[128,2048]{1,0:T(8,128)(2,1)} fusion(f32[128,2048]{1,0:T(8,128)} %copy.31, f32[128,2048]{1,0:T(8,128)} %copy.37), kind=kLoop, calls=%fused_computation.21 | loop fusion | flops 524288 | bytes 2621440 | tf_op jit(solution)/shard_map/convert_element_type | solution.py:262
  62.2 7.1 %shard_map.85 = f32[27,64,128]{2,1,0:T(8,128)} custom-call(bf16[64,4096]{1,0:T(8,128)(2,1)} %bitcast.68, bf16[128,2048]{1,0:T(8,128)(2,1)} %multiply_convert_fusion.up_ref), custom_call_target="tpu_custom_call" | custom-call | tf_op jit(solution)/shard_map/pallas_call | solution.py:225
  69.3 1.4 broadcast_multiply_fusion
  70.7 0.3 copy-done
  71.0 5.6 %select_maximum_fusion.x_ref = f32[9216,128]{1,0:T(8,128)} fusion(f32[3456,128]{1,0:T(8,128)S(1)} %copy-done, f32[3456,128]{1,0:T(8,128)S(1)} %get-tuple-element.10, f32[1728,128]{1,0:T(8,128)S(1)} %bitcast.56), kind=kLoop, calls=%fused_computation | loop fusion | flops 7077888 | bytes 9142272 | tf_op jit(solution)/shard_map/concatenate | solution.py:143
  76.6 55.3 %shard_map.86 = (f32[1728,128]{1,0:T(8,128)}, f32[3456,256]{1,0:T(8,128)}) custom-call(f32[9216,128]{1,0:T(8,128)} %select_maximum_fusion.x_ref), custom_call_target="tpu_custom_call" | custom-call | tf_op jit(solution)/shard_map/pallas_call | solution.py:152
  132.0 0.2 multiply_convert_fusion.1
  132.2 1.2 maximum_bitcast_fusion
  133.3 0.4 copy.39
  133.8 0.2 pad.5.clone
  134.0 0.0 copy-start.9
  134.0 0.5 copy.26
  134.5 0.1 slice.28
  134.7 0.3 copy-done.7
  135.0 4.7 %fusion.11 = bf16[2,32,8,5,64]{4,2,3,1,0:T(8,128)(2,1)S(1)} fusion(bf16[3,3,3,128,64]{3,4,2,1,0:T(8,128)(2,1)S(1)} %bitcast.76, bf16[128,4,32,1,7,2]{0,4,5,2,1,3:T(8,128)(2,1)S(1)} %slice.28, bf16[128,4,32,1,8,5]{0,4,5,2,1,3:T(8,128)(2,1)S(1)} %copy.26, pred[8,5]{0,1:T(8,128)(4,1)S(1)} %copy-done.9), kind=kOutput, calls=%fused_computation.14 | convolution fusion | flops 1114701824 | bytes 2539560 | tf_op jit(solution)/shard_map/conv_general_dilated | solution.py:176
  139.8 0.1 copy.27
  139.9 0.2 copy.28
  140.1 1.0 copy.36
  141.1 0.9 copy.45
  142.0 4.2 %copy.46 = f32[27,128,256]{2,1,0:T(8,128)} copy(f32[27,128,256]{2,1,0:T(8,128)} %bitcast.57) | data formatting | bytes 7077888
  (23 shorter events, 0.1 us)
Async XLA Ops:
  2.7 15.6 %copy-start.1 = (bf16[1,64,2,1024]{3,2,1,0:T(2,128)(2,1)S(1)}, bf16[1,64,2,1024]{3,2,1,0:T(2,128)(2,1)}, u32[]{:S(2)}) copy-start(bf16[1,64,2,1024]{3,2,1,0:T(2,128)(2,1)} %param.6) | copy-start | bytes 786436
  2.7 33.9 %collective-permute-start.1 = (bf16[256,1,256]{0,2,1:T(8,128)(2,1)S(1)}, bf16[256,1,256]{0,2,1:T(8,128)(2,1)}, u32[]{:S(2)}, u32[]{:S(2)}) collective-permute-start(bf16[256,1,256]{0,2,1:T(8,128)(2,1)S(1)} %bitcast.72), channel_id=1, source_target_pairs={{1,0},{2,1},{3,2},{4,3},{5,4},{6,5},{7,6},{8,7},{9,8},{10,9},{11,1... | collective-permute-start | bytes 393224 | tf_op jit(solution)/shard_map/ppermute | solution.py:23
  4.2 33.8 %collective-permute-start = (bf16[256,1,256]{0,2,1:T(8,128)(2,1)S(1)}, bf16[256,1,256]{0,2,1:T(8,128)(2,1)}, u32[]{:S(2)}, u32[]{:S(2)}) collective-permute-start(bf16[256,1,256]{0,2,1:T(8,128)(2,1)S(1)} %bitcast.73), channel_id=1, source_target_pairs={{0,1},{1,2},{2,3},{3,4},{4,5},{5,6},{6,7},{7,8},{8,9},{9,10},{10,1... | collective-permute-start | bytes 393224 | tf_op jit(solution)/shard_map/ppermute | solution.py:21
  12.4 16.3 %collective-permute-start.7 = (bf16[128,1,256]{0,2,1:T(8,128)(2,1)}, bf16[128,1,256]{0,2,1:T(8,128)(2,1)}, u32[]{:S(2)}, u32[]{:S(2)}) collective-permute-start(bf16[128,1,256]{0,2,1:T(8,128)(2,1)} %bitcast.27), channel_id=1, source_target_pairs={{1,0},{2,1},{3,2},{4,3},{5,4},{6,5},{7,6},{8,7},{9,8},{10,9},{11,1... | collective-permute-start | bytes 196616 | tf_op jit(solution)/shard_map/ppermute | solution.py:23
  13.7 17.2 %collective-permute-start.6 = (bf16[128,1,256]{0,2,1:T(8,128)(2,1)}, bf16[128,1,256]{0,2,1:T(8,128)(2,1)}, u32[]{:S(2)}, u32[]{:S(2)}) collective-permute-start(bf16[128,1,256]{0,2,1:T(8,128)(2,1)} %bitcast.27), channel_id=1, source_target_pairs={{0,1},{1,2},{2,3},{3,4},{4,5},{5,6},{6,7},{7,8},{8,9},{9,10},{10,1... | collective-permute-start | bytes 196616 | tf_op jit(solution)/shard_map/ppermute | solution.py:21
  19.5 19.7 %collective-permute-start.4 = (bf16[64,1,1024]{2,1,0:T(2,128)(2,1)}, bf16[64,1,1024]{2,1,0:T(2,128)(2,1)}, u32[]{:S(2)}, u32[]{:S(2)}) collective-permute-start(bf16[64,1,1024]{2,1,0:T(2,128)(2,1)} %get-tuple-element.16), channel_id=1, source_target_pairs={{0,1},{1,2},{2,3},{3,4},{4,5},{5,6},{6,7},{7,8},{8,9},{9,10},{10,1... | collective-permute-start | bytes 393224 | tf_op jit(solution)/shard_map/ppermute | solution.py:21
  22.5 4.8 %copy-start.4 = (bf16[27,128,256]{2,1,0:T(8,128)(2,1)S(1)}, bf16[27,128,256]{2,1,0:T(8,128)(2,1)}, u32[]{:S(2)}) copy-start(bf16[27,128,256]{2,1,0:T(8,128)(2,1)} %param.11) | copy-start | bytes 5308420
  28.7 10.5 %collective-permute-start.5 = (bf16[64,1,1024]{2,1,0:T(2,128)(2,1)}, bf16[64,1,1024]{2,1,0:T(2,128)(2,1)S(1)}, u32[]{:S(2)}, u32[]{:S(2)}) collective-permute-start(bf16[64,1,1024]{2,1,0:T(2,128)(2,1)} %get-tuple-element.17), channel_id=1, source_target_pairs={{1,0},{2,1},{3,2},{4,3},{5,4},{6,5},{7,6},{8,7},{9,8},{10,9},{11,1... | collective-permute-start | bytes 393224 | tf_op jit(solution)/shard_map/ppermute | solution.py:23
  35.2 4.0 %copy-start.2 = (bf16[1,64,2,1024]{3,2,1,0:T(2,128)(2,1)S(1)}, bf16[1,64,2,1024]{3,2,1,0:T(2,128)(2,1)}, u32[]{:S(2)}) copy-start(bf16[1,64,2,1024]{3,2,1,0:T(2,128)(2,1)} %param.6) | copy-start | bytes 786436
  36.6 5.3 %copy-start.5 = (bf16[27,128,256]{2,1,0:T(8,128)(2,1)S(1)}, bf16[27,128,256]{2,1,0:T(8,128)(2,1)}, u32[]{:S(2)}) copy-start(bf16[27,128,256]{2,1,0:T(8,128)(2,1)} %rev.6) | copy-start | bytes 5308420
  36.6 5.3 %copy-start.8 = (bf16[1,256,1,16,16]{1,0,4,3,2:T(2,128)(2,1)S(1)}, bf16[1,256,1,16,16]{1,0,4,3,2:T(2,128)(2,1)}, u32[]{:S(2)}) copy-start(bf16[1,256,1,16,16]{1,0,4,3,2:T(2,128)(2,1)} %copy.18) | copy-start | bytes 393220
  48.2 83.9 %collective-permute-start.2 = (bf16[128,1,1024]{0,2,1:T(8,128)(2,1)}, bf16[128,1,1024]{0,2,1:T(8,128)(2,1)}, u32[]{:S(2)}, u32[]{:S(2)}) collective-permute-start(bf16[128,1,1024]{0,2,1:T(8,128)(2,1)} %get-tuple-element.14), channel_id=1, source_target_pairs={{0,1},{1,2},{2,3},{3,4},{4,5},{5,6},{6,7},{7,8},{8,9},{9,10},{10,1... | collective-permute-start | bytes 786440 | tf_op jit(solution)/shard_map/ppermute | solution.py:21
  54.2 78.0 %collective-permute-start.3 = (bf16[128,1,1024]{0,2,1:T(8,128)(2,1)}, bf16[128,1,1024]{0,2,1:T(8,128)(2,1)}, u32[]{:S(2)}, u32[]{:S(2)}) collective-permute-start(bf16[128,1,1024]{0,2,1:T(8,128)(2,1)} %get-tuple-element.15), channel_id=1, source_target_pairs={{1,0},{2,1},{3,2},{4,3},{5,4},{6,5},{7,6},{8,7},{9,8},{10,9},{11,1... | collective-permute-start | bytes 786440 | tf_op jit(solution)/shard_map/ppermute | solution.py:23
  69.3 1.7 %copy-start = (f32[3456,128]{1,0:T(8,128)S(1)}, f32[3456,128]{1,0:T(8,128)}, u32[]{:S(2)}) copy-start(f32[3456,128]{1,0:T(8,128)} %get-tuple-element.11) | copy-start | bytes 5308420
  76.6 55.3 %copy-start.3 = (f32[128,32,32]{0,2,1:T(8,128)S(1)}, f32[128,32,32]{0,2,1:T(8,128)}, u32[]{:S(2)}) copy-start(f32[128,32,32]{0,2,1:T(8,128)} %copy.23) | copy-start | bytes 1572868
  134.0 1.0 copy-start.7
  134.0 1.0 copy-start.9
  139.7 1.3 copy-start.6

commit v8 on v7

--- a/solution.py
+++ b/solution.py
@@ -230,6 +230,39 @@
     )(source_pad.reshape(chan_in, -1), grad_hidden.reshape(chan_out, -1))
 
 
+def _back_a_body(pad_ref, w_ref, back_ref):
+    cells = back_ref.shape[1]
+    plane = pad_ref.shape[1] // 4
+    side = 32
+    spot = lax.broadcasted_iota(jnp.int32, (1, cells), 1)
+    column = spot % side
+    row = (spot // side) % side
+    back = jnp.zeros((back_ref.shape[0], cells), jnp.float32)
+    for b in range(3):
+        for c in range(3):
+            shift = (b - 1) * side + (c - 1)
+            total = jnp.zeros_like(back)
+            for a in range(3):
+                total = total + jnp.dot(
+                    w_ref[9 * a + 3 * b + c],
+                    pad_ref[:, (2 - a) * plane : (2 - a) * plane + cells],
+                    preferred_element_type=jnp.float32,
+                )
+            back_in = (column - c + 1 >= 0) & (column - c + 1 < side) & (row - b + 1 >= 0) & (row - b + 1 < side)
+            back = back + jnp.where(back_in, pltpu.roll(total, shift % cells, 1), 0.0)
+    back_ref[...] = back.astype(back_ref.dtype)
+
+
+def back_flat(hidden_pad, weight_a, cells):
+    chan_in, chan_out = weight_a.shape[1], hidden_pad.shape[0]
+    return pl.pallas_call(
+        _back_a_body,
+        out_shape=jax.ShapeDtypeStruct((chan_in, cells), jnp.bfloat16),
+        in_specs=[pl.BlockSpec(memory_space=pltpu.VMEM)] * 2,
+        out_specs=pl.BlockSpec(memory_space=pltpu.VMEM),
+    )(hidden_pad.reshape(chan_out, -1), weight_a)
+
+
 def per_device(layer_input, hidden_pre, output_pre, output_grad, weight_a, weight_b):
     side = math.isqrt(layer_input.shape[3])
     half = side // 2
@@ -263,9 +296,9 @@
         jnp.bfloat16
     )
     grad_hidden = grad_hidden.reshape(width_a, depth_a, side * side)
-    hidden_pad = padded_2(grad_hidden, (("space", 1),), 1).reshape(width_a, depth_a + 2, side, side)
+    hidden_pad = padded_2(grad_hidden, (("space", 1),), 1)
+    back_a = back_flat(hidden_pad, weight_a, depth_a * side * side)
     source_pad = padded_2(source, (("space", 1),), 1)
-    back_a = back_cells(hidden_pad, weight_a)
     sums_a = kernel_terms_flat(source_pad, grad_hidden)
     input_grad = back_a.astype(jnp.bfloat16).reshape(1, chan_in, depth_a, side * side)
     samples = lax.axis_size("dp")

time: 147 us -> 139 us (0.946)
  local copies, waits for them, and re-layouts: 32.5 us -> 23.8 us
  matrix products: 11.4 us -> 5.77 us
  waiting for transfers between devices: 0.02 us -> 4.09 us
  other arithmetic: 14.1 us -> 16.2 us
  Pallas kernels: 62.5 us -> 64.6 us
  starting transfers between devices: 24.7 us -> 23.1 us
    conv_general_dilated x3 -> x2, matrix products: 11.4 us -> 5.77 us  [conv_cells(): lax.conv_general_dilated(field[None], shaped, (1, 1, 1), ((0, 0), (1, 1),...]
    pallas_call x0 -> x1, Pallas kernels: none -> 4.6 us  [back_flat(): pl.pallas_call(_back_a_body, out_shape=jax.ShapeDtypeStruct((chan_in, cel...]
    ppermute x4, waiting for transfers between devices: 0.01 us -> 4.08 us  [padded_2(): lax.ppermute(head, axis, [((i + 1) % count, i) for i in range(ends)])]
    concatenate x5 -> x4, local copies, waits for them, and re-layouts: 4.56 us -> 0.71 us  [padded_2(): jnp.concatenate([lax.ppermute(tail, axis, [(i, (i + 1) % count) for i in...]
    select_n x0 -> x1, other arithmetic: none -> 2.93 us  [slopes(): jnp.where(values > 0, jnp.ones_like(values), negative_slope * jnp.ones_li...]
    pallas_call x1, Pallas kernels: 55.3 us -> 52.6 us  [all_reduce(): pl.pallas_call(_all_reduce_kernel, out_shape=(jax.ShapeDtypeStruct((rows_...]
    mul x3 -> x2, local copies, waits for them, and re-layouts: 3.69 us -> 1.51 us  [per_device(): jnp.repeat(jnp.repeat(jnp.repeat(back_b, 2, 1), 2, 2), 2, 3) * 0.125]
    reshape x0 -> x1, local copies, waits for them, and re-layouts: none -> 1.85 us  [per_device(): back_a.astype(jnp.bfloat16).reshape(1, chan_in, depth_a, side * side)]
  transfers between devices with their start and end apart: 8 -> 8, of which waited for: 0 -> 1; matrix products, arithmetic and copies ran while one was open for 22% -> 14% of each run, Pallas kernels for 43% -> 38%
where the time goes in v8:
time: 139 us
  Pallas kernels  64.6 us (46%)
  local copies, waits for them, and re-layouts  23.8 us (17%)
  starting transfers between devices  23.1 us (17%)
  other arithmetic  16.2 us (12%)
  matrix products  5.77 us (4%)
  waiting for transfers between devices  4.09 us (3%)
    pallas_call x1, Pallas kernels, all_reduce(): pl.pallas_call(_all_reduce_kernel, out_shape=(jax.ShapeDtypeStruct((rows_...  52.6 us
    ppermute x4, starting transfers between devices, padded_2(): lax.ppermute(tail, axis, [(i, (i + 1) % count) for i in range(ends)])  17.8 us
    unnamed x21, local copies, waits for them, and re-layouts  10.4 us
    pallas_call x1, Pallas kernels, kernel_terms_flat(): pl.pallas_call(_terms_a_body, out_shape=jax.ShapeDtypeStruct((27, chan_in...  7.34 us
    conv_general_dilated x2, matrix products, conv_cells(): lax.conv_general_dilated(field[None], shaped, (1, 1, 1), ((0, 0), (1, 1),...  5.77 us
    concatenate x1, other arithmetic, all_reduce(): jnp.concatenate([sums_a.reshape(rows_a, 128) * scale_a, wide[:, :128], wi...  5.63 us
    ppermute x4, starting transfers between devices, padded_2(): lax.ppermute(head, axis, [((i + 1) % count, i) for i in range(ends)])  5.34 us
    pallas_call x1, Pallas kernels, back_flat(): pl.pallas_call(_back_a_body, out_shape=jax.ShapeDtypeStruct((chan_in, cel...  4.6 us
  transfers between devices with their start and end apart: 8, of which 1 were waited for; matrix products, arithmetic and copies ran while one was open for 14% of the time, Pallas kernels for 38%

profile of v8, /device:TPU:1, one launch (start us, length us, event | category | flops | bytes accessed | tf_op | source)
XLA Modules:
  0.0 138.6 jit_solution(7199225663303959044)
XLA Ops:
  0.6 0.0 copy-start.3
  0.6 1.0 copy.25
  1.7 1.0 copy.24
  2.7 0.1 multiply_convert_fusion.1
  2.8 1.3 collective-permute-start.1
  4.1 5.0 %collective-permute-start = (bf16[256,1,256]{0,2,1:T(8,128)(2,1)S(1)}, bf16[256,1,256]{0,2,1:T(8,128)(2,1)S(1)}, u32[]{:S(2)}, u32[]{:S(2)}) collective-permute-start(bf16[256,1,256]{0,2,1:T(8,128)(2,1)S(1)} %bitcast.53), channel_id=1, source_target_pairs={{0,1},{1,2},{2,3},{3,4},{4,5},{5,6},{6,7},{7,8},{8,9},{9,10},{10,1... | collective-permute-start | bytes 393224 | tf_op jit(solution)/shard_map/ppermute | solution.py:21
  9.1 2.9 %compare_select_fusion.1 = (f32[1,128,2,1024]{3,2,1,0:T(2,128)S(1)}, f32[128,1024]{1,0:T(8,128)S(1)}) fusion(bf16[1,128,2,1024]{3,2,1,0:T(2,128)(2,1)} %param.7), kind=kLoop, calls=%fused_computation.4 | loop fusion | flops 1441792 | bytes 2097152 | tf_op jit(solution)/shard_map/jit(_where)/select_n | solution.py:31
  12.0 0.2 copy.31
  12.2 0.4 reduce_sum.18
  12.6 1.3 collective-permute-start.7
  13.9 4.2 %collective-permute-start.6 = (bf16[128,1,256]{0,2,1:T(8,128)(2,1)S(1)}, bf16[128,1,256]{0,2,1:T(8,128)(2,1)S(1)}, u32[]{:S(2)}, u32[]{:S(2)}) collective-permute-start(bf16[128,1,256]{0,2,1:T(8,128)(2,1)S(1)} %bitcast.60), channel_id=1, source_target_pairs={{0,1},{1,2},{2,3},{3,4},{4,5},{5,6},{6,7},{7,8},{8,9},{9,10},{10,1... | collective-permute-start | bytes 196616 | tf_op jit(solution)/shard_map/ppermute | solution.py:21
  18.1 0.0 copy-done.3
  18.1 0.4 fusion.15
  18.5 3.4 %collective-permute-start.4 = (bf16[64,1,1024]{2,1,0:T(2,128)(2,1)S(1)}, bf16[64,1,1024]{2,1,0:T(2,128)(2,1)S(1)}, u32[]{:S(2)}, u32[]{:S(2)}) collective-permute-start(bf16[64,1,1024]{2,1,0:T(2,128)(2,1)S(1)} %get-tuple-element.13), channel_id=1, source_target_pairs={{0,1},{1,2},{2,3},{3,4},{4,5},{5,6},{6,7},{7,8},{8,9},{9,10},{10,1... | collective-permute-start | bytes 393224 | tf_op jit(solution)/shard_map/ppermute | solution.py:21
  21.9 0.9 copy.27
  22.8 1.3 copy.38
  24.1 0.1 copy.33
  24.2 2.9 %rev.3 = bf16[27,128,256]{2,1,0:T(8,128)(2,1)} reverse(bf16[27,128,256]{2,1,0:T(8,128)(2,1)} %param.11), dimensions={0} | reverse | bytes 3538944 | tf_op jit(solution)/shard_map/rev | solution.py:188
  27.1 0.0 collective-permute-done.7
  27.1 1.5 %collective-permute-start.5 = (bf16[64,1,1024]{2,1,0:T(2,128)(2,1)S(1)}, bf16[64,1,1024]{2,1,0:T(2,128)(2,1)S(1)}, u32[]{:S(2)}, u32[]{:S(2)}) collective-permute-start(bf16[64,1,1024]{2,1,0:T(2,128)(2,1)S(1)} %get-tuple-element.14), channel_id=1, source_target_pairs={{1,0},{2,1},{3,2},{4,3},{5,4},{6,5},{7,6},{8,7},{9,8},{10,9},{11,1... | collective-permute-start | bytes 393224 | tf_op jit(solution)/shard_map/ppermute | solution.py:23
  28.6 0.1 copy.34
  28.7 0.0 collective-permute-done.6
  28.7 0.1 copy.32
  28.8 2.3 %convolution_multiply_fusion = f32[3,3,3,128,256]{4,3,2,1,0:T(8,128)S(1)} fusion(bf16[1,128,1,16,16]{1,0,4,3,2:T(2,128)(2,1)S(1)} %copy.34, bf16[1,128,1,16,16]{1,0,4,3,2:T(2,128)(2,1)S(1)} %copy.33, bf16[1,128,1,16,16]{1,0,4,3,2:T(2,128)(2,1)S(1)} %copy.32, bf16[1,256,1,16,16]{1,4,3,2,0:T(8,128)(2,1)S(1)} %bitcast.55), kind=kOutput, calls=%fused_computation.5 | convolution fusion | flops 417497088 | bytes 3866624 | tf_op jit(solution)/shard_map/transpose(jvp())/conv_general_dilated | solution.py:176
  31.2 0.0 copy-start.5
  31.2 0.0 copy-start.6
  31.2 1.5 %fusion.13 = (f32[3456,128]{1,0:T(8,128)S(1)}, f32[3456,128]{1,0:T(8,128)}) fusion(f32[3456,256]{1,0:T(8,128)S(1)} %bitcast.41), kind=kLoop, calls=%fused_computation.29 | loop fusion | bytes 7077888 | tf_op jit(solution)/shard_map/slice | solution.py:143
  32.7 0.0 collective-permute-done.1
  32.7 0.3 copy.28
  32.9 0.0 collective-permute-done
  32.9 0.3 copy.26
  33.2 0.0 collective-permute-done.4
  33.2 4.1 %collective-permute-done.5 = bf16[64,1,1024]{2,1,0:T(2,128)(2,1)S(1)} collective-permute-done((bf16[64,1,1024]{2,1,0:T(2,128)(2,1)S(1)}, bf16[64,1,1024]{2,1,0:T(2,128)(2,1)S(1)}, u32[]{:S(2)}, u32[]{:S(2)}) %collective-permute-start.5) | collective-permute-done | bytes 131104 | tf_op jit(solution)/shard_map/ppermute | solution.py:23
  37.3 0.9 pad_maximum_fusion.3
  38.2 1.0 copy.37
  39.1 0.0 copy-done.5
  39.1 0.0 copy-done.6
  39.1 3.4 %convolution_multiply_fusion.1 = f32[1,128,1,16,16]{1,0,4,3,2:T(1,128)S(1)} fusion(bf16[3,3,3,256,128]{3,4,2,1,0:T(8,128)(2,1)S(1)} %bitcast.50, bf16[1,256,1,16,16]{1,0,4,3,2:T(2,128)(2,1)S(1)} %copy.28, bf16[1,256,1,16,16]{1,0,4,3,2:T(2,128)(2,1)S(1)} %copy-done.6, bf16[1,256,1,16,16]{1,0,4,3,2:T(2,128)(2,1)S(1)} %copy.26), kind=kOutput, calls=%fused_computation.6 | convolution fusion | flops 417234944 | bytes 2293760 | tf_op jit(solution)/shard_map/conv_general_dilated | solution.py:176
  42.6 0.0 copy-start.2
  42.6 0.7 copy-done.2
  43.3 0.3 broadcast_in_dim.21
  43.6 0.2 copy.29
  43.8 0.0 copy-done.4
  43.8 0.7 fusion.1
  44.5 1.5 %broadcast_in_dim.24 = f32[128,2,32,16,2]{0,4,3,2,1:T(2,128)S(1)} broadcast(f32[128,32,16]{0,2,1:T(8,128)} %bitcast.43), dimensions={0,2,3} | broadcast | bytes 1310720 | tf_op jit(solution)/shard_map/broadcast_in_dim | solution.py:293
  46.0 1.3 copy.30
  47.3 2.5 %multiply_convert_fusion.up_ref = bf16[128,2048]{1,0:T(8,128)(2,1)} fusion(f32[128,2048]{1,0:T(8,128)} %copy.30, f32[128,2048]{1,0:T(8,128)} %bitcast.35), kind=kLoop, calls=%fused_computation.11 | loop fusion | flops 524288 | bytes 2621440 | tf_op jit(solution)/shard_map/convert_element_type | solution.py:295
  49.8 7.3 %shard_map.86 = f32[27,64,128]{2,1,0:T(8,128)} custom-call(bf16[64,4096]{1,0:T(8,128)(2,1)} %bitcast.49, bf16[128,2048]{1,0:T(8,128)(2,1)} %multiply_convert_fusion.up_ref), custom_call_target="tpu_custom_call" | custom-call | tf_op jit(solution)/shard_map/pallas_call | solution.py:225
  57.1 1.4 %broadcast_multiply_fusion = f32[27,64,128]{2,1,0:T(8,128)S(1)} fusion(f32[27,64,128]{2,1,0:T(8,128)} %shard_map.86), kind=kLoop, calls=%fused_computation.17 | loop fusion | flops 221184 | bytes 1769472 | tf_op jit(solution)/shard_map/mul | solution.py:143
  58.5 1.7 %fusion.14 = (bf16[128,1,1024]{2,1,0:T(2,128)(2,1)}, bf16[128,1,1024]{2,1,0:T(2,128)(2,1)}) fusion(bf16[128,2,1024]{2,1,0:T(2,128)(2,1)S(1)} %fusion.1), kind=kLoop, calls=%fused_computation.30 | loop fusion | bytes 1048576 | tf_op jit(solution)/shard_map/slice | solution.py:18
  60.2 5.2 %collective-permute-start.2 = (bf16[128,1,1024]{2,1,0:T(2,128)(2,1)}, bf16[128,1,1024]{2,1,0:T(2,128)(2,1)S(1)}, u32[]{:S(2)}, u32[]{:S(2)}) collective-permute-start(bf16[128,1,1024]{2,1,0:T(2,128)(2,1)} %get-tuple-element.11), channel_id=1, source_target_pairs={{0,1},{1,2},{2,3},{3,4},{4,5},{5,6},{6,7},{7,8},{8,9},{9,10},{10,1... | collective-permute-start | bytes 786440 | tf_op jit(solution)/shard_map/ppermute | solution.py:21
  65.4 1.3 collective-permute-start.3
  66.7 0.0 copy-done
  66.7 5.6 %select_maximum_fusion.x_ref = f32[9216,128]{1,0:T(8,128)} fusion(f32[3456,128]{1,0:T(8,128)S(1)} %copy-done, f32[3456,128]{1,0:T(8,128)S(1)} %get-tuple-element.7, f32[1728,128]{1,0:T(8,128)S(1)} %bitcast.39), kind=kLoop, calls=%fused_computation | loop fusion | flops 7077888 | bytes 9142272 | tf_op jit(solution)/shard_map/concatenate | solution.py:143
  72.4 52.6 %shard_map.87 = (f32[1728,128]{1,0:T(8,128)}, f32[3456,256]{1,0:T(8,128)}) custom-call(f32[9216,128]{1,0:T(8,128)} %select_maximum_fusion.x_ref), custom_call_target="tpu_custom_call" | custom-call | tf_op jit(solution)/shard_map/pallas_call | solution.py:152
  125.0 0.0 collective-permute-done.2
  125.0 0.0 collective-permute-done.3
  125.0 1.8 %pad_maximum_fusion = bf16[128,4,1024]{2,1,0:T(4,128)(2,1)S(1)} fusion(bf16[128,1,1024]{2,1,0:T(2,128)(2,1)S(1)} %collective-permute-done.3, bf16[128,2,1024]{2,1,0:T(2,128)(2,1)S(1)} %fusion.1, bf16[128,1,1024]{2,1,0:T(2,128)(2,1)S(1)} %collective-permute-done.2), kind=kLoop, calls=%fused_computation.8 | loop fusion | flops 3145728 | bytes 2097152 | tf_op jit(solution)/shard_map/concatenate | solution.py:19
  126.8 0.0 copy-start.1
  126.8 1.3 copy.36
  128.1 4.6 %shard_map.85 = bf16[64,2048]{1,0:T(8,128)(2,1)} custom-call(bf16[128,4096]{1,0:T(8,128)(2,1)} %bitcast.38, bf16[27,64,128]{2,1,0:T(8,128)(2,1)} %w_ref.1), custom_call_target="tpu_custom_call" | custom-call | tf_op jit(solution)/shard_map/pallas_call | solution.py:258
  132.8 1.8 %reshape.211 = bf16[1,64,2,1024]{3,2,1,0:T(2,128)(2,1)} reshape(bf16[64,2048]{1,0:T(8,128)(2,1)} %shard_map.85) | data formatting | bytes 524288 | tf_op jit(solution)/shard_map/reshape | solution.py:303
  134.6 2.2 %copy.43 = f32[27,64,128]{2,1,0:T(8,128)} copy(f32[27,64,128]{2,1,0:T(8,128)} %bitcast.51) | data formatting | bytes 1769472
  136.8 1.8 %copy.44 = f32[27,128,256]{2,1,0:T(8,128)} copy(f32[27,128,256]{2,1,0:T(8,128)S(1)} %bitcast.40) | data formatting | bytes 7077888
  (6 shorter events, 0.1 us)
Async XLA Ops:
  0.6 17.5 %copy-start.3 = (bf16[1,64,2,1024]{3,2,1,0:T(2,128)(2,1)S(1)}, bf16[1,64,2,1024]{3,2,1,0:T(2,128)(2,1)}, u32[]{:S(2)}) copy-start(bf16[1,64,2,1024]{3,2,1,0:T(2,128)(2,1)} %param.6) | copy-start | bytes 786436
  2.8 29.9 %collective-permute-start.1 = (bf16[256,1,256]{0,2,1:T(8,128)(2,1)S(1)}, bf16[256,1,256]{0,2,1:T(8,128)(2,1)S(1)}, u32[]{:S(2)}, u32[]{:S(2)}) collective-permute-start(bf16[256,1,256]{0,2,1:T(8,128)(2,1)S(1)} %bitcast.52), channel_id=1, source_target_pairs={{1,0},{2,1},{3,2},{4,3},{5,4},{6,5},{7,6},{8,7},{9,8},{10,9},{11,1... | collective-permute-start | bytes 393224 | tf_op jit(solution)/shard_map/ppermute | solution.py:23
  4.1 28.9 %collective-permute-start = (bf16[256,1,256]{0,2,1:T(8,128)(2,1)S(1)}, bf16[256,1,256]{0,2,1:T(8,128)(2,1)S(1)}, u32[]{:S(2)}, u32[]{:S(2)}) collective-permute-start(bf16[256,1,256]{0,2,1:T(8,128)(2,1)S(1)} %bitcast.53), channel_id=1, source_target_pairs={{0,1},{1,2},{2,3},{3,4},{4,5},{5,6},{6,7},{7,8},{8,9},{9,10},{10,1... | collective-permute-start | bytes 393224 | tf_op jit(solution)/shard_map/ppermute | solution.py:21
  12.6 14.5 %collective-permute-start.7 = (bf16[128,1,256]{0,2,1:T(8,128)(2,1)S(1)}, bf16[128,1,256]{0,2,1:T(8,128)(2,1)S(1)}, u32[]{:S(2)}, u32[]{:S(2)}) collective-permute-start(bf16[128,1,256]{0,2,1:T(8,128)(2,1)S(1)} %bitcast.59), channel_id=1, source_target_pairs={{1,0},{2,1},{3,2},{4,3},{5,4},{6,5},{7,6},{8,7},{9,8},{10,9},{11,1... | collective-permute-start | bytes 196616 | tf_op jit(solution)/shard_map/ppermute | solution.py:23
  13.9 14.8 %collective-permute-start.6 = (bf16[128,1,256]{0,2,1:T(8,128)(2,1)S(1)}, bf16[128,1,256]{0,2,1:T(8,128)(2,1)S(1)}, u32[]{:S(2)}, u32[]{:S(2)}) collective-permute-start(bf16[128,1,256]{0,2,1:T(8,128)(2,1)S(1)} %bitcast.60), channel_id=1, source_target_pairs={{0,1},{1,2},{2,3},{3,4},{4,5},{5,6},{6,7},{7,8},{8,9},{9,10},{10,1... | collective-permute-start | bytes 196616 | tf_op jit(solution)/shard_map/ppermute | solution.py:21
  18.5 14.7 %collective-permute-start.4 = (bf16[64,1,1024]{2,1,0:T(2,128)(2,1)S(1)}, bf16[64,1,1024]{2,1,0:T(2,128)(2,1)S(1)}, u32[]{:S(2)}, u32[]{:S(2)}) collective-permute-start(bf16[64,1,1024]{2,1,0:T(2,128)(2,1)S(1)} %get-tuple-element.13), channel_id=1, source_target_pairs={{0,1},{1,2},{2,3},{3,4},{4,5},{5,6},{6,7},{7,8},{8,9},{9,10},{10,1... | collective-permute-start | bytes 393224 | tf_op jit(solution)/shard_map/ppermute | solution.py:21
  27.1 10.1 %collective-permute-start.5 = (bf16[64,1,1024]{2,1,0:T(2,128)(2,1)S(1)}, bf16[64,1,1024]{2,1,0:T(2,128)(2,1)S(1)}, u32[]{:S(2)}, u32[]{:S(2)}) collective-permute-start(bf16[64,1,1024]{2,1,0:T(2,128)(2,1)S(1)} %get-tuple-element.14), channel_id=1, source_target_pairs={{1,0},{2,1},{3,2},{4,3},{5,4},{6,5},{7,6},{8,7},{9,8},{10,9},{11,1... | collective-permute-start | bytes 393224 | tf_op jit(solution)/shard_map/ppermute | solution.py:23
  31.2 8.0 %copy-start.5 = (bf16[27,128,256]{2,1,0:T(8,128)(2,1)S(1)}, bf16[27,128,256]{2,1,0:T(8,128)(2,1)}, u32[]{:S(2)}) copy-start(bf16[27,128,256]{2,1,0:T(8,128)(2,1)} %rev.3) | copy-start | bytes 5308420
  31.2 8.0 %copy-start.6 = (bf16[1,256,1,16,16]{1,0,4,3,2:T(2,128)(2,1)S(1)}, bf16[1,256,1,16,16]{1,0,4,3,2:T(2,128)(2,1)}, u32[]{:S(2)}) copy-start(bf16[1,256,1,16,16]{1,0,4,3,2:T(2,128)(2,1)} %copy.27) | copy-start | bytes 393220
  39.1 4.7 %copy-start.4 = (bf16[1,128,2,1024]{3,2,1,0:T(2,128)(2,1)S(1)}, bf16[1,128,2,1024]{3,2,1,0:T(2,128)(2,1)}, u32[]{:S(2)}) copy-start(bf16[1,128,2,1024]{3,2,1,0:T(2,128)(2,1)} %param.7) | copy-start | bytes 1572868
  42.6 0.7 copy-start.2
  57.1 9.6 %copy-start = (f32[3456,128]{1,0:T(8,128)S(1)}, f32[3456,128]{1,0:T(8,128)}, u32[]{:S(2)}) copy-start(f32[3456,128]{1,0:T(8,128)} %get-tuple-element.8) | copy-start | bytes 5308420
  60.2 64.8 %collective-permute-start.2 = (bf16[128,1,1024]{2,1,0:T(2,128)(2,1)}, bf16[128,1,1024]{2,1,0:T(2,128)(2,1)S(1)}, u32[]{:S(2)}, u32[]{:S(2)}) collective-permute-start(bf16[128,1,1024]{2,1,0:T(2,128)(2,1)} %get-tuple-element.11), channel_id=1, source_target_pairs={{0,1},{1,2},{2,3},{3,4},{4,5},{5,6},{6,7},{7,8},{8,9},{9,10},{10,1... | collective-permute-start | bytes 786440 | tf_op jit(solution)/shard_map/ppermute | solution.py:21
  65.4 59.6 %collective-permute-start.3 = (bf16[128,1,1024]{2,1,0:T(2,128)(2,1)}, bf16[128,1,1024]{2,1,0:T(2,128)(2,1)S(1)}, u32[]{:S(2)}, u32[]{:S(2)}) collective-permute-start(bf16[128,1,1024]{2,1,0:T(2,128)(2,1)} %get-tuple-element.12), channel_id=1, source_target_pairs={{1,0},{2,1},{3,2},{4,3},{5,4},{6,5},{7,6},{8,7},{9,8},{10,9},{11,1... | collective-permute-start | bytes 786440 | tf_op jit(solution)/shard_map/ppermute | solution.py:23
  126.8 10.0 %copy-start.1 = (f32[3456,256]{1,0:T(8,128)S(1)}, f32[3456,256]{1,0:T(8,128)}, u32[]{:S(2)}) copy-start(f32[3456,256]{1,0:T(8,128)} %get-tuple-element.6) | copy-start | bytes 10616836

commit v9 on v8

--- a/solution.py
+++ b/solution.py
@@ -197,16 +197,16 @@
     return pull(upstream.astype(jnp.float32))[0]
 
 
-def _terms_a_body(src_ref, up_ref, terms_ref):
+def _terms_a_body(low_ref, mid_ref, high_ref, up_ref, terms_ref):
     cells = up_ref.shape[1]
-    width = src_ref.shape[1]
+    width = 2 * cells
     plane = width // 4
     side = 32
     spot = lax.broadcasted_iota(jnp.int32, (1, cells), 1)
     column = spot % side
     row = (spot // side) % side
     upstream = up_ref[...]
-    field = src_ref[...].astype(jnp.float32)
+    field = jnp.concatenate([low_ref[...], mid_ref[...], high_ref[...]], axis=1).astype(jnp.float32)
     for b in range(3):
         for c in range(3):
             shift = (b - 1) * side + (c - 1)
@@ -220,19 +220,30 @@
                 )
 
 
-def kernel_terms_flat(source_pad, grad_hidden):
-    chan_in, chan_out = source_pad.shape[0], grad_hidden.shape[0]
+def kernel_terms_flat(source, grad_hidden):
+    chan_in, chan_out = source.shape[0], grad_hidden.shape[0]
+    low, high = halo_planes(source)
     return pl.pallas_call(
         _terms_a_body,
         out_shape=jax.ShapeDtypeStruct((27, chan_in, chan_out), jnp.float32),
-        in_specs=[pl.BlockSpec(memory_space=pltpu.VMEM)] * 2,
+        in_specs=[pl.BlockSpec(memory_space=pltpu.VMEM)] * 4,
         out_specs=pl.BlockSpec(memory_space=pltpu.VMEM),
-    )(source_pad.reshape(chan_in, -1), grad_hidden.reshape(chan_out, -1))
-
-
-def _back_a_body(pad_ref, w_ref, back_ref):
+    )(low, source.reshape(chan_in, -1), high, grad_hidden.reshape(chan_out, -1))
+
+
+def halo_planes(cells):
+    count = lax.axis_size("space")
+    head = cells[:, 0]
+    tail = cells[:, -1]
+    low = lax.ppermute(tail, "space", [(i, i + 1) for i in range(count - 1)])
+    high = lax.ppermute(head, "space", [(i + 1, i) for i in range(count - 1)])
+    return low, high
+
+
+def _back_a_body(low_ref, mid_ref, high_ref, w_ref, back_ref):
     cells = back_ref.shape[1]
-    plane = pad_ref.shape[1] // 4
+    plane = cells // 2
+    padded = jnp.concatenate([low_ref[...], mid_ref[...], high_ref[...]], axis=1)
     side = 32
     spot = lax.broadcasted_iota(jnp.int32, (1, cells), 1)
     column = spot % side
@@ -245,7 +256,7 @@
             for a in range(3):
                 total = total + jnp.dot(
                     w_ref[9 * a + 3 * b + c],
-                    pad_ref[:, (2 - a) * plane : (2 - a) * plane + cells],
+                    padded[:, (2 - a) * plane : (2 - a) * plane + cells],
                     preferred_element_type=jnp.float32,
                 )
             back_in = (column - c + 1 >= 0) & (column - c + 1 < side) & (row - b + 1 >= 0) & (row - b + 1 < side)
@@ -253,14 +264,16 @@
     back_ref[...] = back.astype(back_ref.dtype)
 
 
-def back_flat(hidden_pad, weight_a, cells):
-    chan_in, chan_out = weight_a.shape[1], hidden_pad.shape[0]
+def back_flat(grad_hidden, weight_a):
+    chan_in, chan_out = weight_a.shape[1], grad_hidden.shape[0]
+    cells = grad_hidden.shape[1] * grad_hidden.shape[2]
+    low, high = halo_planes(grad_hidden)
     return pl.pallas_call(
         _back_a_body,
         out_shape=jax.ShapeDtypeStruct((chan_in, cells), jnp.bfloat16),
-        in_specs=[pl.BlockSpec(memory_space=pltpu.VMEM)] * 2,
+        in_specs=[pl.BlockSpec(memory_space=pltpu.VMEM)] * 4,
         out_specs=pl.BlockSpec(memory_space=pltpu.VMEM),
-    )(hidden_pad.reshape(chan_out, -1), weight_a)
+    )(low, grad_hidden.reshape(chan_out, -1), high, weight_a)
 
 
 def per_device(layer_input, hidden_pre, output_pre, output_grad, weight_a, weight_b):
@@ -296,10 +309,8 @@
         jnp.bfloat16
     )
     grad_hidden = grad_hidden.reshape(width_a, depth_a, side * side)
-    hidden_pad = padded_2(grad_hidden, (("space", 1),), 1)
-    back_a = back_flat(hidden_pad, weight_a, depth_a * side * side)
-    source_pad = padded_2(source, (("space", 1),), 1)
-    sums_a = kernel_terms_flat(source_pad, grad_hidden)
+    back_a = back_flat(grad_hidden, weight_a)
+    sums_a = kernel_terms_flat(source, grad_hidden)
     input_grad = back_a.astype(jnp.bfloat16).reshape(1, chan_in, depth_a, side * side)
     samples = lax.axis_size("dp")
     planes_a = depth_a * lax.axis_size("space")

time: 139 us -> 144 us (1.036)
  local copies, waits for them, and re-layouts: 23.8 us -> 29.1 us
  waiting for transfers between devices: 4.09 us -> 0.02 us
  Pallas kernels: 64.6 us -> 68.6 us
  other arithmetic: 16.2 us -> 13.2 us
  starting transfers between devices: 23.1 us -> 25 us
    ppermute x0 -> x4, starting transfers between devices: none -> 12.8 us  [the longest x2 10.2 us: halo_planes(): low = lax.ppermute(tail, 'space', [(i, i + 1) for i in range(count - 1)])]
    ppermute x4 -> x2, starting transfers between devices: 17.8 us -> 9.65 us  [padded_2(): lax.ppermute(tail, axis, [(i, (i + 1) % count) for i in range(ends)])]
    pallas_call x1, Pallas kernels: 52.6 us -> 56.8 us  [all_reduce(): pl.pallas_call(_all_reduce_kernel, out_shape=(jax.ShapeDtypeStruct((rows_...]
    ppermute x4 -> x2, waiting for transfers between devices: 4.08 us -> 0.01 us  [padded_2(): lax.ppermute(head, axis, [((i + 1) % count, i) for i in range(ends)])]
    mul x2, local copies, waits for them, and re-layouts: 1.51 us -> 4.6 us  [per_device(): jnp.repeat(jnp.repeat(jnp.repeat(back_b, 2, 1), 2, 2), 2, 3) * 0.125]
    select_n x1 -> x0, other arithmetic: 2.93 us -> none  [slopes(): jnp.where(values > 0, jnp.ones_like(values), negative_slope * jnp.ones_li...]
    ppermute x4 -> x2, starting transfers between devices: 5.34 us -> 2.57 us  [padded_2(): lax.ppermute(head, axis, [((i + 1) % count, i) for i in range(ends)])]
    concatenate x2 -> x0, other arithmetic: 2.64 us -> none  [padded_2(): jnp.concatenate([lax.ppermute(tail, axis, [(i, (i + 1) % count) for i in...]
  transfers between devices with their start and end apart: 8 -> 8, of which waited for: 1 -> 0; matrix products, arithmetic and copies ran while one was open for 14% -> 28% of each run, Pallas kernels for 38% -> 45%
where the time goes in v9:
time: 144 us
  Pallas kernels  68.6 us (48%)
  local copies, waits for them, and re-layouts  29.1 us (20%)
  starting transfers between devices  25 us (17%)
  other arithmetic  13.2 us (9%)
  matrix products  6.69 us (5%)
    pallas_call x1, Pallas kernels, all_reduce(): pl.pallas_call(_all_reduce_kernel, out_shape=(jax.ShapeDtypeStruct((rows_...  56.8 us
    ppermute x2, starting transfers between devices, halo_planes(): low = lax.ppermute(tail, 'space', [(i, i + 1) for i in range(count - 1)])  10.2 us
    ppermute x2, starting transfers between devices, padded_2(): lax.ppermute(tail, axis, [(i, (i + 1) % count) for i in range(ends)])  9.65 us
    unnamed x17, local copies, waits for them, and re-layouts  8.85 us
    pallas_call x1, Pallas kernels, kernel_terms_flat(): pl.pallas_call(_terms_a_body, out_shape=jax.ShapeDtypeStruct((27, chan_in...  7.18 us
    conv_general_dilated x2, matrix products, conv_cells(): lax.conv_general_dilated(field[None], shaped, (1, 1, 1), ((0, 0), (1, 1),...  6.69 us
    concatenate x1, other arithmetic, all_reduce(): jnp.concatenate([sums_a.reshape(rows_a, 128) * scale_a, wide[:, :128], wi...  5.62 us
    pallas_call x1, Pallas kernels, back_flat(): pl.pallas_call(_back_a_body, out_shape=jax.ShapeDtypeStruct((chan_in, cel...  4.66 us
  transfers between devices with their start and end apart: 8, of which 0 were waited for; matrix products, arithmetic and copies ran while one was open for 28% of the time, Pallas kernels for 45%

profile of v9, /device:TPU:1, one launch (start us, length us, event | category | flops | bytes accessed | tf_op | source)
XLA Modules:
  0.0 143.6 jit_solution(12684652629949039371)
XLA Ops:
  0.6 0.0 copy-start.3
  0.6 1.0 copy.31
  1.7 1.0 copy.30
  2.7 0.7 multiply_convert_fusion.1
  3.4 1.3 collective-permute-start.1
  4.7 5.7 %collective-permute-start = (bf16[256,1,256]{0,2,1:T(8,128)(2,1)}, bf16[256,1,256]{0,2,1:T(8,128)(2,1)}, u32[]{:S(2)}, u32[]{:S(2)}) collective-permute-start(bf16[256,1,256]{0,2,1:T(8,128)(2,1)} %bitcast), channel_id=1, source_target_pairs={{0,1},{1,2},{2,3},{3,4},{4,5},{5,6},{6,7},{7,8},{8,9},{9,10},{10,1... | collective-permute-start | bytes 393224 | tf_op jit(solution)/shard_map/ppermute | solution.py:21
  10.4 1.3 fusion
  11.7 0.2 copy.40
  11.9 0.4 reduce_sum.18
  12.3 1.3 collective-permute-start.7
  13.6 4.0 %collective-permute-start.6 = (bf16[128,1,256]{0,2,1:T(8,128)(2,1)S(1)}, bf16[128,1,256]{0,2,1:T(8,128)(2,1)S(1)}, u32[]{:S(2)}, u32[]{:S(2)}) collective-permute-start(bf16[128,1,256]{0,2,1:T(8,128)(2,1)S(1)} %bitcast.60), channel_id=1, source_target_pairs={{0,1},{1,2},{2,3},{3,4},{4,5},{5,6},{6,7},{7,8},{8,9},{9,10},{10,1... | collective-permute-start | bytes 196616 | tf_op jit(solution)/shard_map/ppermute | solution.py:21
  17.6 0.0 copy-done.3
  17.7 0.7 slice_bitcast_fusion.2
  18.4 1.3 collective-permute-start.5
  19.7 1.9 %copy.33 = bf16[1,256,1,16,16]{1,0,4,3,2:T(2,128)(2,1)} copy(bf16[1,256,1,16,16]{1,4,3,2,0:T(8,128)(2,1)} %bitcast.2) | data formatting | bytes 262144 | tf_op jit(solution)/shard_map/mul | solution.py:291
  21.6 0.7 copy.46
  22.3 0.1 copy.42
  22.4 0.8 copy.37
  23.2 1.3 copy.45
  24.6 2.9 %rev.3 = bf16[27,128,256]{2,1,0:T(8,128)(2,1)} reverse(bf16[27,128,256]{2,1,0:T(8,128)(2,1)} %param.11), dimensions={0} | reverse | bytes 3538944 | tf_op jit(solution)/shard_map/rev | solution.py:188
  27.4 0.0 collective-permute-done.7
  27.4 4.6 %collective-permute-start.4 = (bf16[64,1024]{1,0:T(8,128)(2,1)}, bf16[64,1024]{1,0:T(8,128)(2,1)}, u32[]{:S(2)}, u32[]{:S(2)}) collective-permute-start(bf16[64,1024]{1,0:T(8,128)(2,1)} %get-tuple-element.14), channel_id=1, source_target_pairs={{0,1},{1,2},{2,3},{3,4},{4,5},{5,6},{6,7},{7,8},{8,9},{9,10},{10,1... | collective-permute-start | bytes 393224 | tf_op jit(solution)/shard_map/ppermute | solution.py:238
  32.1 0.1 copy.43
  32.2 0.0 collective-permute-done.6
  32.2 0.1 copy.41
  32.3 3.2 %convolution_multiply_fusion = f32[3,3,3,128,256]{4,3,2,1,0:T(8,128)S(1)} fusion(bf16[1,128,1,16,16]{1,0,4,3,2:T(2,128)(2,1)S(1)} %copy.43, bf16[1,128,1,16,16]{1,0,4,3,2:T(2,128)(2,1)S(1)} %copy.42, bf16[1,128,1,16,16]{1,0,4,3,2:T(2,128)(2,1)S(1)} %copy.41, bf16[1,256,1,16,16]{1,4,3,2,0:T(8,128)(2,1)} %bitcast.2), kind=kOutput, calls=%fused_computation.3 | convolution fusion | flops 417497088 | bytes 3866624 | tf_op jit(solution)/shard_map/transpose(jvp())/conv_general_dilated | solution.py:176
  35.5 0.0 copy-start.2
  35.6 0.0 copy-start.4
  35.6 0.2 fusion.13
  35.8 0.0 collective-permute-done.1
  35.8 1.3 copy.34
  37.1 0.0 collective-permute-done
  37.1 1.2 copy.32
  38.3 0.0 copy-done.2
  38.3 0.0 copy-done.4
  38.3 3.4 %convolution_multiply_fusion.1 = f32[1,128,1,16,16]{1,0,4,3,2:T(1,128)S(1)} fusion(bf16[3,3,3,256,128]{3,4,2,1,0:T(8,128)(2,1)S(1)} %bitcast.53, bf16[1,256,1,16,16]{1,0,4,3,2:T(2,128)(2,1)S(1)} %copy.34, bf16[1,256,1,16,16]{1,0,4,3,2:T(2,128)(2,1)S(1)} %copy-done.4, bf16[1,256,1,16,16]{1,0,4,3,2:T(2,128)(2,1)S(1)} %copy.32), kind=kOutput, calls=%fused_computation.6 | convolution fusion | flops 417234944 | bytes 2293760 | tf_op jit(solution)/shard_map/conv_general_dilated | solution.py:176
  41.8 0.0 copy-start.1
  41.8 0.7 copy-done.1
  42.5 1.1 broadcast_in_dim.21
  43.6 2.0 %copy.35 = f32[128,1024]{1,0:T(8,128)} copy(f32[128,1024]{0,1:T(8,128)} %bitcast.52) | data formatting | bytes 1048576 | tf_op jit(solution)/shard_map/mul | solution.py:306
  45.6 1.4 fusion.1
  47.0 0.8 slice_bitcast_fusion
  47.8 1.3 collective-permute-start.3
  49.1 5.6 %collective-permute-start.2 = (bf16[128,1024]{1,0:T(8,128)(2,1)}, bf16[128,1024]{1,0:T(8,128)(2,1)}, u32[]{:S(2)}, u32[]{:S(2)}) collective-permute-start(bf16[128,1024]{1,0:T(8,128)(2,1)} %get-tuple-element.12), channel_id=1, source_target_pairs={{0,1},{1,2},{2,3},{3,4},{4,5},{5,6},{6,7},{7,8},{8,9},{9,10},{10,1... | collective-permute-start | bytes 786440 | tf_op jit(solution)/shard_map/ppermute | solution.py:238
  54.7 2.4 %broadcast_in_dim.24 = f32[128,2,32,16,2]{0,4,3,2,1:T(2,128)} broadcast(f32[128,32,16]{0,2,1:T(8,128)} %bitcast.50), dimensions={0,2,3} | broadcast | bytes 1310720 | tf_op jit(solution)/shard_map/broadcast_in_dim | solution.py:306
  57.2 2.6 %copy.38 = f32[128,2048]{1,0:T(8,128)} copy(f32[128,2048]{0,1:T(8,128)} %bitcast.43) | data formatting | bytes 2097152 | tf_op jit(solution)/shard_map/mul | solution.py:306
  59.7 2.5 %multiply_convert_fusion.mid_ref.up_ref = bf16[128,2048]{1,0:T(8,128)(2,1)} fusion(f32[128,2048]{1,0:T(8,128)} %copy.38, f32[128,2048]{1,0:T(8,128)} %bitcast.44), kind=kLoop, calls=%fused_computation.10 | loop fusion | flops 524288 | bytes 2621440 | tf_op jit(solution)/shard_map/convert_element_type | solution.py:308
  62.2 0.0 collective-permute-done.5.high_ref
  62.2 0.0 collective-permute-done.4.low_ref
  62.2 7.2 %shard_map.86 = f32[27,64,128]{2,1,0:T(8,128)} custom-call(bf16[64,1024]{1,0:T(8,128)(2,1)} %collective-permute-done.4.low_ref, bf16[64,2048]{1,0:T(8,128)(2,1)} %bitcast.56, bf16[64,1024]{1,0:T(8,128)(2,1)} %collective-permute-done.5.high_ref, bf16[128,2048]{1,0:T(8,128)(2,1)} %multiply_convert_fusion.mid_ref.up_ref), custom_call_target="tpu_custom_call" | custom-call | tf_op jit(solution)/shard_map/pallas_call | solution.py:226
  69.4 1.3 broadcast_multiply_fusion
  70.6 5.6 %select_maximum_fusion.x_ref = f32[9216,128]{1,0:T(8,128)} fusion(f32[3456,128]{1,0:T(8,128)S(1)} %get-tuple-element.8, f32[3456,128]{1,0:T(8,128)S(1)} %get-tuple-element.7, f32[1728,128]{1,0:T(8,128)S(1)} %bitcast.46), kind=kLoop, calls=%fused_computation | loop fusion | flops 7077888 | bytes 9142272 | tf_op jit(solution)/shard_map/concatenate | solution.py:143
  76.2 56.8 %shard_map.87 = (f32[1728,128]{1,0:T(8,128)}, f32[3456,256]{1,0:T(8,128)}) custom-call(f32[9216,128]{1,0:T(8,128)} %select_maximum_fusion.x_ref), custom_call_target="tpu_custom_call" | custom-call | tf_op jit(solution)/shard_map/pallas_call | solution.py:152
  133.1 0.0 copy-start
  133.1 0.0 collective-permute-done.3.high_ref
  133.1 0.0 collective-permute-done.2.low_ref
  133.1 4.7 %shard_map.85 = bf16[64,2048]{1,0:T(8,128)(2,1)} custom-call(bf16[128,1024]{1,0:T(8,128)(2,1)} %collective-permute-done.2.low_ref, bf16[128,2048]{1,0:T(8,128)(2,1)} %multiply_convert_fusion.mid_ref.up_ref, bf16[128,1024]{1,0:T(8,128)(2,1)} %collective-permute-done.3.high_ref, bf16[27,64,128]{2,1,0:T(8,128)(2,1)} %w_ref.1), custom_call_target="tpu_custom_call" | custom-call | tf_op jit(solution)/shard_map/pallas_call | solution.py:271
  137.7 1.8 %reshape.204 = bf16[1,64,2,1024]{3,2,1,0:T(2,128)(2,1)} reshape(bf16[64,2048]{1,0:T(8,128)(2,1)} %shard_map.85) | data formatting | bytes 524288 | tf_op jit(solution)/shard_map/reshape | solution.py:314
  139.6 2.2 %copy.57 = f32[27,64,128]{2,1,0:T(8,128)} copy(f32[27,64,128]{2,1,0:T(8,128)} %bitcast.57) | data formatting | bytes 1769472
  141.8 0.0 copy-done
  141.8 1.8 %copy.58 = f32[27,128,256]{2,1,0:T(8,128)} copy(f32[27,128,256]{2,1,0:T(8,128)S(1)} %bitcast.47) | data formatting | bytes 7077888
  (4 shorter events, 0.1 us)
Async XLA Ops:
  0.6 17.0 %copy-start.3 = (bf16[1,64,2,1024]{3,2,1,0:T(2,128)(2,1)S(1)}, bf16[1,64,2,1024]{3,2,1,0:T(2,128)(2,1)}, u32[]{:S(2)}) copy-start(bf16[1,64,2,1024]{3,2,1,0:T(2,128)(2,1)} %param.6) | copy-start | bytes 786436
  3.4 32.4 %collective-permute-start.1 = (bf16[256,1,256]{0,2,1:T(8,128)(2,1)}, bf16[256,1,256]{0,2,1:T(8,128)(2,1)}, u32[]{:S(2)}, u32[]{:S(2)}) collective-permute-start(bf16[256,1,256]{0,2,1:T(8,128)(2,1)} %bitcast), channel_id=1, source_target_pairs={{1,0},{2,1},{3,2},{4,3},{5,4},{6,5},{7,6},{8,7},{9,8},{10,9},{11,1... | collective-permute-start | bytes 393224 | tf_op jit(solution)/shard_map/ppermute | solution.py:23
  4.7 32.4 %collective-permute-start = (bf16[256,1,256]{0,2,1:T(8,128)(2,1)}, bf16[256,1,256]{0,2,1:T(8,128)(2,1)}, u32[]{:S(2)}, u32[]{:S(2)}) collective-permute-start(bf16[256,1,256]{0,2,1:T(8,128)(2,1)} %bitcast), channel_id=1, source_target_pairs={{0,1},{1,2},{2,3},{3,4},{4,5},{5,6},{6,7},{7,8},{8,9},{9,10},{10,1... | collective-permute-start | bytes 393224 | tf_op jit(solution)/shard_map/ppermute | solution.py:21
  12.3 15.1 %collective-permute-start.7 = (bf16[128,1,256]{0,2,1:T(8,128)(2,1)S(1)}, bf16[128,1,256]{0,2,1:T(8,128)(2,1)S(1)}, u32[]{:S(2)}, u32[]{:S(2)}) collective-permute-start(bf16[128,1,256]{0,2,1:T(8,128)(2,1)S(1)} %bitcast.59), channel_id=1, source_target_pairs={{1,0},{2,1},{3,2},{4,3},{5,4},{6,5},{7,6},{8,7},{9,8},{10,9},{11,1... | collective-permute-start | bytes 196616 | tf_op jit(solution)/shard_map/ppermute | solution.py:23
  13.6 18.6 %collective-permute-start.6 = (bf16[128,1,256]{0,2,1:T(8,128)(2,1)S(1)}, bf16[128,1,256]{0,2,1:T(8,128)(2,1)S(1)}, u32[]{:S(2)}, u32[]{:S(2)}) collective-permute-start(bf16[128,1,256]{0,2,1:T(8,128)(2,1)S(1)} %bitcast.60), channel_id=1, source_target_pairs={{0,1},{1,2},{2,3},{3,4},{4,5},{5,6},{6,7},{7,8},{8,9},{9,10},{10,1... | collective-permute-start | bytes 196616 | tf_op jit(solution)/shard_map/ppermute | solution.py:21
  18.4 43.8 %collective-permute-start.5 = (bf16[64,1024]{1,0:T(8,128)(2,1)}, bf16[64,1024]{1,0:T(8,128)(2,1)}, u32[]{:S(2)}, u32[]{:S(2)}) collective-permute-start(bf16[64,1024]{1,0:T(8,128)(2,1)} %get-tuple-element.13), channel_id=1, source_target_pairs={{1,0},{2,1},{3,2},{4,3},{5,4},{6,5},{7,6},{8,7},{9,8},{10,9},{11,1... | collective-permute-start | bytes 393224 | tf_op jit(solution)/shard_map/ppermute | solution.py:239
  27.4 34.8 %collective-permute-start.4 = (bf16[64,1024]{1,0:T(8,128)(2,1)}, bf16[64,1024]{1,0:T(8,128)(2,1)}, u32[]{:S(2)}, u32[]{:S(2)}) collective-permute-start(bf16[64,1024]{1,0:T(8,128)(2,1)} %get-tuple-element.14), channel_id=1, source_target_pairs={{0,1},{1,2},{2,3},{3,4},{4,5},{5,6},{6,7},{7,8},{8,9},{9,10},{10,1... | collective-permute-start | bytes 393224 | tf_op jit(solution)/shard_map/ppermute | solution.py:238
  35.5 2.7 %copy-start.2 = (bf16[27,128,256]{2,1,0:T(8,128)(2,1)S(1)}, bf16[27,128,256]{2,1,0:T(8,128)(2,1)}, u32[]{:S(2)}) copy-start(bf16[27,128,256]{2,1,0:T(8,128)(2,1)} %rev.3) | copy-start | bytes 5308420
  35.6 2.7 %copy-start.4 = (bf16[1,256,1,16,16]{1,0,4,3,2:T(2,128)(2,1)S(1)}, bf16[1,256,1,16,16]{1,0,4,3,2:T(2,128)(2,1)}, u32[]{:S(2)}) copy-start(bf16[1,256,1,16,16]{1,0,4,3,2:T(2,128)(2,1)} %copy.33) | copy-start | bytes 393220
  41.8 0.7 copy-start.1
  47.8 85.2 %collective-permute-start.3 = (bf16[128,1024]{1,0:T(8,128)(2,1)}, bf16[128,1024]{1,0:T(8,128)(2,1)}, u32[]{:S(2)}, u32[]{:S(2)}) collective-permute-start(bf16[128,1024]{1,0:T(8,128)(2,1)} %get-tuple-element.11), channel_id=1, source_target_pairs={{1,0},{2,1},{3,2},{4,3},{5,4},{6,5},{7,6},{8,7},{9,8},{10,9},{11,1... | collective-permute-start | bytes 786440 | tf_op jit(solution)/shard_map/ppermute | solution.py:239
  49.1 83.9 %collective-permute-start.2 = (bf16[128,1024]{1,0:T(8,128)(2,1)}, bf16[128,1024]{1,0:T(8,128)(2,1)}, u32[]{:S(2)}, u32[]{:S(2)}) collective-permute-start(bf16[128,1024]{1,0:T(8,128)(2,1)} %get-tuple-element.12), channel_id=1, source_target_pairs={{0,1},{1,2},{2,3},{3,4},{4,5},{5,6},{6,7},{7,8},{8,9},{9,10},{10,1... | collective-permute-start | bytes 786440 | tf_op jit(solution)/shard_map/ppermute | solution.py:238
  133.1 8.7 %copy-start = (f32[3456,256]{1,0:T(8,128)S(1)}, f32[3456,256]{1,0:T(8,128)}, u32[]{:S(2)}) copy-start(f32[3456,256]{1,0:T(8,128)} %get-tuple-element.6) | copy-start | bytes 10616836

commit v10 on v8

--- a/solution.py
+++ b/solution.py
@@ -305,6 +305,7 @@
     planes_a = depth_a * lax.axis_size("space")
     scale_a = 1.0 / math.sqrt(samples * planes_a * side * side)
     scale_b = 1.0 / math.sqrt(samples * (planes_a // 2) * half * half)
+    sums_a, sums_b, input_grad = lax.optimization_barrier((sums_a, sums_b, input_grad))
     total_a, total_b = all_reduce(sums_a, sums_b, scale_a, scale_b)
     return (input_grad, total_a, total_b)
 

time: 139 us -> 147 us (1.058)
  local copies, waits for them, and re-layouts: 23.8 us -> 26.3 us
  matrix products: 5.77 us -> 7.4 us
    concatenate x4, local copies, waits for them, and re-layouts: 0.71 us -> 4.2 us  [padded_2(): jnp.concatenate([lax.ppermute(tail, axis, [(i, (i + 1) % count) for i in...]
    select_n x1 -> x0, other arithmetic: 2.93 us -> none  [slopes(): jnp.where(values > 0, jnp.ones_like(values), negative_slope * jnp.ones_li...]
    reduce_sum x1 -> x2, other arithmetic: 0.38 us -> 3.29 us  [per_device(): pooled = active.reshape(width_a, depth_b, 2, half, 2, half, 2).mean(axis=...]
    conv_general_dilated x2, matrix products: 5.77 us -> 7.4 us  [conv_cells(): lax.conv_general_dilated(field[None], shaped, (1, 1, 1), ((0, 0), (1, 1),...]
    unnamed x21 -> x17, local copies, waits for them, and re-layouts: 10.4 us -> 11.7 us
  transfers between devices with their start and end apart: 8 -> 8, of which waited for: 1 -> 2; matrix products, arithmetic and copies ran while one was open for 14% -> 13% of each run, Pallas kernels for 38% -> 5%
where the time goes in v10:
time: 147 us; the launch traced here: 146 us
  Pallas kernels  65.6 us (45%)
  local copies, waits for them, and re-layouts  26.3 us (18%)
  starting transfers between devices  23.7 us (16%)
  other arithmetic  16.9 us (11%)
  matrix products  7.4 us (5%)
  waiting for transfers between devices  4.95 us (3%)
    pallas_call x1, Pallas kernels, all_reduce(): pl.pallas_call(_all_reduce_kernel, out_shape=(jax.ShapeDtypeStruct((rows_...  53.8 us
    ppermute x4, starting transfers between devices, padded_2(): lax.ppermute(tail, axis, [(i, (i + 1) % count) for i in range(ends)])  18.2 us
    unnamed x17, local copies, waits for them, and re-layouts  11.7 us
    conv_general_dilated x2, matrix products, conv_cells(): lax.conv_general_dilated(field[None], shaped, (1, 1, 1), ((0, 0), (1, 1),...  7.4 us
    pallas_call x1, Pallas kernels, kernel_terms_flat(): pl.pallas_call(_terms_a_body, out_shape=jax.ShapeDtypeStruct((27, chan_in...  7.13 us
    concatenate x1, other arithmetic, all_reduce(): jnp.concatenate([sums_a.reshape(rows_a, 128) * scale_a, wide[:, :128], wi...  5.88 us
    ppermute x4, starting transfers between devices, padded_2(): lax.ppermute(head, axis, [((i + 1) % count, i) for i in range(ends)])  5.55 us
    ppermute x4, waiting for transfers between devices, padded_2(): lax.ppermute(head, axis, [((i + 1) % count, i) for i in range(ends)])  4.94 us
  transfers between devices with their start and end apart: 8, of which 2 were waited for; matrix products, arithmetic and copies ran while one was open for 13% of the time, Pallas kernels for 5%

profile of v10, /device:TPU:1, one launch (start us, length us, event | category | flops | bytes accessed | tf_op | source)
XLA Modules:
  0.0 145.9 jit_solution(10531091975473028022)
XLA Ops:
  0.6 0.0 copy-start.1
  0.6 1.0 copy.25
  1.7 1.0 copy.24
  2.7 0.1 multiply_convert_fusion.1
  2.8 1.3 collective-permute-start.3
  4.1 5.7 %collective-permute-start.2 = (bf16[256,1,256]{0,2,1:T(8,128)(2,1)S(1)}, bf16[256,1,256]{0,2,1:T(8,128)(2,1)}, u32[]{:S(2)}, u32[]{:S(2)}) collective-permute-start(bf16[256,1,256]{0,2,1:T(8,128)(2,1)S(1)} %bitcast.55), channel_id=1, source_target_pairs={{0,1},{1,2},{2,3},{3,4},{4,5},{5,6},{6,7},{7,8},{8,9},{9,10},{10,1... | collective-permute-start | bytes 393224 | tf_op jit(solution)/shard_map/ppermute | solution.py:21
  9.7 2.9 %fusion = (f32[128,1024]{1,0:T(8,128)S(1)}, f32[1,128,2,1024]{3,2,1,0:T(2,128)S(1)}) fusion(bf16[1,128,2,1024]{3,2,1,0:T(2,128)(2,1)} %param.7), kind=kLoop, calls=%fused_computation.7 | loop fusion | flops 1441792 | bytes 2097152 | tf_op jit(solution)/shard_map/reduce_sum | solution.py:285
  12.7 0.2 copy.30
  12.9 0.4 reduce_sum.18
  13.2 0.6 multiply_convert_fusion.2
  13.9 1.3 collective-permute-start.5
  15.2 4.6 %collective-permute-start.4 = (bf16[128,1,256]{0,2,1:T(8,128)(2,1)}, bf16[128,1,256]{0,2,1:T(8,128)(2,1)}, u32[]{:S(2)}, u32[]{:S(2)}) collective-permute-start(bf16[128,1,256]{0,2,1:T(8,128)(2,1)} %bitcast.11), channel_id=1, source_target_pairs={{0,1},{1,2},{2,3},{3,4},{4,5},{5,6},{6,7},{7,8},{8,9},{9,10},{10,1... | collective-permute-start | bytes 196616 | tf_op jit(solution)/shard_map/ppermute | solution.py:21
  19.8 0.0 copy-done.1
  19.8 1.1 fusion.16
  20.9 2.3 %collective-permute-start = (bf16[64,1,1024]{2,1,0:T(2,128)(2,1)}, bf16[64,1,1024]{2,1,0:T(2,128)(2,1)S(1)}, u32[]{:S(2)}, u32[]{:S(2)}) collective-permute-start(bf16[64,1,1024]{2,1,0:T(2,128)(2,1)} %get-tuple-element.19), channel_id=1, source_target_pairs={{0,1},{1,2},{2,3},{3,4},{4,5},{5,6},{6,7},{7,8},{8,9},{9,10},{10,1... | collective-permute-start | bytes 393224 | tf_op jit(solution)/shard_map/ppermute | solution.py:21
  23.2 0.3 copy.27
  23.4 0.3 copy.37
  23.8 0.1 copy.32
  23.9 2.9 %rev.3 = bf16[27,128,256]{2,1,0:T(8,128)(2,1)} reverse(bf16[27,128,256]{2,1,0:T(8,128)(2,1)} %param.11), dimensions={0} | reverse | bytes 3538944 | tf_op jit(solution)/shard_map/rev | solution.py:188
  26.8 0.0 collective-permute-done.5
  26.8 0.0 copy-start.4
  26.8 0.6 copy-done.4
  27.4 1.5 %collective-permute-start.1 = (bf16[64,1,1024]{2,1,0:T(2,128)(2,1)S(1)}, bf16[64,1,1024]{2,1,0:T(2,128)(2,1)S(1)}, u32[]{:S(2)}, u32[]{:S(2)}) collective-permute-start(bf16[64,1,1024]{2,1,0:T(2,128)(2,1)S(1)} %get-tuple-element.20), channel_id=1, source_target_pairs={{1,0},{2,1},{3,2},{4,3},{5,4},{6,5},{7,6},{8,7},{9,8},{10,9},{11,1... | collective-permute-start | bytes 393224 | tf_op jit(solution)/shard_map/ppermute | solution.py:23
  28.9 0.9 copy.33
  29.8 0.0 collective-permute-done.4
  29.8 0.9 copy.31
  30.8 0.0 copy-start.3
  30.8 4.0 %fusion.5 = f32[3,3,3,128,256]{4,3,2,1,0:T(8,128)} fusion(bf16[1,128,1,16,16]{1,0,4,3,2:T(2,128)(2,1)S(1)} %copy.33, bf16[1,128,1,16,16]{1,0,4,3,2:T(2,128)(2,1)S(1)} %copy.32, bf16[1,128,1,16,16]{1,0,4,3,2:T(2,128)(2,1)S(1)} %copy.31, bf16[1,256,1,16,16]{1,4,3,2,0:T(8,128)(2,1)S(1)} %bitcast.57), kind=kOutput, calls=%fused_computation.18 | convolution fusion | flops 416612352 | bytes 3866624 | tf_op jit(solution)/shard_map/transpose(jvp())/conv_general_dilated | solution.py:176
  34.8 0.0 collective-permute-done.3
  34.8 1.2 copy.28
  36.0 0.0 collective-permute-done.2
  36.0 1.2 copy.26
  37.1 0.0 collective-permute-done
  37.1 0.4 collective-permute-done.1
  37.5 0.9 pad_maximum_fusion.3
  38.4 1.0 copy.36
  39.4 0.0 copy-done.3
  39.4 3.4 %convolution_multiply_fusion = f32[1,128,1,16,16]{1,0,4,3,2:T(1,128)S(1)} fusion(bf16[3,3,3,256,128]{3,4,2,1,0:T(8,128)(2,1)S(1)} %bitcast.52, bf16[1,256,1,16,16]{1,0,4,3,2:T(2,128)(2,1)S(1)} %copy.28, bf16[1,256,1,16,16]{1,0,4,3,2:T(2,128)(2,1)S(1)} %copy.27, bf16[1,256,1,16,16]{1,0,4,3,2:T(2,128)(2,1)S(1)} %copy.26), kind=kOutput, calls=%fused_computation.6 | convolution fusion | flops 417234944 | bytes 2293760 | tf_op jit(solution)/shard_map/conv_general_dilated | solution.py:176
  42.8 0.3 broadcast_in_dim.23
  43.1 0.2 copy.35
  43.3 0.0 copy-done.2
  43.3 0.7 fusion.1
  44.1 0.5 broadcast_in_dim.21
  44.6 1.3 copy.29
  45.9 1.5 %fusion.15 = (bf16[128,1,1024]{2,1,0:T(2,128)(2,1)}, bf16[128,1,1024]{2,1,0:T(2,128)(2,1)S(1)}) fusion(bf16[128,2,1024]{2,1,0:T(2,128)(2,1)S(1)} %fusion.1), kind=kLoop, calls=%fused_computation.31 | loop fusion | bytes 1048576 | tf_op jit(solution)/shard_map/slice | solution.py:18
  47.4 5.6 %collective-permute-start.6 = (bf16[128,1,1024]{2,1,0:T(2,128)(2,1)}, bf16[128,1,1024]{2,1,0:T(2,128)(2,1)S(1)}, u32[]{:S(2)}, u32[]{:S(2)}) collective-permute-start(bf16[128,1,1024]{2,1,0:T(2,128)(2,1)} %get-tuple-element.15), channel_id=1, source_target_pairs={{0,1},{1,2},{2,3},{3,4},{4,5},{5,6},{6,7},{7,8},{8,9},{9,10},{10,1... | collective-permute-start | bytes 786440 | tf_op jit(solution)/shard_map/ppermute | solution.py:21
  53.1 1.5 %collective-permute-start.7 = (bf16[128,1,1024]{2,1,0:T(2,128)(2,1)S(1)}, bf16[128,1,1024]{2,1,0:T(2,128)(2,1)S(1)}, u32[]{:S(2)}, u32[]{:S(2)}) collective-permute-start(bf16[128,1,1024]{2,1,0:T(2,128)(2,1)S(1)} %get-tuple-element.16), channel_id=1, source_target_pairs={{1,0},{2,1},{3,2},{4,3},{5,4},{6,5},{7,6},{8,7},{9,8},{10,9},{11,1... | collective-permute-start | bytes 786440 | tf_op jit(solution)/shard_map/ppermute | solution.py:23
  54.6 2.1 %multiply_convert_fusion.up_ref = bf16[128,2048]{1,0:T(8,128)(2,1)} fusion(f32[128,2048]{1,0:T(8,128)} %copy.29, f32[128,2048]{1,0:T(8,128)S(1)} %bitcast.37), kind=kLoop, calls=%fused_computation.11 | loop fusion | flops 524288 | bytes 2621440 | tf_op jit(solution)/shard_map/convert_element_type | solution.py:295
  56.7 7.1 %shard_map.85 = f32[27,64,128]{2,1,0:T(8,128)} custom-call(bf16[64,4096]{1,0:T(8,128)(2,1)} %bitcast.51, bf16[128,2048]{1,0:T(8,128)(2,1)} %multiply_convert_fusion.up_ref), custom_call_target="tpu_custom_call" | custom-call | tf_op jit(solution)/shard_map/pallas_call | solution.py:225
  63.8 0.0 collective-permute-done.6
  63.8 4.5 %collective-permute-done.7 = bf16[128,1,1024]{2,1,0:T(2,128)(2,1)S(1)} collective-permute-done((bf16[128,1,1024]{2,1,0:T(2,128)(2,1)S(1)}, bf16[128,1,1024]{2,1,0:T(2,128)(2,1)S(1)}, u32[]{:S(2)}, u32[]{:S(2)}) %collective-permute-start.7) | collective-permute-done | bytes 262176 | tf_op jit(solution)/shard_map/ppermute | solution.py:23
  68.4 1.8 %pad_maximum_fusion = bf16[128,4,1024]{2,1,0:T(4,128)(2,1)S(1)} fusion(bf16[128,1,1024]{2,1,0:T(2,128)(2,1)S(1)} %collective-permute-done.7, bf16[128,2,1024]{2,1,0:T(2,128)(2,1)S(1)} %fusion.1, bf16[128,1,1024]{2,1,0:T(2,128)(2,1)S(1)} %collective-permute-done.6), kind=kLoop, calls=%fused_computation.8 | loop fusion | flops 3145728 | bytes 2097152 | tf_op jit(solution)/shard_map/concatenate | solution.py:19
  70.1 0.0 copy-start
  70.1 1.3 copy.38
  71.5 4.6 %shard_map.86 = bf16[64,2048]{1,0:T(8,128)(2,1)} custom-call(bf16[128,4096]{1,0:T(8,128)(2,1)} %bitcast.40, bf16[27,64,128]{2,1,0:T(8,128)(2,1)} %w_ref.1), custom_call_target="tpu_custom_call" | custom-call | tf_op jit(solution)/shard_map/pallas_call | solution.py:258
  76.1 1.8 %reshape.216 = bf16[1,64,2,1024]{3,2,1,0:T(2,128)(2,1)} reshape(bf16[64,2048]{1,0:T(8,128)(2,1)} %shard_map.86) | data formatting | bytes 524288 | tf_op jit(solution)/shard_map/reshape | solution.py:303
  77.9 1.3 broadcast_multiply_fusion.1
  79.2 0.0 copy-done
  79.2 0.3 broadcast_multiply_fusion
  79.5 0.2 fusion.14
  79.8 5.9 %select_maximum_fusion.x_ref = f32[9216,128]{1,0:T(8,128)} fusion(f32[3456,128]{1,0:T(8,128)S(1)} %get-tuple-element.14, f32[3456,128]{1,0:T(8,128)S(1)} %get-tuple-element.13, f32[1728,128]{1,0:T(8,128)S(1)} %bitcast.41), kind=kLoop, calls=%fused_computation | loop fusion | flops 7077888 | bytes 9142272 | tf_op jit(solution)/shard_map/concatenate | solution.py:143
  85.7 53.8 %shard_map.87 = (f32[1728,128]{1,0:T(8,128)}, f32[3456,256]{1,0:T(8,128)}) custom-call(f32[9216,128]{1,0:T(8,128)} %select_maximum_fusion.x_ref), custom_call_target="tpu_custom_call" | custom-call | tf_op jit(solution)/shard_map/pallas_call | solution.py:152
  139.5 2.2 %copy.43 = f32[27,64,128]{2,1,0:T(8,128)} copy(f32[27,64,128]{2,1,0:T(8,128)} %bitcast.53) | data formatting | bytes 1769472
  141.7 4.2 %copy.44 = f32[27,128,256]{2,1,0:T(8,128)} copy(f32[27,128,256]{2,1,0:T(8,128)} %bitcast.43) | data formatting | bytes 7077888
  (3 shorter events, 0.0 us)
Async XLA Ops:
  0.6 19.2 %copy-start.1 = (bf16[1,64,2,1024]{3,2,1,0:T(2,128)(2,1)S(1)}, bf16[1,64,2,1024]{3,2,1,0:T(2,128)(2,1)}, u32[]{:S(2)}) copy-start(bf16[1,64,2,1024]{3,2,1,0:T(2,128)(2,1)} %param.6) | copy-start | bytes 786436
  2.8 32.0 %collective-permute-start.3 = (bf16[256,1,256]{0,2,1:T(8,128)(2,1)S(1)}, bf16[256,1,256]{0,2,1:T(8,128)(2,1)}, u32[]{:S(2)}, u32[]{:S(2)}) collective-permute-start(bf16[256,1,256]{0,2,1:T(8,128)(2,1)S(1)} %bitcast.54), channel_id=1, source_target_pairs={{1,0},{2,1},{3,2},{4,3},{5,4},{6,5},{7,6},{8,7},{9,8},{10,9},{11,1... | collective-permute-start | bytes 393224 | tf_op jit(solution)/shard_map/ppermute | solution.py:23
  4.1 31.9 %collective-permute-start.2 = (bf16[256,1,256]{0,2,1:T(8,128)(2,1)S(1)}, bf16[256,1,256]{0,2,1:T(8,128)(2,1)}, u32[]{:S(2)}, u32[]{:S(2)}) collective-permute-start(bf16[256,1,256]{0,2,1:T(8,128)(2,1)S(1)} %bitcast.55), channel_id=1, source_target_pairs={{0,1},{1,2},{2,3},{3,4},{4,5},{5,6},{6,7},{7,8},{8,9},{9,10},{10,1... | collective-permute-start | bytes 393224 | tf_op jit(solution)/shard_map/ppermute | solution.py:21
  13.9 12.9 %collective-permute-start.5 = (bf16[128,1,256]{0,2,1:T(8,128)(2,1)}, bf16[128,1,256]{0,2,1:T(8,128)(2,1)S(1)}, u32[]{:S(2)}, u32[]{:S(2)}) collective-permute-start(bf16[128,1,256]{0,2,1:T(8,128)(2,1)} %bitcast.11), channel_id=1, source_target_pairs={{1,0},{2,1},{3,2},{4,3},{5,4},{6,5},{7,6},{8,7},{9,8},{10,9},{11,1... | collective-permute-start | bytes 196616 | tf_op jit(solution)/shard_map/ppermute | solution.py:23
  15.2 14.6 %collective-permute-start.4 = (bf16[128,1,256]{0,2,1:T(8,128)(2,1)}, bf16[128,1,256]{0,2,1:T(8,128)(2,1)}, u32[]{:S(2)}, u32[]{:S(2)}) collective-permute-start(bf16[128,1,256]{0,2,1:T(8,128)(2,1)} %bitcast.11), channel_id=1, source_target_pairs={{0,1},{1,2},{2,3},{3,4},{4,5},{5,6},{6,7},{7,8},{8,9},{9,10},{10,1... | collective-permute-start | bytes 196616 | tf_op jit(solution)/shard_map/ppermute | solution.py:21
  20.9 16.3 %collective-permute-start = (bf16[64,1,1024]{2,1,0:T(2,128)(2,1)}, bf16[64,1,1024]{2,1,0:T(2,128)(2,1)S(1)}, u32[]{:S(2)}, u32[]{:S(2)}) collective-permute-start(bf16[64,1,1024]{2,1,0:T(2,128)(2,1)} %get-tuple-element.19), channel_id=1, source_target_pairs={{0,1},{1,2},{2,3},{3,4},{4,5},{5,6},{6,7},{7,8},{8,9},{9,10},{10,1... | collective-permute-start | bytes 393224 | tf_op jit(solution)/shard_map/ppermute | solution.py:21
  26.8 0.6 copy-start.4
  27.4 10.1 %collective-permute-start.1 = (bf16[64,1,1024]{2,1,0:T(2,128)(2,1)S(1)}, bf16[64,1,1024]{2,1,0:T(2,128)(2,1)S(1)}, u32[]{:S(2)}, u32[]{:S(2)}) collective-permute-start(bf16[64,1,1024]{2,1,0:T(2,128)(2,1)S(1)} %get-tuple-element.20), channel_id=1, source_target_pairs={{1,0},{2,1},{3,2},{4,3},{5,4},{6,5},{7,6},{8,7},{9,8},{10,9},{11,1... | collective-permute-start | bytes 393224 | tf_op jit(solution)/shard_map/ppermute | solution.py:23
  30.8 8.6 %copy-start.3 = (bf16[27,128,256]{2,1,0:T(8,128)(2,1)S(1)}, bf16[27,128,256]{2,1,0:T(8,128)(2,1)}, u32[]{:S(2)}) copy-start(bf16[27,128,256]{2,1,0:T(8,128)(2,1)} %rev.3) | copy-start | bytes 5308420
  39.4 3.9 %copy-start.2 = (bf16[1,128,2,1024]{3,2,1,0:T(2,128)(2,1)S(1)}, bf16[1,128,2,1024]{3,2,1,0:T(2,128)(2,1)}, u32[]{:S(2)}) copy-start(bf16[1,128,2,1024]{3,2,1,0:T(2,128)(2,1)} %param.7) | copy-start | bytes 1572868
  47.4 16.4 %collective-permute-start.6 = (bf16[128,1,1024]{2,1,0:T(2,128)(2,1)}, bf16[128,1,1024]{2,1,0:T(2,128)(2,1)S(1)}, u32[]{:S(2)}, u32[]{:S(2)}) collective-permute-start(bf16[128,1,1024]{2,1,0:T(2,128)(2,1)} %get-tuple-element.15), channel_id=1, source_target_pairs={{0,1},{1,2},{2,3},{3,4},{4,5},{5,6},{6,7},{7,8},{8,9},{9,10},{10,1... | collective-permute-start | bytes 786440 | tf_op jit(solution)/shard_map/ppermute | solution.py:21
  53.1 15.3 %collective-permute-start.7 = (bf16[128,1,1024]{2,1,0:T(2,128)(2,1)S(1)}, bf16[128,1,1024]{2,1,0:T(2,128)(2,1)S(1)}, u32[]{:S(2)}, u32[]{:S(2)}) collective-permute-start(bf16[128,1,1024]{2,1,0:T(2,128)(2,1)S(1)} %get-tuple-element.16), channel_id=1, source_target_pairs={{1,0},{2,1},{3,2},{4,3},{5,4},{6,5},{7,6},{8,7},{9,8},{10,9},{11,1... | collective-permute-start | bytes 786440 | tf_op jit(solution)/shard_map/ppermute | solution.py:23
  70.1 9.1 %copy-start = (f32[3,3,3,128,256]{4,3,2,1,0:T(8,128)S(1)}, f32[3,3,3,128,256]{4,3,2,1,0:T(8,128)}, u32[]{:S(2)}) copy-start(f32[3,3,3,128,256]{4,3,2,1,0:T(8,128)} %fusion.5) | copy-start | bytes 10616836

commit v11 on v8

--- a/solution.py
+++ b/solution.py
@@ -231,7 +231,7 @@
 
 
 def _back_a_body(pad_ref, w_ref, back_ref):
-    cells = back_ref.shape[1]
+    cells = back_ref.shape[1] * back_ref.shape[2]
     plane = pad_ref.shape[1] // 4
     side = 32
     spot = lax.broadcasted_iota(jnp.int32, (1, cells), 1)
@@ -250,14 +250,16 @@
                 )
             back_in = (column - c + 1 >= 0) & (column - c + 1 < side) & (row - b + 1 >= 0) & (row - b + 1 < side)
             back = back + jnp.where(back_in, pltpu.roll(total, shift % cells, 1), 0.0)
-    back_ref[...] = back.astype(back_ref.dtype)
+    plane = back_ref.shape[2]
+    for z in range(back_ref.shape[1]):
+        back_ref[:, z, :] = back[:, z * plane : (z + 1) * plane].astype(back_ref.dtype)
 
 
 def back_flat(hidden_pad, weight_a, cells):
     chan_in, chan_out = weight_a.shape[1], hidden_pad.shape[0]
     return pl.pallas_call(
         _back_a_body,
-        out_shape=jax.ShapeDtypeStruct((chan_in, cells), jnp.bfloat16),
+        out_shape=jax.ShapeDtypeStruct((chan_in, cells // 1024, 1024), jnp.bfloat16),
         in_specs=[pl.BlockSpec(memory_space=pltpu.VMEM)] * 2,
         out_specs=pl.BlockSpec(memory_space=pltpu.VMEM),
     )(hidden_pad.reshape(chan_out, -1), weight_a)

time: 139 us -> 138 us (level)
    reshape x1 -> x0, local copies, waits for them, and re-layouts: 1.85 us -> none  [per_device(): back_a.astype(jnp.bfloat16).reshape(1, chan_in, depth_a, side * side)]
where the time goes in v11:
time: 138 us
  Pallas kernels  64.3 us (47%)
  local copies, waits for them, and re-layouts  23.1 us (17%)
  starting transfers between devices  23.1 us (17%)
  other arithmetic  16.2 us (12%)
  matrix products  5.77 us (4%)
  waiting for transfers between devices  4.09 us (3%)
    pallas_call x1, Pallas kernels, all_reduce(): pl.pallas_call(_all_reduce_kernel, out_shape=(jax.ShapeDtypeStruct((rows_...  52.6 us
    ppermute x4, starting transfers between devices, padded_2(): lax.ppermute(tail, axis, [(i, (i + 1) % count) for i in range(ends)])  17.8 us
    unnamed x21, local copies, waits for them, and re-layouts  11.5 us
    pallas_call x1, Pallas kernels, kernel_terms_flat(): pl.pallas_call(_terms_a_body, out_shape=jax.ShapeDtypeStruct((27, chan_in...  7.34 us
    conv_general_dilated x2, matrix products, conv_cells(): lax.conv_general_dilated(field[None], shaped, (1, 1, 1), ((0, 0), (1, 1),...  5.77 us
    concatenate x1, other arithmetic, all_reduce(): jnp.concatenate([sums_a.reshape(rows_a, 128) * scale_a, wide[:, :128], wi...  5.63 us
    ppermute x4, starting transfers between devices, padded_2(): lax.ppermute(head, axis, [((i + 1) % count, i) for i in range(ends)])  5.34 us
    pallas_call x1, Pallas kernels, back_flat(): pl.pallas_call(_back_a_body, out_shape=jax.ShapeDtypeStruct((chan_in, cel...  4.31 us
  transfers between devices with their start and end apart: 8, of which 1 were waited for; matrix products, arithmetic and copies ran while one was open for 14% of the time, Pallas kernels for 38%

profile of v11, /device:TPU:1, one launch (start us, length us, event | category | flops | bytes accessed | tf_op | source)
XLA Modules:
  0.0 137.5 jit_solution(9850878413550272441)
XLA Ops:
  0.6 0.0 copy-start.2
  0.6 1.0 copy.25
  1.7 1.0 copy.24
  2.7 0.1 multiply_convert_fusion.1
  2.8 1.3 collective-permute-start.1
  4.1 5.0 %collective-permute-start = (bf16[256,1,256]{0,2,1:T(8,128)(2,1)S(1)}, bf16[256,1,256]{0,2,1:T(8,128)(2,1)S(1)}, u32[]{:S(2)}, u32[]{:S(2)}) collective-permute-start(bf16[256,1,256]{0,2,1:T(8,128)(2,1)S(1)} %bitcast.54), channel_id=1, source_target_pairs={{0,1},{1,2},{2,3},{3,4},{4,5},{5,6},{6,7},{7,8},{8,9},{9,10},{10,1... | collective-permute-start | bytes 393224 | tf_op jit(solution)/shard_map/ppermute | solution.py:21
  9.1 2.9 %compare_select_fusion.1 = (f32[1,128,2,1024]{3,2,1,0:T(2,128)S(1)}, f32[128,1024]{1,0:T(8,128)S(1)}) fusion(bf16[1,128,2,1024]{3,2,1,0:T(2,128)(2,1)} %param.7), kind=kLoop, calls=%fused_computation.4 | loop fusion | flops 1441792 | bytes 2097152 | tf_op jit(solution)/shard_map/jit(_where)/select_n | solution.py:31
  12.0 0.2 copy.31
  12.2 0.4 reduce_sum.18
  12.6 1.3 collective-permute-start.7
  13.9 4.2 %collective-permute-start.6 = (bf16[128,1,256]{0,2,1:T(8,128)(2,1)S(1)}, bf16[128,1,256]{0,2,1:T(8,128)(2,1)S(1)}, u32[]{:S(2)}, u32[]{:S(2)}) collective-permute-start(bf16[128,1,256]{0,2,1:T(8,128)(2,1)S(1)} %bitcast.62), channel_id=1, source_target_pairs={{0,1},{1,2},{2,3},{3,4},{4,5},{5,6},{6,7},{7,8},{8,9},{9,10},{10,1... | collective-permute-start | bytes 196616 | tf_op jit(solution)/shard_map/ppermute | solution.py:21
  18.1 0.0 copy-done.2
  18.1 0.4 fusion.15
  18.5 3.4 %collective-permute-start.4 = (bf16[64,1,1024]{2,1,0:T(2,128)(2,1)S(1)}, bf16[64,1,1024]{2,1,0:T(2,128)(2,1)S(1)}, u32[]{:S(2)}, u32[]{:S(2)}) collective-permute-start(bf16[64,1,1024]{2,1,0:T(2,128)(2,1)S(1)} %get-tuple-element.13), channel_id=1, source_target_pairs={{0,1},{1,2},{2,3},{3,4},{4,5},{5,6},{6,7},{7,8},{8,9},{9,10},{10,1... | collective-permute-start | bytes 393224 | tf_op jit(solution)/shard_map/ppermute | solution.py:21
  21.9 0.9 copy.27
  22.8 1.3 copy.38
  24.1 0.1 copy.33
  24.2 2.9 %rev.3 = bf16[27,128,256]{2,1,0:T(8,128)(2,1)} reverse(bf16[27,128,256]{2,1,0:T(8,128)(2,1)} %param.11), dimensions={0} | reverse | bytes 3538944 | tf_op jit(solution)/shard_map/rev | solution.py:188
  27.1 0.0 collective-permute-done.7
  27.1 1.5 %collective-permute-start.5 = (bf16[64,1,1024]{2,1,0:T(2,128)(2,1)S(1)}, bf16[64,1,1024]{2,1,0:T(2,128)(2,1)S(1)}, u32[]{:S(2)}, u32[]{:S(2)}) collective-permute-start(bf16[64,1,1024]{2,1,0:T(2,128)(2,1)S(1)} %get-tuple-element.14), channel_id=1, source_target_pairs={{1,0},{2,1},{3,2},{4,3},{5,4},{6,5},{7,6},{8,7},{9,8},{10,9},{11,1... | collective-permute-start | bytes 393224 | tf_op jit(solution)/shard_map/ppermute | solution.py:23
  28.6 0.1 copy.34
  28.7 0.0 collective-permute-done.6
  28.7 0.1 copy.32
  28.8 2.3 %convolution_multiply_fusion = f32[3,3,3,128,256]{4,3,2,1,0:T(8,128)S(1)} fusion(bf16[1,128,1,16,16]{1,0,4,3,2:T(2,128)(2,1)S(1)} %copy.34, bf16[1,128,1,16,16]{1,0,4,3,2:T(2,128)(2,1)S(1)} %copy.33, bf16[1,128,1,16,16]{1,0,4,3,2:T(2,128)(2,1)S(1)} %copy.32, bf16[1,256,1,16,16]{1,4,3,2,0:T(8,128)(2,1)S(1)} %bitcast.56), kind=kOutput, calls=%fused_computation.5 | convolution fusion | flops 417497088 | bytes 3866624 | tf_op jit(solution)/shard_map/transpose(jvp())/conv_general_dilated | solution.py:176
  31.2 0.0 copy-start.4
  31.2 0.0 copy-start.6
  31.2 1.5 %fusion.13 = (f32[3456,128]{1,0:T(8,128)S(1)}, f32[3456,128]{1,0:T(8,128)}) fusion(f32[3456,256]{1,0:T(8,128)S(1)} %bitcast.42), kind=kLoop, calls=%fused_computation.29 | loop fusion | bytes 7077888 | tf_op jit(solution)/shard_map/slice | solution.py:143
  32.7 0.0 collective-permute-done.1
  32.7 0.3 copy.28
  32.9 0.0 collective-permute-done
  32.9 0.3 copy.26
  33.2 0.0 collective-permute-done.4
  33.2 4.1 %collective-permute-done.5 = bf16[64,1,1024]{2,1,0:T(2,128)(2,1)S(1)} collective-permute-done((bf16[64,1,1024]{2,1,0:T(2,128)(2,1)S(1)}, bf16[64,1,1024]{2,1,0:T(2,128)(2,1)S(1)}, u32[]{:S(2)}, u32[]{:S(2)}) %collective-permute-start.5) | collective-permute-done | bytes 131104 | tf_op jit(solution)/shard_map/ppermute | solution.py:23
  37.3 0.9 pad_maximum_fusion.3
  38.2 1.0 copy.37
  39.1 0.0 copy-done.4
  39.1 0.0 copy-done.6
  39.1 3.4 %convolution_multiply_fusion.1 = f32[1,128,1,16,16]{1,0,4,3,2:T(1,128)S(1)} fusion(bf16[3,3,3,256,128]{3,4,2,1,0:T(8,128)(2,1)S(1)} %bitcast.51, bf16[1,256,1,16,16]{1,0,4,3,2:T(2,128)(2,1)S(1)} %copy.28, bf16[1,256,1,16,16]{1,0,4,3,2:T(2,128)(2,1)S(1)} %copy-done.6, bf16[1,256,1,16,16]{1,0,4,3,2:T(2,128)(2,1)S(1)} %copy.26), kind=kOutput, calls=%fused_computation.6 | convolution fusion | flops 417234944 | bytes 2293760 | tf_op jit(solution)/shard_map/conv_general_dilated | solution.py:176
  42.6 0.0 copy-start.1
  42.6 0.7 copy-done.1
  43.3 0.3 broadcast_in_dim.21
  43.6 0.2 copy.29
  43.8 0.0 copy-done.3
  43.8 0.7 fusion.1
  44.5 1.5 %broadcast_in_dim.24 = f32[128,2,32,16,2]{0,4,3,2,1:T(2,128)S(1)} broadcast(f32[128,32,16]{0,2,1:T(8,128)} %bitcast.44), dimensions={0,2,3} | broadcast | bytes 1310720 | tf_op jit(solution)/shard_map/broadcast_in_dim | solution.py:295
  46.0 1.3 copy.30
  47.3 2.5 %multiply_convert_fusion.up_ref = bf16[128,2048]{1,0:T(8,128)(2,1)} fusion(f32[128,2048]{1,0:T(8,128)} %copy.30, f32[128,2048]{1,0:T(8,128)} %bitcast.36), kind=kLoop, calls=%fused_computation.11 | loop fusion | flops 524288 | bytes 2621440 | tf_op jit(solution)/shard_map/convert_element_type | solution.py:297
  49.8 7.3 %shard_map.86 = f32[27,64,128]{2,1,0:T(8,128)} custom-call(bf16[64,4096]{1,0:T(8,128)(2,1)} %bitcast.50, bf16[128,2048]{1,0:T(8,128)(2,1)} %multiply_convert_fusion.up_ref), custom_call_target="tpu_custom_call" | custom-call | tf_op jit(solution)/shard_map/pallas_call | solution.py:225
  57.1 1.4 %broadcast_multiply_fusion = f32[27,64,128]{2,1,0:T(8,128)S(1)} fusion(f32[27,64,128]{2,1,0:T(8,128)} %shard_map.86), kind=kLoop, calls=%fused_computation.17 | loop fusion | flops 221184 | bytes 1769472 | tf_op jit(solution)/shard_map/mul | solution.py:143
  58.5 1.7 %fusion.14 = (bf16[128,1,1024]{2,1,0:T(2,128)(2,1)}, bf16[128,1,1024]{2,1,0:T(2,128)(2,1)}) fusion(bf16[128,2,1024]{2,1,0:T(2,128)(2,1)S(1)} %fusion.1), kind=kLoop, calls=%fused_computation.30 | loop fusion | bytes 1048576 | tf_op jit(solution)/shard_map/slice | solution.py:18
  60.2 5.2 %collective-permute-start.2 = (bf16[128,1,1024]{2,1,0:T(2,128)(2,1)}, bf16[128,1,1024]{2,1,0:T(2,128)(2,1)S(1)}, u32[]{:S(2)}, u32[]{:S(2)}) collective-permute-start(bf16[128,1,1024]{2,1,0:T(2,128)(2,1)} %get-tuple-element.11), channel_id=1, source_target_pairs={{0,1},{1,2},{2,3},{3,4},{4,5},{5,6},{6,7},{7,8},{8,9},{9,10},{10,1... | collective-permute-start | bytes 786440 | tf_op jit(solution)/shard_map/ppermute | solution.py:21
  65.4 1.3 collective-permute-start.3
  66.7 0.0 copy-done
  66.7 5.6 %select_maximum_fusion.x_ref = f32[9216,128]{1,0:T(8,128)} fusion(f32[3456,128]{1,0:T(8,128)S(1)} %copy-done, f32[3456,128]{1,0:T(8,128)S(1)} %get-tuple-element.7, f32[1728,128]{1,0:T(8,128)S(1)} %bitcast.40), kind=kLoop, calls=%fused_computation | loop fusion | flops 7077888 | bytes 9142272 | tf_op jit(solution)/shard_map/concatenate | solution.py:143
  72.4 52.6 %shard_map.87 = (f32[1728,128]{1,0:T(8,128)}, f32[3456,256]{1,0:T(8,128)}) custom-call(f32[9216,128]{1,0:T(8,128)} %select_maximum_fusion.x_ref), custom_call_target="tpu_custom_call" | custom-call | tf_op jit(solution)/shard_map/pallas_call | solution.py:152
  125.0 0.0 copy-start.5
  125.0 0.0 collective-permute-done.2
  125.0 0.0 collective-permute-done.3
  125.0 1.8 %pad_maximum_fusion = bf16[128,4,1024]{2,1,0:T(4,128)(2,1)S(1)} fusion(bf16[128,1,1024]{2,1,0:T(2,128)(2,1)S(1)} %collective-permute-done.3, bf16[128,2,1024]{2,1,0:T(2,128)(2,1)S(1)} %fusion.1, bf16[128,1,1024]{2,1,0:T(2,128)(2,1)S(1)} %collective-permute-done.2), kind=kLoop, calls=%fused_computation.8 | loop fusion | flops 3145728 | bytes 2097152 | tf_op jit(solution)/shard_map/concatenate | solution.py:19
  126.8 1.3 copy.36
  128.1 4.3 %shard_map.85 = bf16[64,2,1024]{2,1,0:T(2,128)(2,1)} custom-call(bf16[128,4096]{1,0:T(8,128)(2,1)} %bitcast.39, bf16[27,64,128]{2,1,0:T(8,128)(2,1)} %w_ref.1), custom_call_target="tpu_custom_call" | custom-call | tf_op jit(solution)/shard_map/pallas_call | solution.py:260
  132.5 0.0 copy-done.5
  132.5 0.9 copy.43
  133.4 4.2 %copy.44 = f32[27,128,256]{2,1,0:T(8,128)} copy(f32[27,128,256]{2,1,0:T(8,128)} %bitcast.41) | data formatting | bytes 7077888
  (5 shorter events, 0.1 us)
Async XLA Ops:
  0.6 17.5 %copy-start.2 = (bf16[1,64,2,1024]{3,2,1,0:T(2,128)(2,1)S(1)}, bf16[1,64,2,1024]{3,2,1,0:T(2,128)(2,1)}, u32[]{:S(2)}) copy-start(bf16[1,64,2,1024]{3,2,1,0:T(2,128)(2,1)} %param.6) | copy-start | bytes 786436
  2.8 29.9 %collective-permute-start.1 = (bf16[256,1,256]{0,2,1:T(8,128)(2,1)S(1)}, bf16[256,1,256]{0,2,1:T(8,128)(2,1)S(1)}, u32[]{:S(2)}, u32[]{:S(2)}) collective-permute-start(bf16[256,1,256]{0,2,1:T(8,128)(2,1)S(1)} %bitcast.53), channel_id=1, source_target_pairs={{1,0},{2,1},{3,2},{4,3},{5,4},{6,5},{7,6},{8,7},{9,8},{10,9},{11,1... | collective-permute-start | bytes 393224 | tf_op jit(solution)/shard_map/ppermute | solution.py:23
  4.1 28.9 %collective-permute-start = (bf16[256,1,256]{0,2,1:T(8,128)(2,1)S(1)}, bf16[256,1,256]{0,2,1:T(8,128)(2,1)S(1)}, u32[]{:S(2)}, u32[]{:S(2)}) collective-permute-start(bf16[256,1,256]{0,2,1:T(8,128)(2,1)S(1)} %bitcast.54), channel_id=1, source_target_pairs={{0,1},{1,2},{2,3},{3,4},{4,5},{5,6},{6,7},{7,8},{8,9},{9,10},{10,1... | collective-permute-start | bytes 393224 | tf_op jit(solution)/shard_map/ppermute | solution.py:21
  12.6 14.5 %collective-permute-start.7 = (bf16[128,1,256]{0,2,1:T(8,128)(2,1)S(1)}, bf16[128,1,256]{0,2,1:T(8,128)(2,1)S(1)}, u32[]{:S(2)}, u32[]{:S(2)}) collective-permute-start(bf16[128,1,256]{0,2,1:T(8,128)(2,1)S(1)} %bitcast.61), channel_id=1, source_target_pairs={{1,0},{2,1},{3,2},{4,3},{5,4},{6,5},{7,6},{8,7},{9,8},{10,9},{11,1... | collective-permute-start | bytes 196616 | tf_op jit(solution)/shard_map/ppermute | solution.py:23
  13.9 14.8 %collective-permute-start.6 = (bf16[128,1,256]{0,2,1:T(8,128)(2,1)S(1)}, bf16[128,1,256]{0,2,1:T(8,128)(2,1)S(1)}, u32[]{:S(2)}, u32[]{:S(2)}) collective-permute-start(bf16[128,1,256]{0,2,1:T(8,128)(2,1)S(1)} %bitcast.62), channel_id=1, source_target_pairs={{0,1},{1,2},{2,3},{3,4},{4,5},{5,6},{6,7},{7,8},{8,9},{9,10},{10,1... | collective-permute-start | bytes 196616 | tf_op jit(solution)/shard_map/ppermute | solution.py:21
  18.5 14.7 %collective-permute-start.4 = (bf16[64,1,1024]{2,1,0:T(2,128)(2,1)S(1)}, bf16[64,1,1024]{2,1,0:T(2,128)(2,1)S(1)}, u32[]{:S(2)}, u32[]{:S(2)}) collective-permute-start(bf16[64,1,1024]{2,1,0:T(2,128)(2,1)S(1)} %get-tuple-element.13), channel_id=1, source_target_pairs={{0,1},{1,2},{2,3},{3,4},{4,5},{5,6},{6,7},{7,8},{8,9},{9,10},{10,1... | collective-permute-start | bytes 393224 | tf_op jit(solution)/shard_map/ppermute | solution.py:21
  27.1 10.1 %collective-permute-start.5 = (bf16[64,1,1024]{2,1,0:T(2,128)(2,1)S(1)}, bf16[64,1,1024]{2,1,0:T(2,128)(2,1)S(1)}, u32[]{:S(2)}, u32[]{:S(2)}) collective-permute-start(bf16[64,1,1024]{2,1,0:T(2,128)(2,1)S(1)} %get-tuple-element.14), channel_id=1, source_target_pairs={{1,0},{2,1},{3,2},{4,3},{5,4},{6,5},{7,6},{8,7},{9,8},{10,9},{11,1... | collective-permute-start | bytes 393224 | tf_op jit(solution)/shard_map/ppermute | solution.py:23
  31.2 8.0 %copy-start.4 = (bf16[27,128,256]{2,1,0:T(8,128)(2,1)S(1)}, bf16[27,128,256]{2,1,0:T(8,128)(2,1)}, u32[]{:S(2)}) copy-start(bf16[27,128,256]{2,1,0:T(8,128)(2,1)} %rev.3) | copy-start | bytes 5308420
  31.2 8.0 %copy-start.6 = (bf16[1,256,1,16,16]{1,0,4,3,2:T(2,128)(2,1)S(1)}, bf16[1,256,1,16,16]{1,0,4,3,2:T(2,128)(2,1)}, u32[]{:S(2)}) copy-start(bf16[1,256,1,16,16]{1,0,4,3,2:T(2,128)(2,1)} %copy.27) | copy-start | bytes 393220
  39.1 4.7 %copy-start.3 = (bf16[1,128,2,1024]{3,2,1,0:T(2,128)(2,1)S(1)}, bf16[1,128,2,1024]{3,2,1,0:T(2,128)(2,1)}, u32[]{:S(2)}) copy-start(bf16[1,128,2,1024]{3,2,1,0:T(2,128)(2,1)} %param.7) | copy-start | bytes 1572868
  42.6 0.7 copy-start.1
  57.1 9.6 %copy-start = (f32[3456,128]{1,0:T(8,128)S(1)}, f32[3456,128]{1,0:T(8,128)}, u32[]{:S(2)}) copy-start(f32[3456,128]{1,0:T(8,128)} %get-tuple-element.8) | copy-start | bytes 5308420
  60.2 64.8 %collective-permute-start.2 = (bf16[128,1,1024]{2,1,0:T(2,128)(2,1)}, bf16[128,1,1024]{2,1,0:T(2,128)(2,1)S(1)}, u32[]{:S(2)}, u32[]{:S(2)}) collective-permute-start(bf16[128,1,1024]{2,1,0:T(2,128)(2,1)} %get-tuple-element.11), channel_id=1, source_target_pairs={{0,1},{1,2},{2,3},{3,4},{4,5},{5,6},{6,7},{7,8},{8,9},{9,10},{10,1... | collective-permute-start | bytes 786440 | tf_op jit(solution)/shard_map/ppermute | solution.py:21
  65.4 59.6 %collective-permute-start.3 = (bf16[128,1,1024]{2,1,0:T(2,128)(2,1)}, bf16[128,1,1024]{2,1,0:T(2,128)(2,1)S(1)}, u32[]{:S(2)}, u32[]{:S(2)}) collective-permute-start(bf16[128,1,1024]{2,1,0:T(2,128)(2,1)} %get-tuple-element.12), channel_id=1, source_target_pairs={{1,0},{2,1},{3,2},{4,3},{5,4},{6,5},{7,6},{8,7},{9,8},{10,9},{11,1... | collective-permute-start | bytes 786440 | tf_op jit(solution)/shard_map/ppermute | solution.py:23
  125.0 7.4 %copy-start.5 = (f32[1728,128]{1,0:T(8,128)S(1)}, f32[1728,128]{1,0:T(8,128)}, u32[]{:S(2)}) copy-start(f32[1728,128]{1,0:T(8,128)} %get-tuple-element.5) | copy-start | bytes 2654212

commit v12 on v11

--- a/solution.py
+++ b/solution.py
@@ -230,9 +230,10 @@
     )(source_pad.reshape(chan_in, -1), grad_hidden.reshape(chan_out, -1))
 
 
-def _back_a_body(pad_ref, w_ref, back_ref):
+def _back_a_body(low_ref, mid_ref, high_ref, w_ref, back_ref):
     cells = back_ref.shape[1] * back_ref.shape[2]
-    plane = pad_ref.shape[1] // 4
+    plane = back_ref.shape[2]
+    padded = jnp.concatenate([low_ref[...], mid_ref[...], high_ref[...]], axis=1)
     side = 32
     spot = lax.broadcasted_iota(jnp.int32, (1, cells), 1)
     column = spot % side
@@ -245,7 +246,7 @@
             for a in range(3):
                 total = total + jnp.dot(
                     w_ref[9 * a + 3 * b + c],
-                    pad_ref[:, (2 - a) * plane : (2 - a) * plane + cells],
+                    padded[:, (2 - a) * plane : (2 - a) * plane + cells],
                     preferred_element_type=jnp.float32,
                 )
             back_in = (column - c + 1 >= 0) & (column - c + 1 < side) & (row - b + 1 >= 0) & (row - b + 1 < side)
@@ -255,14 +256,17 @@
         back_ref[:, z, :] = back[:, z * plane : (z + 1) * plane].astype(back_ref.dtype)
 
 
-def back_flat(hidden_pad, weight_a, cells):
-    chan_in, chan_out = weight_a.shape[1], hidden_pad.shape[0]
+def back_flat(grad_hidden, weight_a):
+    chan_in, chan_out = weight_a.shape[1], grad_hidden.shape[0]
+    count = lax.axis_size("space")
+    low = lax.ppermute(grad_hidden[:, -1], "space", [(i, i + 1) for i in range(count - 1)])
+    high = lax.ppermute(grad_hidden[:, 0], "space", [(i + 1, i) for i in range(count - 1)])
     return pl.pallas_call(
         _back_a_body,
-        out_shape=jax.ShapeDtypeStruct((chan_in, cells // 1024, 1024), jnp.bfloat16),
-        in_specs=[pl.BlockSpec(memory_space=pltpu.VMEM)] * 2,
+        out_shape=jax.ShapeDtypeStruct((chan_in,) + grad_hidden.shape[1:], jnp.bfloat16),
+        in_specs=[pl.BlockSpec(memory_space=pltpu.VMEM)] * 4,
         out_specs=pl.BlockSpec(memory_space=pltpu.VMEM),
-    )(hidden_pad.reshape(chan_out, -1), weight_a)
+    )(low, grad_hidden.reshape(chan_out, -1), high, weight_a)
 
 
 def per_device(layer_input, hidden_pre, output_pre, output_grad, weight_a, weight_b):
@@ -298,8 +302,7 @@
         jnp.bfloat16
     )
     grad_hidden = grad_hidden.reshape(width_a, depth_a, side * side)
-    hidden_pad = padded_2(grad_hidden, (("space", 1),), 1)
-    back_a = back_flat(hidden_pad, weight_a, depth_a * side * side)
+    back_a = back_flat(grad_hidden, weight_a)
     source_pad = padded_2(source, (("space", 1),), 1)
     sums_a = kernel_terms_flat(source_pad, grad_hidden)
     input_grad = back_a.astype(jnp.bfloat16).reshape(1, chan_in, depth_a, side * side)

time: 138 us -> 144 us (1.043)
  local copies, waits for them, and re-layouts: 23.1 us -> 28.7 us
  starting transfers between devices: 23.1 us -> 25.2 us
  waiting for transfers between devices: 4.09 us -> 2.11 us
    ppermute x0 -> x2, starting transfers between devices: none -> 7.99 us  [the longest x1 6.71 us: back_flat(): lax.ppermute(grad_hidden[:, -1], 'space', [(i, i + 1) for i in range(coun...]
    ppermute x4 -> x3, starting transfers between devices: 17.8 us -> 13.2 us  [padded_2(): lax.ppermute(tail, axis, [(i, (i + 1) % count) for i in range(ends)])]
    mul x2, local copies, waits for them, and re-layouts: 1.51 us -> 4.6 us  [per_device(): jnp.repeat(jnp.repeat(jnp.repeat(back_b, 2, 1), 2, 2), 2, 3) * 0.125]
    select_n x1 -> x0, other arithmetic: 2.93 us -> none  [slopes(): jnp.where(values > 0, jnp.ones_like(values), negative_slope * jnp.ones_li...]
    ppermute x4 -> x3, waiting for transfers between devices: 4.08 us -> 2.1 us  [padded_2(): lax.ppermute(head, axis, [((i + 1) % count, i) for i in range(ends)])]
    concatenate x4, local copies, waits for them, and re-layouts: 0.71 us -> 2.65 us  [padded_2(): jnp.concatenate([lax.ppermute(tail, axis, [(i, (i + 1) % count) for i in...]
    broadcast_in_dim x2, local copies, waits for them, and re-layouts: 1.73 us -> 3.51 us  [per_device(): jnp.repeat(jnp.repeat(jnp.repeat(back_b, 2, 1), 2, 2), 2, 3) * 0.125]
    rev x1, local copies, waits for them, and re-layouts: 2.87 us -> 1.32 us  [back_cells(): flipped = kernel[::-1].transpose(0, 2, 1)]
  transfers between devices with their start and end apart: 8 -> 8, of which waited for: 1 -> 1; matrix products, arithmetic and copies ran while one was open for 14% -> 20% of each run, Pallas kernels for 38% -> 42%
where the time goes in v12:
time: 144 us
  Pallas kernels  64.9 us (45%)
  local copies, waits for them, and re-layouts  28.7 us (20%)
  starting transfers between devices  25.2 us (18%)
  other arithmetic  15 us (10%)
  matrix products  6.74 us (5%)
  waiting for transfers between devices  2.11 us (1%)
    pallas_call x1, Pallas kernels, all_reduce(): pl.pallas_call(_all_reduce_kernel, out_shape=(jax.ShapeDtypeStruct((rows_...  53.5 us
    ppermute x3, starting transfers between devices, padded_2(): lax.ppermute(tail, axis, [(i, (i + 1) % count) for i in range(ends)])  13.2 us
    unnamed x18, local copies, waits for them, and re-layouts  11.4 us
    pallas_call x1, Pallas kernels, kernel_terms_flat(): pl.pallas_call(_terms_a_body, out_shape=jax.ShapeDtypeStruct((27, chan_in...  7.13 us
    conv_general_dilated x2, matrix products, conv_cells(): lax.conv_general_dilated(field[None], shaped, (1, 1, 1), ((0, 0), (1, 1),...  6.74 us
    ppermute x1, starting transfers between devices, back_flat(): lax.ppermute(grad_hidden[:, -1], 'space', [(i, i + 1) for i in range(coun...  6.71 us
    concatenate x1, other arithmetic, all_reduce(): jnp.concatenate([sums_a.reshape(rows_a, 128) * scale_a, wide[:, :128], wi...  5.63 us
    mul x2, local copies, waits for them, and re-layouts, per_device(): jnp.repeat(jnp.repeat(jnp.repeat(back_b, 2, 1), 2, 2), 2, 3) * 0.125  4.6 us
  transfers between devices with their start and end apart: 8, of which 1 were waited for; matrix products, arithmetic and copies ran while one was open for 20% of the time, Pallas kernels for 42%

profile of v12, /device:TPU:1, one launch (start us, length us, event | category | flops | bytes accessed | tf_op | source)
XLA Modules:
  0.0 143.6 jit_solution(10215330718277993572)
XLA Ops:
  0.6 0.0 copy-start.1
  0.6 1.0 copy.29
  1.7 1.0 copy.28
  2.7 0.7 multiply_convert_fusion.1
  3.4 1.3 collective-permute-start.1
  4.7 5.7 %collective-permute-start = (bf16[256,1,256]{0,2,1:T(8,128)(2,1)}, bf16[256,1,256]{0,2,1:T(8,128)(2,1)}, u32[]{:S(2)}, u32[]{:S(2)}) collective-permute-start(bf16[256,1,256]{0,2,1:T(8,128)(2,1)} %bitcast), channel_id=1, source_target_pairs={{0,1},{1,2},{2,3},{3,4},{4,5},{5,6},{6,7},{7,8},{8,9},{9,10},{10,1... | collective-permute-start | bytes 393224 | tf_op jit(solution)/shard_map/ppermute | solution.py:21
  10.3 1.3 fusion
  11.7 0.2 copy.37
  11.9 0.4 reduce_sum.18
  12.3 0.0 copy-start.3
  12.3 1.4 collective-permute-start.7
  13.7 4.0 %collective-permute-start.6 = (bf16[128,1,256]{0,2,1:T(8,128)(2,1)S(1)}, bf16[128,1,256]{0,2,1:T(8,128)(2,1)S(1)}, u32[]{:S(2)}, u32[]{:S(2)}) collective-permute-start(bf16[128,1,256]{0,2,1:T(8,128)(2,1)S(1)} %bitcast.56), channel_id=1, source_target_pairs={{0,1},{1,2},{2,3},{3,4},{4,5},{5,6},{6,7},{7,8},{8,9},{9,10},{10,1... | collective-permute-start | bytes 196616 | tf_op jit(solution)/shard_map/ppermute | solution.py:21
  17.7 0.0 copy-done.1
  17.7 1.2 fusion.14
  18.9 3.6 %collective-permute-start.4 = (bf16[64,1,1024]{2,1,0:T(2,128)(2,1)}, bf16[64,1,1024]{2,1,0:T(2,128)(2,1)}, u32[]{:S(2)}, u32[]{:S(2)}) collective-permute-start(bf16[64,1,1024]{2,1,0:T(2,128)(2,1)} %get-tuple-element.13), channel_id=1, source_target_pairs={{0,1},{1,2},{2,3},{3,4},{4,5},{5,6},{6,7},{7,8},{8,9},{9,10},{10,1... | collective-permute-start | bytes 393224 | tf_op jit(solution)/shard_map/ppermute | solution.py:21
  22.5 1.9 %copy.31 = bf16[1,256,1,16,16]{1,0,4,3,2:T(2,128)(2,1)} copy(bf16[1,256,1,16,16]{1,4,3,2,0:T(8,128)(2,1)} %bitcast.2) | data formatting | bytes 262144 | tf_op jit(solution)/shard_map/mul | solution.py:284
  24.4 0.1 copy.39
  24.5 0.8 copy.35
  25.3 1.3 copy.42
  26.6 0.0 copy-done.3
  26.6 1.3 rev.3
  27.9 0.0 collective-permute-done.7
  27.9 1.3 collective-permute-start.5
  29.2 0.1 copy.40
  29.3 0.0 collective-permute-done.6
  29.4 0.1 copy.38
  29.5 3.3 %convolution_multiply_fusion = f32[3,3,3,128,256]{4,3,2,1,0:T(8,128)S(1)} fusion(bf16[1,128,1,16,16]{1,0,4,3,2:T(2,128)(2,1)S(1)} %copy.40, bf16[1,128,1,16,16]{1,0,4,3,2:T(2,128)(2,1)S(1)} %copy.39, bf16[1,128,1,16,16]{1,0,4,3,2:T(2,128)(2,1)S(1)} %copy.38, bf16[1,256,1,16,16]{1,4,3,2,0:T(8,128)(2,1)} %bitcast.2), kind=kOutput, calls=%fused_computation.3 | convolution fusion | flops 417497088 | bytes 3866624 | tf_op jit(solution)/shard_map/transpose(jvp())/conv_general_dilated | solution.py:176
  32.8 0.0 copy-start.2
  32.8 0.0 copy-start.4
  32.8 0.0 copy-start.5
  32.8 0.2 fusion.13
  33.0 0.0 collective-permute-done.1
  33.1 1.3 copy.32
  34.4 0.0 collective-permute-done
  34.4 1.2 copy.30
  35.5 0.0 collective-permute-done.4
  35.5 2.1 %collective-permute-done.5 = bf16[64,1,1024]{2,1,0:T(2,128)(2,1)S(1)} collective-permute-done((bf16[64,1,1024]{2,1,0:T(2,128)(2,1)}, bf16[64,1,1024]{2,1,0:T(2,128)(2,1)S(1)}, u32[]{:S(2)}, u32[]{:S(2)}) %collective-permute-start.5) | collective-permute-done | bytes 131104 | tf_op jit(solution)/shard_map/ppermute | solution.py:23
  37.6 0.0 copy-done.2
  37.6 1.8 %pad_maximum_fusion.2 = bf16[64,4,1024]{2,1,0:T(4,128)(2,1)S(1)} fusion(bf16[64,1,1024]{2,1,0:T(2,128)(2,1)S(1)} %collective-permute-done.5, bf16[64,2,1024]{2,1,0:T(2,128)(2,1)S(1)} %bitcast.46, bf16[64,1,1024]{2,1,0:T(2,128)(2,1)} %collective-permute-done.4), kind=kLoop, calls=%fused_computation.15 | loop fusion | flops 1572864 | bytes 1048576 | tf_op jit(solution)/shard_map/concatenate | solution.py:19
  39.5 1.0 copy.43
  40.4 0.0 copy-done.4
  40.4 0.0 copy-done.5
  40.4 3.4 %convolution_multiply_fusion.1 = f32[1,128,1,16,16]{1,0,4,3,2:T(1,128)S(1)} fusion(bf16[3,3,3,256,128]{3,4,2,1,0:T(8,128)(2,1)S(1)} %bitcast.51, bf16[1,256,1,16,16]{1,0,4,3,2:T(2,128)(2,1)S(1)} %copy.32, bf16[1,256,1,16,16]{1,0,4,3,2:T(2,128)(2,1)S(1)} %copy-done.5, bf16[1,256,1,16,16]{1,0,4,3,2:T(2,128)(2,1)S(1)} %copy.30), kind=kOutput, calls=%fused_computation.6 | convolution fusion | flops 417234944 | bytes 2293760 | tf_op jit(solution)/shard_map/conv_general_dilated | solution.py:176
  43.9 0.0 copy-start
  43.9 0.7 copy-done
  44.6 1.1 broadcast_in_dim.21
  45.7 2.0 %copy.33 = f32[128,1024]{1,0:T(8,128)} copy(f32[128,1024]{0,1:T(8,128)} %bitcast.49) | data formatting | bytes 1048576 | tf_op jit(solution)/shard_map/mul | solution.py:299
  47.8 1.4 fusion.1
  49.2 0.8 slice_bitcast_fusion
  50.0 1.3 collective-permute-start.3
  51.3 6.7 %collective-permute-start.2 = (bf16[128,1024]{1,0:T(8,128)(2,1)}, bf16[128,1024]{1,0:T(8,128)(2,1)}, u32[]{:S(2)}, u32[]{:S(2)}) collective-permute-start(bf16[128,1024]{1,0:T(8,128)(2,1)} %get-tuple-element.12), channel_id=1, source_target_pairs={{0,1},{1,2},{2,3},{3,4},{4,5},{5,6},{6,7},{7,8},{8,9},{9,10},{10,1... | collective-permute-start | bytes 786440 | tf_op jit(solution)/shard_map/ppermute | solution.py:262
  58.0 2.4 %broadcast_in_dim.24 = f32[128,2,32,16,2]{0,4,3,2,1:T(2,128)} broadcast(f32[128,32,16]{0,2,1:T(8,128)} %bitcast.44), dimensions={0,2,3} | broadcast | bytes 1310720 | tf_op jit(solution)/shard_map/broadcast_in_dim | solution.py:299
  60.4 2.6 %copy.36 = f32[128,2048]{1,0:T(8,128)} copy(f32[128,2048]{0,1:T(8,128)} %bitcast.37) | data formatting | bytes 2097152 | tf_op jit(solution)/shard_map/mul | solution.py:299
  63.0 2.5 %multiply_convert_fusion.mid_ref.up_ref = bf16[128,2048]{1,0:T(8,128)(2,1)} fusion(f32[128,2048]{1,0:T(8,128)} %copy.36, f32[128,2048]{1,0:T(8,128)} %bitcast.38), kind=kLoop, calls=%fused_computation.10 | loop fusion | flops 524288 | bytes 2621440 | tf_op jit(solution)/shard_map/convert_element_type | solution.py:301
  65.4 7.1 %shard_map.86 = f32[27,64,128]{2,1,0:T(8,128)} custom-call(bf16[64,4096]{1,0:T(8,128)(2,1)} %bitcast.50, bf16[128,2048]{1,0:T(8,128)(2,1)} %multiply_convert_fusion.mid_ref.up_ref), custom_call_target="tpu_custom_call" | custom-call | tf_op jit(solution)/shard_map/pallas_call | solution.py:225
  72.5 1.3 broadcast_multiply_fusion
  73.8 5.6 %select_maximum_fusion.x_ref = f32[9216,128]{1,0:T(8,128)} fusion(f32[3456,128]{1,0:T(8,128)S(1)} %get-tuple-element.8, f32[3456,128]{1,0:T(8,128)S(1)} %get-tuple-element.7, f32[1728,128]{1,0:T(8,128)S(1)} %bitcast.40), kind=kLoop, calls=%fused_computation | loop fusion | flops 7077888 | bytes 9142272 | tf_op jit(solution)/shard_map/concatenate | solution.py:143
  79.4 53.5 %shard_map.87 = (f32[1728,128]{1,0:T(8,128)}, f32[3456,256]{1,0:T(8,128)}) custom-call(f32[9216,128]{1,0:T(8,128)} %select_maximum_fusion.x_ref), custom_call_target="tpu_custom_call" | custom-call | tf_op jit(solution)/shard_map/pallas_call | solution.py:152
  132.9 0.0 collective-permute-done.3.high_ref
  132.9 0.0 collective-permute-done.2.low_ref
  132.9 4.4 %shard_map.85 = bf16[64,2,1024]{2,1,0:T(2,128)(2,1)} custom-call(bf16[128,1024]{1,0:T(8,128)(2,1)} %collective-permute-done.2.low_ref, bf16[128,2048]{1,0:T(8,128)(2,1)} %multiply_convert_fusion.mid_ref.up_ref, bf16[128,1024]{1,0:T(8,128)(2,1)} %collective-permute-done.3.high_ref, bf16[27,64,128]{2,1,0:T(8,128)(2,1)} %w_ref.1), custom_call_target="tpu_custom_call" | custom-call | tf_op jit(solution)/shard_map/pallas_call | solution.py:264
  137.3 2.2 %copy.52 = f32[27,64,128]{2,1,0:T(8,128)} copy(f32[27,64,128]{2,1,0:T(8,128)} %bitcast.52) | data formatting | bytes 1769472
  139.5 4.2 %copy.53 = f32[27,128,256]{2,1,0:T(8,128)} copy(f32[27,128,256]{2,1,0:T(8,128)} %bitcast.41) | data formatting | bytes 7077888
  (3 shorter events, 0.0 us)
Async XLA Ops:
  0.6 17.1 %copy-start.1 = (bf16[1,64,2,1024]{3,2,1,0:T(2,128)(2,1)S(1)}, bf16[1,64,2,1024]{3,2,1,0:T(2,128)(2,1)}, u32[]{:S(2)}) copy-start(bf16[1,64,2,1024]{3,2,1,0:T(2,128)(2,1)} %param.6) | copy-start | bytes 786436
  3.4 29.6 %collective-permute-start.1 = (bf16[256,1,256]{0,2,1:T(8,128)(2,1)}, bf16[256,1,256]{0,2,1:T(8,128)(2,1)}, u32[]{:S(2)}, u32[]{:S(2)}) collective-permute-start(bf16[256,1,256]{0,2,1:T(8,128)(2,1)} %bitcast), channel_id=1, source_target_pairs={{1,0},{2,1},{3,2},{4,3},{5,4},{6,5},{7,6},{8,7},{9,8},{10,9},{11,1... | collective-permute-start | bytes 393224 | tf_op jit(solution)/shard_map/ppermute | solution.py:23
  4.7 29.7 %collective-permute-start = (bf16[256,1,256]{0,2,1:T(8,128)(2,1)}, bf16[256,1,256]{0,2,1:T(8,128)(2,1)}, u32[]{:S(2)}, u32[]{:S(2)}) collective-permute-start(bf16[256,1,256]{0,2,1:T(8,128)(2,1)} %bitcast), channel_id=1, source_target_pairs={{0,1},{1,2},{2,3},{3,4},{4,5},{5,6},{6,7},{7,8},{8,9},{9,10},{10,1... | collective-permute-start | bytes 393224 | tf_op jit(solution)/shard_map/ppermute | solution.py:21
  12.3 14.3 %copy-start.3 = (bf16[27,128,256]{2,1,0:T(8,128)(2,1)S(1)}, bf16[27,128,256]{2,1,0:T(8,128)(2,1)}, u32[]{:S(2)}) copy-start(bf16[27,128,256]{2,1,0:T(8,128)(2,1)} %param.11) | copy-start | bytes 5308420
  12.3 15.6 %collective-permute-start.7 = (bf16[128,1,256]{0,2,1:T(8,128)(2,1)S(1)}, bf16[128,1,256]{0,2,1:T(8,128)(2,1)S(1)}, u32[]{:S(2)}, u32[]{:S(2)}) collective-permute-start(bf16[128,1,256]{0,2,1:T(8,128)(2,1)S(1)} %bitcast.55), channel_id=1, source_target_pairs={{1,0},{2,1},{3,2},{4,3},{5,4},{6,5},{7,6},{8,7},{9,8},{10,9},{11,1... | collective-permute-start | bytes 196616 | tf_op jit(solution)/shard_map/ppermute | solution.py:23
  13.7 15.6 %collective-permute-start.6 = (bf16[128,1,256]{0,2,1:T(8,128)(2,1)S(1)}, bf16[128,1,256]{0,2,1:T(8,128)(2,1)S(1)}, u32[]{:S(2)}, u32[]{:S(2)}) collective-permute-start(bf16[128,1,256]{0,2,1:T(8,128)(2,1)S(1)} %bitcast.56), channel_id=1, source_target_pairs={{0,1},{1,2},{2,3},{3,4},{4,5},{5,6},{6,7},{7,8},{8,9},{9,10},{10,1... | collective-permute-start | bytes 196616 | tf_op jit(solution)/shard_map/ppermute | solution.py:21
  18.9 16.6 %collective-permute-start.4 = (bf16[64,1,1024]{2,1,0:T(2,128)(2,1)}, bf16[64,1,1024]{2,1,0:T(2,128)(2,1)}, u32[]{:S(2)}, u32[]{:S(2)}) collective-permute-start(bf16[64,1,1024]{2,1,0:T(2,128)(2,1)} %get-tuple-element.13), channel_id=1, source_target_pairs={{0,1},{1,2},{2,3},{3,4},{4,5},{5,6},{6,7},{7,8},{8,9},{9,10},{10,1... | collective-permute-start | bytes 393224 | tf_op jit(solution)/shard_map/ppermute | solution.py:21
  27.9 9.7 %collective-permute-start.5 = (bf16[64,1,1024]{2,1,0:T(2,128)(2,1)}, bf16[64,1,1024]{2,1,0:T(2,128)(2,1)S(1)}, u32[]{:S(2)}, u32[]{:S(2)}) collective-permute-start(bf16[64,1,1024]{2,1,0:T(2,128)(2,1)} %get-tuple-element.14), channel_id=1, source_target_pairs={{1,0},{2,1},{3,2},{4,3},{5,4},{6,5},{7,6},{8,7},{9,8},{10,9},{11,1... | collective-permute-start | bytes 393224 | tf_op jit(solution)/shard_map/ppermute | solution.py:23
  32.8 4.9 %copy-start.2 = (bf16[1,64,2,1024]{3,2,1,0:T(2,128)(2,1)S(1)}, bf16[1,64,2,1024]{3,2,1,0:T(2,128)(2,1)}, u32[]{:S(2)}) copy-start(bf16[1,64,2,1024]{3,2,1,0:T(2,128)(2,1)} %param.6) | copy-start | bytes 786436
  32.8 7.7 %copy-start.4 = (bf16[27,128,256]{2,1,0:T(8,128)(2,1)S(1)}, bf16[27,128,256]{2,1,0:T(8,128)(2,1)}, u32[]{:S(2)}) copy-start(bf16[27,128,256]{2,1,0:T(8,128)(2,1)} %rev.3) | copy-start | bytes 5308420
  32.8 7.6 %copy-start.5 = (bf16[1,256,1,16,16]{1,0,4,3,2:T(2,128)(2,1)S(1)}, bf16[1,256,1,16,16]{1,0,4,3,2:T(2,128)(2,1)}, u32[]{:S(2)}) copy-start(bf16[1,256,1,16,16]{1,0,4,3,2:T(2,128)(2,1)} %copy.31) | copy-start | bytes 393220
  43.9 0.7 copy-start
  50.0 82.9 %collective-permute-start.3 = (bf16[128,1024]{1,0:T(8,128)(2,1)}, bf16[128,1024]{1,0:T(8,128)(2,1)}, u32[]{:S(2)}, u32[]{:S(2)}) collective-permute-start(bf16[128,1024]{1,0:T(8,128)(2,1)} %get-tuple-element.11), channel_id=1, source_target_pairs={{1,0},{2,1},{3,2},{4,3},{5,4},{6,5},{7,6},{8,7},{9,8},{10,9},{11,1... | collective-permute-start | bytes 786440 | tf_op jit(solution)/shard_map/ppermute | solution.py:263
  51.3 81.7 %collective-permute-start.2 = (bf16[128,1024]{1,0:T(8,128)(2,1)}, bf16[128,1024]{1,0:T(8,128)(2,1)}, u32[]{:S(2)}, u32[]{:S(2)}) collective-permute-start(bf16[128,1024]{1,0:T(8,128)(2,1)} %get-tuple-element.12), channel_id=1, source_target_pairs={{0,1},{1,2},{2,3},{3,4},{4,5},{5,6},{6,7},{7,8},{8,9},{9,10},{10,1... | collective-permute-start | bytes 786440 | tf_op jit(solution)/shard_map/ppermute | solution.py:262

commit v13 on v11

--- a/solution.py
+++ b/solution.py
@@ -185,8 +185,16 @@
 
 
 def back_cells(padded, kernel):
-    flipped = kernel[::-1].transpose(0, 2, 1)
-    return conv_cells(padded, flipped)
+    shaped = kernel.reshape(3, 3, 3, kernel.shape[1], kernel.shape[2])
+    result = lax.conv_general_dilated(
+        padded[None, :, ::-1, ::-1, ::-1],
+        shaped,
+        (1, 1, 1),
+        ((0, 0), (1, 1), (1, 1)),
+        dimension_numbers=("NCDHW", "DHWOI", "NCDHW"),
+        preferred_element_type=jnp.float32,
+    )
+    return result[0, :, ::-1, ::-1, ::-1]
 
 
 def kernel_terms(padded, upstream):

time: 138 us -> 142 us (1.029)
  other arithmetic: 16.2 us -> 22.1 us
  waiting for transfers between devices: 4.09 us -> 0.02 us
  Pallas kernels: 64.3 us -> 66.6 us
  starting transfers between devices: 23.1 us -> 24.9 us
  local copies, waits for them, and re-layouts: 23.1 us -> 21.4 us
    ppermute x4, waiting for transfers between devices: 4.08 us -> 0.01 us  [padded_2(): lax.ppermute(head, axis, [((i + 1) % count, i) for i in range(ends)])]
    conv_general_dilated x2 -> x1, matrix products: 5.77 us -> 2.38 us  [conv_cells(): lax.conv_general_dilated(field[None], shaped, (1, 1, 1), ((0, 0), (1, 1),...]
    concatenate x2 -> x3, other arithmetic: 2.64 us -> 5.89 us  [padded_2(): jnp.concatenate([lax.ppermute(tail, axis, [(i, (i + 1) % count) for i in...]
    conv_general_dilated x0 -> x1, matrix products: none -> 3.07 us  [back_cells(): lax.conv_general_dilated(padded[None, :, ::-1, ::-1, ::-1], shaped, (1, 1...]
    rev x1, local copies, waits for them, and re-layouts: 2.87 us -> 0.27 us  [back_cells(): padded[None, :, ::-1, ::-1, ::-1]]
    pallas_call x1, Pallas kernels: 52.6 us -> 55.1 us  [all_reduce(): pl.pallas_call(_all_reduce_kernel, out_shape=(jax.ShapeDtypeStruct((rows_...]
    reduce_sum x1, local copies, waits for them, and re-layouts: 0.19 us -> 2.03 us  [per_device(): pooled = active.reshape(width_a, depth_b, 2, half, 2, half, 2).mean(axis=...]
    ppermute x4, starting transfers between devices: 17.8 us -> 19.4 us  [padded_2(): lax.ppermute(tail, axis, [(i, (i + 1) % count) for i in range(ends)])]
  transfers between devices with their start and end apart: 8 -> 8, of which waited for: 1 -> 0; matrix products, arithmetic and copies ran while one was open for 14% -> 21% of each run, Pallas kernels for 38% -> 44%
where the time goes in v13:
time: 142 us; the launch traced here: 141 us
  Pallas kernels  66.6 us (47%)
  starting transfers between devices  24.9 us (18%)
  other arithmetic  22.1 us (16%)
  local copies, waits for them, and re-layouts  21.4 us (15%)
  matrix products  5.45 us (4%)
    pallas_call x1, Pallas kernels, all_reduce(): pl.pallas_call(_all_reduce_kernel, out_shape=(jax.ShapeDtypeStruct((rows_...  55.1 us
    ppermute x4, starting transfers between devices, padded_2(): lax.ppermute(tail, axis, [(i, (i + 1) % count) for i in range(ends)])  19.4 us
    unnamed x17, local copies, waits for them, and re-layouts  11.6 us
    pallas_call x1, Pallas kernels, kernel_terms_flat(): pl.pallas_call(_terms_a_body, out_shape=jax.ShapeDtypeStruct((27, chan_in...  7.13 us
    concatenate x3, other arithmetic, padded_2(): jnp.concatenate([lax.ppermute(tail, axis, [(i, (i + 1) % count) for i in...  5.89 us
    ppermute x4, starting transfers between devices, padded_2(): lax.ppermute(head, axis, [((i + 1) % count, i) for i in range(ends)])  5.56 us
    concatenate x1, other arithmetic, all_reduce(): jnp.concatenate([sums_a.reshape(rows_a, 128) * scale_a, wide[:, :128], wi...  5.3 us
    pallas_call x1, Pallas kernels, back_flat(): pl.pallas_call(_back_a_body, out_shape=jax.ShapeDtypeStruct((chan_in, cel...  4.3 us
  transfers between devices with their start and end apart: 8, of which 0 were waited for; matrix products, arithmetic and copies ran while one was open for 21% of the time, Pallas kernels for 44%

profile of v13, /device:TPU:1, one launch (start us, length us, event | category | flops | bytes accessed | tf_op | source)
XLA Modules:
  0.0 141.4 jit_solution(9151998420085203386)
XLA Ops:
  0.6 0.0 copy-start
  0.6 0.0 copy-start.3
  0.7 1.1 copy.24
  1.8 1.0 copy.23
  2.8 0.1 multiply_convert_fusion.1
  2.9 1.3 collective-permute-start.1
  4.2 5.7 %collective-permute-start = (bf16[256,1,256]{0,2,1:T(8,128)(2,1)S(1)}, bf16[256,1,256]{0,2,1:T(8,128)(2,1)}, u32[]{:S(2)}, u32[]{:S(2)}) collective-permute-start(bf16[256,1,256]{0,2,1:T(8,128)(2,1)S(1)} %bitcast.55), channel_id=1, source_target_pairs={{0,1},{1,2},{2,3},{3,4},{4,5},{5,6},{6,7},{7,8},{8,9},{9,10},{10,1... | collective-permute-start | bytes 393224 | tf_op jit(solution)/shard_map/ppermute | solution.py:21
  9.8 3.7 %compare_select_fusion.1 = (f32[1,128,2,1024]{3,2,1,0:T(2,128)S(1)}, f32[128,1024]{1,0:T(8,128)}) fusion(bf16[1,128,2,1024]{3,2,1,0:T(2,128)(2,1)} %param.7), kind=kLoop, calls=%fused_computation.4 | loop fusion | flops 1441792 | bytes 2097152 | tf_op jit(solution)/shard_map/jit(_where)/select_n | solution.py:31
  13.6 2.0 %copy.28 = f32[128,1024]{0,1:T(8,128)} copy(f32[128,1024]{1,0:T(8,128)} %get-tuple-element.10) | data formatting | bytes 1048576 | tf_op jit(solution)/shard_map/reduce_sum | solution.py:295
  15.6 1.4 %reduce_sum.18 = f32[128,16,16]{0,2,1:T(8,128)S(1)} reduce(f32[128,16,2,16,2]{0,4,3,2,1:T(2,128)} %bitcast.48, f32[]{:T(128)} %constant.6.clone.1), dimensions={2,4}, to_apply=%region_1.2 | reduce | flops 98304 | bytes 655364 | tf_op jit(solution)/shard_map/reduce_sum | solution.py:295
  17.0 1.3 collective-permute-start.7
  18.3 4.0 %collective-permute-start.6 = (bf16[128,1,256]{0,2,1:T(8,128)(2,1)S(1)}, bf16[128,1,256]{0,2,1:T(8,128)(2,1)S(1)}, u32[]{:S(2)}, u32[]{:S(2)}) collective-permute-start(bf16[128,1,256]{0,2,1:T(8,128)(2,1)S(1)} %bitcast.62), channel_id=1, source_target_pairs={{0,1},{1,2},{2,3},{3,4},{4,5},{5,6},{6,7},{7,8},{8,9},{9,10},{10,1... | collective-permute-start | bytes 196616 | tf_op jit(solution)/shard_map/ppermute | solution.py:21
  22.3 0.0 copy-done.3
  22.3 1.2 fusion.13
  23.5 3.6 %collective-permute-start.4 = (bf16[64,1,1024]{2,1,0:T(2,128)(2,1)}, bf16[64,1,1024]{2,1,0:T(2,128)(2,1)}, u32[]{:S(2)}, u32[]{:S(2)}) collective-permute-start(bf16[64,1,1024]{2,1,0:T(2,128)(2,1)} %get-tuple-element.13), channel_id=1, source_target_pairs={{0,1},{1,2},{2,3},{3,4},{4,5},{5,6},{6,7},{7,8},{8,9},{9,10},{10,1... | collective-permute-start | bytes 393224 | tf_op jit(solution)/shard_map/ppermute | solution.py:21
  27.1 1.3 copy.35
  28.5 0.1 copy.30
  28.6 0.0 collective-permute-done.7
  28.6 1.5 %collective-permute-start.5 = (bf16[64,1,1024]{2,1,0:T(2,128)(2,1)}, bf16[64,1,1024]{2,1,0:T(2,128)(2,1)}, u32[]{:S(2)}, u32[]{:S(2)}) collective-permute-start(bf16[64,1,1024]{2,1,0:T(2,128)(2,1)} %get-tuple-element.14), channel_id=1, source_target_pairs={{1,0},{2,1},{3,2},{4,3},{5,4},{6,5},{7,6},{8,7},{9,8},{10,9},{11,1... | collective-permute-start | bytes 393224 | tf_op jit(solution)/shard_map/ppermute | solution.py:23
  30.0 0.1 copy.31
  30.2 0.0 collective-permute-done.6
  30.2 0.1 copy.29
  30.3 2.4 %convolution_multiply_fusion = f32[3,3,3,128,256]{4,3,2,1,0:T(8,128)S(1)} fusion(bf16[1,128,1,16,16]{1,0,4,3,2:T(2,128)(2,1)S(1)} %copy.31, bf16[1,128,1,16,16]{1,0,4,3,2:T(2,128)(2,1)S(1)} %copy.30, bf16[1,128,1,16,16]{1,0,4,3,2:T(2,128)(2,1)S(1)} %copy.29, bf16[1,256,1,16,16]{1,4,3,2,0:T(8,128)(2,1)S(1)} %bitcast.56), kind=kOutput, calls=%fused_computation.5 | convolution fusion | flops 417497088 | bytes 3866624 | tf_op jit(solution)/shard_map/transpose(jvp())/conv_general_dilated | solution.py:176
  32.7 2.0 %fusion.11 = (f32[3456,128]{1,0:T(8,128)}, f32[3456,128]{1,0:T(8,128)}) fusion(f32[3456,256]{1,0:T(8,128)S(1)} %bitcast.43), kind=kLoop, calls=%fused_computation.27 | loop fusion | bytes 7077888 | tf_op jit(solution)/shard_map/slice | solution.py:143
  34.7 0.0 collective-permute-done.1
  34.7 0.0 collective-permute-done
  34.7 0.9 pad_maximum_fusion.2
  35.7 0.3 rev.6
  36.0 0.0 copy-done
  36.0 3.1 %fusion.2 = f32[1,128,1,16,16]{1,0,4,3,2:T(1,128)S(1)} fusion(bf16[3,3,3,128,256]{4,3,2,1,0:T(8,128)(2,1)S(1)} %bitcast.35, bf16[1,256,3,16,16]{1,4,3,2,0:T(8,128)(2,1)S(1)} %bitcast.58), kind=kOutput, calls=%fused_computation.11 | convolution fusion | flops 416022528 | bytes 2293760 | tf_op jit(solution)/shard_map/conv_general_dilated | solution.py:189
  39.0 0.1 reverse_multiply_fusion
  39.2 0.0 copy-start.1
  39.2 0.7 copy-done.1
  39.9 0.3 broadcast_in_dim.25
  40.2 0.2 copy.26
  40.4 0.0 copy-start.2
  40.4 1.8 %fusion.1 = bf16[128,2,1024]{2,1,0:T(2,128)(2,1)S(1)} fusion(f32[128,1024]{1,0:T(8,128)S(1)} %copy.26, bf16[1,128,2,1024]{3,2,1,0:T(2,128)(2,1)} %param.7), kind=kLoop, calls=%fused_computation.9 | loop fusion | flops 1310720 | bytes 1572864 | tf_op jit(solution)/shard_map/convert_element_type | solution.py:305
  42.2 0.0 collective-permute-done.4
  42.2 0.0 collective-permute-done.5
  42.2 1.9 %pad_maximum_fusion.1 = bf16[64,4,1024]{2,1,0:T(4,128)(2,1)S(1)} fusion(bf16[64,1,1024]{2,1,0:T(2,128)(2,1)} %collective-permute-done.5, bf16[64,2,1024]{2,1,0:T(2,128)(2,1)S(1)} %bitcast.47, bf16[64,1,1024]{2,1,0:T(2,128)(2,1)} %collective-permute-done.4), kind=kLoop, calls=%fused_computation.13 | loop fusion | flops 1572864 | bytes 1048576 | tf_op jit(solution)/shard_map/concatenate | solution.py:19
  44.2 1.0 copy.34
  45.1 0.0 copy-done.2
  45.1 0.5 broadcast_in_dim.28
  45.6 1.3 copy.27
  47.0 1.7 %fusion.12 = (bf16[128,1,1024]{2,1,0:T(2,128)(2,1)}, bf16[128,1,1024]{2,1,0:T(2,128)(2,1)}) fusion(bf16[128,2,1024]{2,1,0:T(2,128)(2,1)S(1)} %fusion.1), kind=kLoop, calls=%fused_computation.28 | loop fusion | bytes 1048576 | tf_op jit(solution)/shard_map/slice | solution.py:18
  48.7 6.1 %collective-permute-start.2 = (bf16[128,1,1024]{2,1,0:T(2,128)(2,1)}, bf16[128,1,1024]{2,1,0:T(2,128)(2,1)}, u32[]{:S(2)}, u32[]{:S(2)}) collective-permute-start(bf16[128,1,1024]{2,1,0:T(2,128)(2,1)} %get-tuple-element.11), channel_id=1, source_target_pairs={{0,1},{1,2},{2,3},{3,4},{4,5},{5,6},{6,7},{7,8},{8,9},{9,10},{10,1... | collective-permute-start | bytes 786440 | tf_op jit(solution)/shard_map/ppermute | solution.py:21
  54.8 1.5 %collective-permute-start.3 = (bf16[128,1,1024]{2,1,0:T(2,128)(2,1)}, bf16[128,1,1024]{2,1,0:T(2,128)(2,1)}, u32[]{:S(2)}, u32[]{:S(2)}) collective-permute-start(bf16[128,1,1024]{2,1,0:T(2,128)(2,1)} %get-tuple-element.12), channel_id=1, source_target_pairs={{1,0},{2,1},{3,2},{4,3},{5,4},{6,5},{7,6},{8,7},{9,8},{10,9},{11,1... | collective-permute-start | bytes 786440 | tf_op jit(solution)/shard_map/ppermute | solution.py:23
  56.3 2.5 %multiply_convert_fusion.up_ref = bf16[128,2048]{1,0:T(8,128)(2,1)} fusion(f32[128,2048]{1,0:T(8,128)} %copy.27, f32[128,2048]{1,0:T(8,128)} %bitcast.37), kind=kLoop, calls=%fused_computation.10 | loop fusion | flops 524288 | bytes 2621440 | tf_op jit(solution)/shard_map/convert_element_type | solution.py:305
  58.8 7.1 %shard_map.86 = f32[27,64,128]{2,1,0:T(8,128)} custom-call(bf16[64,4096]{1,0:T(8,128)(2,1)} %bitcast.51, bf16[128,2048]{1,0:T(8,128)(2,1)} %multiply_convert_fusion.up_ref), custom_call_target="tpu_custom_call" | custom-call | tf_op jit(solution)/shard_map/pallas_call | solution.py:233
  65.9 1.3 broadcast_multiply_fusion
  67.2 5.3 %select_maximum_fusion.x_ref = f32[9216,128]{1,0:T(8,128)} fusion(f32[3456,128]{1,0:T(8,128)} %get-tuple-element.8, f32[3456,128]{1,0:T(8,128)} %get-tuple-element.7, f32[1728,128]{1,0:T(8,128)S(1)} %bitcast.41), kind=kLoop, calls=%fused_computation | loop fusion | flops 7077888 | bytes 9142272 | tf_op jit(solution)/shard_map/concatenate | solution.py:143
  72.5 55.1 %shard_map.87 = (f32[1728,128]{1,0:T(8,128)}, f32[3456,256]{1,0:T(8,128)}) custom-call(f32[9216,128]{1,0:T(8,128)} %select_maximum_fusion.x_ref), custom_call_target="tpu_custom_call" | custom-call | tf_op jit(solution)/shard_map/pallas_call | solution.py:152
  127.6 0.0 copy-start.4
  127.6 0.0 collective-permute-done.2
  127.6 0.0 collective-permute-done.3
  127.6 3.0 %pad_maximum_fusion = bf16[128,4,1024]{2,1,0:T(4,128)(2,1)S(1)} fusion(bf16[128,1,1024]{2,1,0:T(2,128)(2,1)} %collective-permute-done.3, bf16[128,2,1024]{2,1,0:T(2,128)(2,1)S(1)} %fusion.1, bf16[128,1,1024]{2,1,0:T(2,128)(2,1)} %collective-permute-done.2), kind=kLoop, calls=%fused_computation.7 | loop fusion | flops 3145728 | bytes 2097152 | tf_op jit(solution)/shard_map/concatenate | solution.py:19
  130.7 1.3 copy.33
  132.0 4.3 %shard_map.85 = bf16[64,2,1024]{2,1,0:T(2,128)(2,1)} custom-call(bf16[128,4096]{1,0:T(8,128)(2,1)} %bitcast.40, bf16[27,64,128]{2,1,0:T(8,128)(2,1)} %w_ref.1), custom_call_target="tpu_custom_call" | custom-call | tf_op jit(solution)/shard_map/pallas_call | solution.py:268
  136.3 0.0 copy-done.4
  136.3 0.9 copy.42
  137.2 4.2 %copy.43 = f32[27,128,256]{2,1,0:T(8,128)} copy(f32[27,128,256]{2,1,0:T(8,128)} %bitcast.42) | data formatting | bytes 7077888
  (3 shorter events, 0.0 us)
Async XLA Ops:
  0.6 35.3 %copy-start = (bf16[27,128,256]{2,1,0:T(8,128)(2,1)S(1)}, bf16[27,128,256]{2,1,0:T(8,128)(2,1)}, u32[]{:S(2)}) copy-start(bf16[27,128,256]{2,1,0:T(8,128)(2,1)} %param.11) | copy-start | bytes 5308420
  0.6 21.7 %copy-start.3 = (bf16[1,64,2,1024]{3,2,1,0:T(2,128)(2,1)S(1)}, bf16[1,64,2,1024]{3,2,1,0:T(2,128)(2,1)}, u32[]{:S(2)}) copy-start(bf16[1,64,2,1024]{3,2,1,0:T(2,128)(2,1)} %param.6) | copy-start | bytes 786436
  2.9 31.8 %collective-permute-start.1 = (bf16[256,1,256]{0,2,1:T(8,128)(2,1)S(1)}, bf16[256,1,256]{0,2,1:T(8,128)(2,1)S(1)}, u32[]{:S(2)}, u32[]{:S(2)}) collective-permute-start(bf16[256,1,256]{0,2,1:T(8,128)(2,1)S(1)} %bitcast.54), channel_id=1, source_target_pairs={{1,0},{2,1},{3,2},{4,3},{5,4},{6,5},{7,6},{8,7},{9,8},{10,9},{11,1... | collective-permute-start | bytes 393224 | tf_op jit(solution)/shard_map/ppermute | solution.py:23
  4.2 30.5 %collective-permute-start = (bf16[256,1,256]{0,2,1:T(8,128)(2,1)S(1)}, bf16[256,1,256]{0,2,1:T(8,128)(2,1)}, u32[]{:S(2)}, u32[]{:S(2)}) collective-permute-start(bf16[256,1,256]{0,2,1:T(8,128)(2,1)S(1)} %bitcast.55), channel_id=1, source_target_pairs={{0,1},{1,2},{2,3},{3,4},{4,5},{5,6},{6,7},{7,8},{8,9},{9,10},{10,1... | collective-permute-start | bytes 393224 | tf_op jit(solution)/shard_map/ppermute | solution.py:21
  17.0 11.5 %collective-permute-start.7 = (bf16[128,1,256]{0,2,1:T(8,128)(2,1)S(1)}, bf16[128,1,256]{0,2,1:T(8,128)(2,1)S(1)}, u32[]{:S(2)}, u32[]{:S(2)}) collective-permute-start(bf16[128,1,256]{0,2,1:T(8,128)(2,1)S(1)} %bitcast.61), channel_id=1, source_target_pairs={{1,0},{2,1},{3,2},{4,3},{5,4},{6,5},{7,6},{8,7},{9,8},{10,9},{11,1... | collective-permute-start | bytes 196616 | tf_op jit(solution)/shard_map/ppermute | solution.py:23
  18.3 11.8 %collective-permute-start.6 = (bf16[128,1,256]{0,2,1:T(8,128)(2,1)S(1)}, bf16[128,1,256]{0,2,1:T(8,128)(2,1)S(1)}, u32[]{:S(2)}, u32[]{:S(2)}) collective-permute-start(bf16[128,1,256]{0,2,1:T(8,128)(2,1)S(1)} %bitcast.62), channel_id=1, source_target_pairs={{0,1},{1,2},{2,3},{3,4},{4,5},{5,6},{6,7},{7,8},{8,9},{9,10},{10,1... | collective-permute-start | bytes 196616 | tf_op jit(solution)/shard_map/ppermute | solution.py:21
  23.5 18.7 %collective-permute-start.4 = (bf16[64,1,1024]{2,1,0:T(2,128)(2,1)}, bf16[64,1,1024]{2,1,0:T(2,128)(2,1)}, u32[]{:S(2)}, u32[]{:S(2)}) collective-permute-start(bf16[64,1,1024]{2,1,0:T(2,128)(2,1)} %get-tuple-element.13), channel_id=1, source_target_pairs={{0,1},{1,2},{2,3},{3,4},{4,5},{5,6},{6,7},{7,8},{8,9},{9,10},{10,1... | collective-permute-start | bytes 393224 | tf_op jit(solution)/shard_map/ppermute | solution.py:21
  28.6 13.7 %collective-permute-start.5 = (bf16[64,1,1024]{2,1,0:T(2,128)(2,1)}, bf16[64,1,1024]{2,1,0:T(2,128)(2,1)}, u32[]{:S(2)}, u32[]{:S(2)}) collective-permute-start(bf16[64,1,1024]{2,1,0:T(2,128)(2,1)} %get-tuple-element.14), channel_id=1, source_target_pairs={{1,0},{2,1},{3,2},{4,3},{5,4},{6,5},{7,6},{8,7},{9,8},{10,9},{11,1... | collective-permute-start | bytes 393224 | tf_op jit(solution)/shard_map/ppermute | solution.py:23
  39.2 0.7 copy-start.1
  40.4 4.7 %copy-start.2 = (f32[128,16,2,16]{0,3,2,1:T(8,128)S(1)}, f32[128,16,2,16]{0,3,2,1:T(8,128)}, u32[]{:S(2)}) copy-start(f32[128,16,2,16]{0,3,2,1:T(8,128)} %copy-done.1) | copy-start | bytes 786436
  48.7 78.9 %collective-permute-start.2 = (bf16[128,1,1024]{2,1,0:T(2,128)(2,1)}, bf16[128,1,1024]{2,1,0:T(2,128)(2,1)}, u32[]{:S(2)}, u32[]{:S(2)}) collective-permute-start(bf16[128,1,1024]{2,1,0:T(2,128)(2,1)} %get-tuple-element.11), channel_id=1, source_target_pairs={{0,1},{1,2},{2,3},{3,4},{4,5},{5,6},{6,7},{7,8},{8,9},{9,10},{10,1... | collective-permute-start | bytes 786440 | tf_op jit(solution)/shard_map/ppermute | solution.py:21
  54.8 72.8 %collective-permute-start.3 = (bf16[128,1,1024]{2,1,0:T(2,128)(2,1)}, bf16[128,1,1024]{2,1,0:T(2,128)(2,1)}, u32[]{:S(2)}, u32[]{:S(2)}) collective-permute-start(bf16[128,1,1024]{2,1,0:T(2,128)(2,1)} %get-tuple-element.12), channel_id=1, source_target_pairs={{1,0},{2,1},{3,2},{4,3},{5,4},{6,5},{7,6},{8,7},{9,8},{10,9},{11,1... | collective-permute-start | bytes 786440 | tf_op jit(solution)/shard_map/ppermute | solution.py:23
  127.6 8.7 %copy-start.4 = (f32[1728,128]{1,0:T(8,128)S(1)}, f32[1728,128]{1,0:T(8,128)}, u32[]{:S(2)}) copy-start(f32[1728,128]{1,0:T(8,128)} %get-tuple-element.5) | copy-start | bytes 2654212

commit v14 on v11

--- a/solution.py
+++ b/solution.py
@@ -206,7 +206,7 @@
     column = spot % side
     row = (spot // side) % side
     upstream = up_ref[...]
-    field = src_ref[...].astype(jnp.float32)
+    field = src_ref[...]
     for b in range(3):
         for c in range(3):
             shift = (b - 1) * side + (c - 1)
@@ -214,7 +214,7 @@
             inside = (column + c - 1 >= 0) & (column + c - 1 < side) & (row + b - 1 >= 0) & (row + b - 1 < side)
             for a in range(3):
                 window = moved[:, a * plane : a * plane + cells]
-                window = jnp.where(inside, window, 0.0).astype(jnp.bfloat16)
+                window = jnp.where(inside, window, jnp.zeros_like(window))
                 terms_ref[9 * a + 3 * b + c] = lax.dot_general(
                     window, upstream, (((1,), (1,)), ((), ())), preferred_element_type=jnp.float32
                 )

time: 138 us -> 138 us (level)
  no operation moved by 1% of the time
where the time goes in v14:
time: 138 us; the launch traced here: 137 us
  Pallas kernels  64.2 us (47%)
  local copies, waits for them, and re-layouts  23.1 us (17%)
  starting transfers between devices  23.1 us (17%)
  other arithmetic  16.2 us (12%)
  matrix products  5.77 us (4%)
  waiting for transfers between devices  4.09 us (3%)
    pallas_call x1, Pallas kernels, all_reduce(): pl.pallas_call(_all_reduce_kernel, out_shape=(jax.ShapeDtypeStruct((rows_...  52.6 us
    ppermute x4, starting transfers between devices, padded_2(): lax.ppermute(tail, axis, [(i, (i + 1) % count) for i in range(ends)])  17.8 us
    unnamed x21, local copies, waits for them, and re-layouts  11.5 us
    pallas_call x1, Pallas kernels, kernel_terms_flat(): pl.pallas_call(_terms_a_body, out_shape=jax.ShapeDtypeStruct((27, chan_in...  7.28 us
    conv_general_dilated x2, matrix products, conv_cells(): lax.conv_general_dilated(field[None], shaped, (1, 1, 1), ((0, 0), (1, 1),...  5.77 us
    concatenate x1, other arithmetic, all_reduce(): jnp.concatenate([sums_a.reshape(rows_a, 128) * scale_a, wide[:, :128], wi...  5.63 us
    ppermute x4, starting transfers between devices, padded_2(): lax.ppermute(head, axis, [((i + 1) % count, i) for i in range(ends)])  5.34 us
    pallas_call x1, Pallas kernels, back_flat(): pl.pallas_call(_back_a_body, out_shape=jax.ShapeDtypeStruct((chan_in, cel...  4.31 us
  transfers between devices with their start and end apart: 8, of which 1 were waited for; matrix products, arithmetic and copies ran while one was open for 14% of the time, Pallas kernels for 38%

profile of v14, /device:TPU:1, one launch (start us, length us, event | category | flops | bytes accessed | tf_op | source)
XLA Modules:
  0.0 137.5 jit_solution(16907565028949035133)
XLA Ops:
  0.6 0.0 copy-start.2
  0.6 1.0 copy.25
  1.7 1.0 copy.24
  2.7 0.1 multiply_convert_fusion.1
  2.8 1.3 collective-permute-start.1
  4.1 5.0 %collective-permute-start = (bf16[256,1,256]{0,2,1:T(8,128)(2,1)S(1)}, bf16[256,1,256]{0,2,1:T(8,128)(2,1)S(1)}, u32[]{:S(2)}, u32[]{:S(2)}) collective-permute-start(bf16[256,1,256]{0,2,1:T(8,128)(2,1)S(1)} %bitcast.54), channel_id=1, source_target_pairs={{0,1},{1,2},{2,3},{3,4},{4,5},{5,6},{6,7},{7,8},{8,9},{9,10},{10,1... | collective-permute-start | bytes 393224 | tf_op jit(solution)/shard_map/ppermute | solution.py:21
  9.1 2.9 %compare_select_fusion.1 = (f32[1,128,2,1024]{3,2,1,0:T(2,128)S(1)}, f32[128,1024]{1,0:T(8,128)S(1)}) fusion(bf16[1,128,2,1024]{3,2,1,0:T(2,128)(2,1)} %param.7), kind=kLoop, calls=%fused_computation.4 | loop fusion | flops 1441792 | bytes 2097152 | tf_op jit(solution)/shard_map/jit(_where)/select_n | solution.py:31
  12.0 0.2 copy.31
  12.2 0.4 reduce_sum.18
  12.6 1.3 collective-permute-start.7
  13.9 4.2 %collective-permute-start.6 = (bf16[128,1,256]{0,2,1:T(8,128)(2,1)S(1)}, bf16[128,1,256]{0,2,1:T(8,128)(2,1)S(1)}, u32[]{:S(2)}, u32[]{:S(2)}) collective-permute-start(bf16[128,1,256]{0,2,1:T(8,128)(2,1)S(1)} %bitcast.62), channel_id=1, source_target_pairs={{0,1},{1,2},{2,3},{3,4},{4,5},{5,6},{6,7},{7,8},{8,9},{9,10},{10,1... | collective-permute-start | bytes 196616 | tf_op jit(solution)/shard_map/ppermute | solution.py:21
  18.1 0.0 copy-done.2
  18.1 0.4 fusion.15
  18.5 3.4 %collective-permute-start.4 = (bf16[64,1,1024]{2,1,0:T(2,128)(2,1)S(1)}, bf16[64,1,1024]{2,1,0:T(2,128)(2,1)S(1)}, u32[]{:S(2)}, u32[]{:S(2)}) collective-permute-start(bf16[64,1,1024]{2,1,0:T(2,128)(2,1)S(1)} %get-tuple-element.13), channel_id=1, source_target_pairs={{0,1},{1,2},{2,3},{3,4},{4,5},{5,6},{6,7},{7,8},{8,9},{9,10},{10,1... | collective-permute-start | bytes 393224 | tf_op jit(solution)/shard_map/ppermute | solution.py:21
  21.9 0.9 copy.27
  22.8 1.3 copy.38
  24.1 0.1 copy.33
  24.2 2.9 %rev.3 = bf16[27,128,256]{2,1,0:T(8,128)(2,1)} reverse(bf16[27,128,256]{2,1,0:T(8,128)(2,1)} %param.11), dimensions={0} | reverse | bytes 3538944 | tf_op jit(solution)/shard_map/rev | solution.py:188
  27.1 0.0 collective-permute-done.7
  27.1 1.5 %collective-permute-start.5 = (bf16[64,1,1024]{2,1,0:T(2,128)(2,1)S(1)}, bf16[64,1,1024]{2,1,0:T(2,128)(2,1)S(1)}, u32[]{:S(2)}, u32[]{:S(2)}) collective-permute-start(bf16[64,1,1024]{2,1,0:T(2,128)(2,1)S(1)} %get-tuple-element.14), channel_id=1, source_target_pairs={{1,0},{2,1},{3,2},{4,3},{5,4},{6,5},{7,6},{8,7},{9,8},{10,9},{11,1... | collective-permute-start | bytes 393224 | tf_op jit(solution)/shard_map/ppermute | solution.py:23
  28.6 0.1 copy.34
  28.7 0.0 collective-permute-done.6
  28.7 0.1 copy.32
  28.8 2.3 %convolution_multiply_fusion = f32[3,3,3,128,256]{4,3,2,1,0:T(8,128)S(1)} fusion(bf16[1,128,1,16,16]{1,0,4,3,2:T(2,128)(2,1)S(1)} %copy.34, bf16[1,128,1,16,16]{1,0,4,3,2:T(2,128)(2,1)S(1)} %copy.33, bf16[1,128,1,16,16]{1,0,4,3,2:T(2,128)(2,1)S(1)} %copy.32, bf16[1,256,1,16,16]{1,4,3,2,0:T(8,128)(2,1)S(1)} %bitcast.56), kind=kOutput, calls=%fused_computation.5 | convolution fusion | flops 417497088 | bytes 3866624 | tf_op jit(solution)/shard_map/transpose(jvp())/conv_general_dilated | solution.py:176
  31.2 0.0 copy-start.4
  31.2 0.0 copy-start.6
  31.2 1.5 %fusion.13 = (f32[3456,128]{1,0:T(8,128)S(1)}, f32[3456,128]{1,0:T(8,128)}) fusion(f32[3456,256]{1,0:T(8,128)S(1)} %bitcast.42), kind=kLoop, calls=%fused_computation.29 | loop fusion | bytes 7077888 | tf_op jit(solution)/shard_map/slice | solution.py:143
  32.7 0.0 collective-permute-done.1
  32.7 0.3 copy.28
  32.9 0.0 collective-permute-done
  32.9 0.3 copy.26
  33.2 0.0 collective-permute-done.4
  33.2 4.1 %collective-permute-done.5 = bf16[64,1,1024]{2,1,0:T(2,128)(2,1)S(1)} collective-permute-done((bf16[64,1,1024]{2,1,0:T(2,128)(2,1)S(1)}, bf16[64,1,1024]{2,1,0:T(2,128)(2,1)S(1)}, u32[]{:S(2)}, u32[]{:S(2)}) %collective-permute-start.5) | collective-permute-done | bytes 131104 | tf_op jit(solution)/shard_map/ppermute | solution.py:23
  37.3 0.9 pad_maximum_fusion.3
  38.2 1.0 copy.37
  39.1 0.0 copy-done.4
  39.1 0.0 copy-done.6
  39.1 3.4 %convolution_multiply_fusion.1 = f32[1,128,1,16,16]{1,0,4,3,2:T(1,128)S(1)} fusion(bf16[3,3,3,256,128]{3,4,2,1,0:T(8,128)(2,1)S(1)} %bitcast.51, bf16[1,256,1,16,16]{1,0,4,3,2:T(2,128)(2,1)S(1)} %copy.28, bf16[1,256,1,16,16]{1,0,4,3,2:T(2,128)(2,1)S(1)} %copy-done.6, bf16[1,256,1,16,16]{1,0,4,3,2:T(2,128)(2,1)S(1)} %copy.26), kind=kOutput, calls=%fused_computation.6 | convolution fusion | flops 417234944 | bytes 2293760 | tf_op jit(solution)/shard_map/conv_general_dilated | solution.py:176
  42.6 0.0 copy-start.1
  42.6 0.7 copy-done.1
  43.3 0.3 broadcast_in_dim.21
  43.6 0.2 copy.29
  43.8 0.0 copy-done.3
  43.8 0.7 fusion.1
  44.5 1.5 %broadcast_in_dim.24 = f32[128,2,32,16,2]{0,4,3,2,1:T(2,128)S(1)} broadcast(f32[128,32,16]{0,2,1:T(8,128)} %bitcast.44), dimensions={0,2,3} | broadcast | bytes 1310720 | tf_op jit(solution)/shard_map/broadcast_in_dim | solution.py:295
  46.0 1.3 copy.30
  47.3 2.5 %multiply_convert_fusion.up_ref = bf16[128,2048]{1,0:T(8,128)(2,1)} fusion(f32[128,2048]{1,0:T(8,128)} %copy.30, f32[128,2048]{1,0:T(8,128)} %bitcast.36), kind=kLoop, calls=%fused_computation.11 | loop fusion | flops 524288 | bytes 2621440 | tf_op jit(solution)/shard_map/convert_element_type | solution.py:297
  49.8 7.3 %shard_map.86 = f32[27,64,128]{2,1,0:T(8,128)} custom-call(bf16[64,4096]{1,0:T(8,128)(2,1)} %bitcast.50, bf16[128,2048]{1,0:T(8,128)(2,1)} %multiply_convert_fusion.up_ref), custom_call_target="tpu_custom_call" | custom-call | tf_op jit(solution)/shard_map/pallas_call | solution.py:225
  57.1 1.4 %broadcast_multiply_fusion = f32[27,64,128]{2,1,0:T(8,128)S(1)} fusion(f32[27,64,128]{2,1,0:T(8,128)} %shard_map.86), kind=kLoop, calls=%fused_computation.17 | loop fusion | flops 221184 | bytes 1769472 | tf_op jit(solution)/shard_map/mul | solution.py:143
  58.5 1.7 %fusion.14 = (bf16[128,1,1024]{2,1,0:T(2,128)(2,1)}, bf16[128,1,1024]{2,1,0:T(2,128)(2,1)}) fusion(bf16[128,2,1024]{2,1,0:T(2,128)(2,1)S(1)} %fusion.1), kind=kLoop, calls=%fused_computation.30 | loop fusion | bytes 1048576 | tf_op jit(solution)/shard_map/slice | solution.py:18
  60.2 5.2 %collective-permute-start.2 = (bf16[128,1,1024]{2,1,0:T(2,128)(2,1)}, bf16[128,1,1024]{2,1,0:T(2,128)(2,1)S(1)}, u32[]{:S(2)}, u32[]{:S(2)}) collective-permute-start(bf16[128,1,1024]{2,1,0:T(2,128)(2,1)} %get-tuple-element.11), channel_id=1, source_target_pairs={{0,1},{1,2},{2,3},{3,4},{4,5},{5,6},{6,7},{7,8},{8,9},{9,10},{10,1... | collective-permute-start | bytes 786440 | tf_op jit(solution)/shard_map/ppermute | solution.py:21
  65.4 1.3 collective-permute-start.3
  66.7 0.0 copy-done
  66.7 5.6 %select_maximum_fusion.x_ref = f32[9216,128]{1,0:T(8,128)} fusion(f32[3456,128]{1,0:T(8,128)S(1)} %copy-done, f32[3456,128]{1,0:T(8,128)S(1)} %get-tuple-element.7, f32[1728,128]{1,0:T(8,128)S(1)} %bitcast.40), kind=kLoop, calls=%fused_computation | loop fusion | flops 7077888 | bytes 9142272 | tf_op jit(solution)/shard_map/concatenate | solution.py:143
  72.3 52.6 %shard_map.87 = (f32[1728,128]{1,0:T(8,128)}, f32[3456,256]{1,0:T(8,128)}) custom-call(f32[9216,128]{1,0:T(8,128)} %select_maximum_fusion.x_ref), custom_call_target="tpu_custom_call" | custom-call | tf_op jit(solution)/shard_map/pallas_call | solution.py:152
  125.0 0.0 copy-start.5
  125.0 0.0 collective-permute-done.2
  125.0 0.0 collective-permute-done.3
  125.0 1.8 %pad_maximum_fusion = bf16[128,4,1024]{2,1,0:T(4,128)(2,1)S(1)} fusion(bf16[128,1,1024]{2,1,0:T(2,128)(2,1)S(1)} %collective-permute-done.3, bf16[128,2,1024]{2,1,0:T(2,128)(2,1)S(1)} %fusion.1, bf16[128,1,1024]{2,1,0:T(2,128)(2,1)S(1)} %collective-permute-done.2), kind=kLoop, calls=%fused_computation.8 | loop fusion | flops 3145728 | bytes 2097152 | tf_op jit(solution)/shard_map/concatenate | solution.py:19
  126.8 1.3 copy.36
  128.1 4.3 %shard_map.85 = bf16[64,2,1024]{2,1,0:T(2,128)(2,1)} custom-call(bf16[128,4096]{1,0:T(8,128)(2,1)} %bitcast.39, bf16[27,64,128]{2,1,0:T(8,128)(2,1)} %w_ref.1), custom_call_target="tpu_custom_call" | custom-call | tf_op jit(solution)/shard_map/pallas_call | solution.py:260
  132.4 0.0 copy-done.5
  132.4 0.9 copy.43
  133.3 4.2 %copy.44 = f32[27,128,256]{2,1,0:T(8,128)} copy(f32[27,128,256]{2,1,0:T(8,128)} %bitcast.41) | data formatting | bytes 7077888
  (5 shorter events, 0.1 us)
Async XLA Ops:
  0.6 17.5 %copy-start.2 = (bf16[1,64,2,1024]{3,2,1,0:T(2,128)(2,1)S(1)}, bf16[1,64,2,1024]{3,2,1,0:T(2,128)(2,1)}, u32[]{:S(2)}) copy-start(bf16[1,64,2,1024]{3,2,1,0:T(2,128)(2,1)} %param.6) | copy-start | bytes 786436
  2.8 29.9 %collective-permute-start.1 = (bf16[256,1,256]{0,2,1:T(8,128)(2,1)S(1)}, bf16[256,1,256]{0,2,1:T(8,128)(2,1)S(1)}, u32[]{:S(2)}, u32[]{:S(2)}) collective-permute-start(bf16[256,1,256]{0,2,1:T(8,128)(2,1)S(1)} %bitcast.53), channel_id=1, source_target_pairs={{1,0},{2,1},{3,2},{4,3},{5,4},{6,5},{7,6},{8,7},{9,8},{10,9},{11,1... | collective-permute-start | bytes 393224 | tf_op jit(solution)/shard_map/ppermute | solution.py:23
  4.1 28.9 %collective-permute-start = (bf16[256,1,256]{0,2,1:T(8,128)(2,1)S(1)}, bf16[256,1,256]{0,2,1:T(8,128)(2,1)S(1)}, u32[]{:S(2)}, u32[]{:S(2)}) collective-permute-start(bf16[256,1,256]{0,2,1:T(8,128)(2,1)S(1)} %bitcast.54), channel_id=1, source_target_pairs={{0,1},{1,2},{2,3},{3,4},{4,5},{5,6},{6,7},{7,8},{8,9},{9,10},{10,1... | collective-permute-start | bytes 393224 | tf_op jit(solution)/shard_map/ppermute | solution.py:21
  12.6 14.5 %collective-permute-start.7 = (bf16[128,1,256]{0,2,1:T(8,128)(2,1)S(1)}, bf16[128,1,256]{0,2,1:T(8,128)(2,1)S(1)}, u32[]{:S(2)}, u32[]{:S(2)}) collective-permute-start(bf16[128,1,256]{0,2,1:T(8,128)(2,1)S(1)} %bitcast.61), channel_id=1, source_target_pairs={{1,0},{2,1},{3,2},{4,3},{5,4},{6,5},{7,6},{8,7},{9,8},{10,9},{11,1... | collective-permute-start | bytes 196616 | tf_op jit(solution)/shard_map/ppermute | solution.py:23
  13.9 14.8 %collective-permute-start.6 = (bf16[128,1,256]{0,2,1:T(8,128)(2,1)S(1)}, bf16[128,1,256]{0,2,1:T(8,128)(2,1)S(1)}, u32[]{:S(2)}, u32[]{:S(2)}) collective-permute-start(bf16[128,1,256]{0,2,1:T(8,128)(2,1)S(1)} %bitcast.62), channel_id=1, source_target_pairs={{0,1},{1,2},{2,3},{3,4},{4,5},{5,6},{6,7},{7,8},{8,9},{9,10},{10,1... | collective-permute-start | bytes 196616 | tf_op jit(solution)/shard_map/ppermute | solution.py:21
  18.5 14.7 %collective-permute-start.4 = (bf16[64,1,1024]{2,1,0:T(2,128)(2,1)S(1)}, bf16[64,1,1024]{2,1,0:T(2,128)(2,1)S(1)}, u32[]{:S(2)}, u32[]{:S(2)}) collective-permute-start(bf16[64,1,1024]{2,1,0:T(2,128)(2,1)S(1)} %get-tuple-element.13), channel_id=1, source_target_pairs={{0,1},{1,2},{2,3},{3,4},{4,5},{5,6},{6,7},{7,8},{8,9},{9,10},{10,1... | collective-permute-start | bytes 393224 | tf_op jit(solution)/shard_map/ppermute | solution.py:21
  27.1 10.1 %collective-permute-start.5 = (bf16[64,1,1024]{2,1,0:T(2,128)(2,1)S(1)}, bf16[64,1,1024]{2,1,0:T(2,128)(2,1)S(1)}, u32[]{:S(2)}, u32[]{:S(2)}) collective-permute-start(bf16[64,1,1024]{2,1,0:T(2,128)(2,1)S(1)} %get-tuple-element.14), channel_id=1, source_target_pairs={{1,0},{2,1},{3,2},{4,3},{5,4},{6,5},{7,6},{8,7},{9,8},{10,9},{11,1... | collective-permute-start | bytes 393224 | tf_op jit(solution)/shard_map/ppermute | solution.py:23
  31.2 8.0 %copy-start.4 = (bf16[27,128,256]{2,1,0:T(8,128)(2,1)S(1)}, bf16[27,128,256]{2,1,0:T(8,128)(2,1)}, u32[]{:S(2)}) copy-start(bf16[27,128,256]{2,1,0:T(8,128)(2,1)} %rev.3) | copy-start | bytes 5308420
  31.2 8.0 %copy-start.6 = (bf16[1,256,1,16,16]{1,0,4,3,2:T(2,128)(2,1)S(1)}, bf16[1,256,1,16,16]{1,0,4,3,2:T(2,128)(2,1)}, u32[]{:S(2)}) copy-start(bf16[1,256,1,16,16]{1,0,4,3,2:T(2,128)(2,1)} %copy.27) | copy-start | bytes 393220
  39.1 4.7 %copy-start.3 = (bf16[1,128,2,1024]{3,2,1,0:T(2,128)(2,1)S(1)}, bf16[1,128,2,1024]{3,2,1,0:T(2,128)(2,1)}, u32[]{:S(2)}) copy-start(bf16[1,128,2,1024]{3,2,1,0:T(2,128)(2,1)} %param.7) | copy-start | bytes 1572868
  42.6 0.7 copy-start.1
  57.1 9.6 %copy-start = (f32[3456,128]{1,0:T(8,128)S(1)}, f32[3456,128]{1,0:T(8,128)}, u32[]{:S(2)}) copy-start(f32[3456,128]{1,0:T(8,128)} %get-tuple-element.8) | copy-start | bytes 5308420
  60.2 64.8 %collective-permute-start.2 = (bf16[128,1,1024]{2,1,0:T(2,128)(2,1)}, bf16[128,1,1024]{2,1,0:T(2,128)(2,1)S(1)}, u32[]{:S(2)}, u32[]{:S(2)}) collective-permute-start(bf16[128,1,1024]{2,1,0:T(2,128)(2,1)} %get-tuple-element.11), channel_id=1, source_target_pairs={{0,1},{1,2},{2,3},{3,4},{4,5},{5,6},{6,7},{7,8},{8,9},{9,10},{10,1... | collective-permute-start | bytes 786440 | tf_op jit(solution)/shard_map/ppermute | solution.py:21
  65.4 59.6 %collective-permute-start.3 = (bf16[128,1,1024]{2,1,0:T(2,128)(2,1)}, bf16[128,1,1024]{2,1,0:T(2,128)(2,1)S(1)}, u32[]{:S(2)}, u32[]{:S(2)}) collective-permute-start(bf16[128,1,1024]{2,1,0:T(2,128)(2,1)} %get-tuple-element.12), channel_id=1, source_target_pairs={{1,0},{2,1},{3,2},{4,3},{5,4},{6,5},{7,6},{8,7},{9,8},{10,9},{11,1... | collective-permute-start | bytes 786440 | tf_op jit(solution)/shard_map/ppermute | solution.py:23
  125.0 7.4 %copy-start.5 = (f32[1728,128]{1,0:T(8,128)S(1)}, f32[1728,128]{1,0:T(8,128)}, u32[]{:S(2)}) copy-start(f32[1728,128]{1,0:T(8,128)} %get-tuple-element.5) | copy-start | bytes 2654212
